TPU v7x, 32 devices: a whole 2x2x4 slice. The times are simulated.
32 devices in a mesh: abl: 2 (over y), head: 4 (over x, core), ctx: 4 (over z).
Axes of the slice: x: 2, y: 2, z: 4, core: 2. Of those that a mesh axis runs over, the one named last changes fastest.
Arguments:
- queries: bfloat16 [1024, 6144], P(('abl', 'head', 'ctx')), parts along dimension 0, may hold values from -30 to 30
- keys: bfloat16 [16384, 6144], P(('abl', 'ctx'), 'head'), parts along dimension 0, may hold values from -6 to 6
- values: bfloat16 [16384, 6144], P(('abl', 'ctx'), 'head'), parts along dimension 0, may hold values from -6 to 6
- kept_rows: int32 [128], P(('abl', 'ctx')), parts along dimension 0, may hold values from 0 to 1, as said below
- out_weight: bfloat16 [6144, 6144], P('head'), may hold values from -6 to 6
Outputs:
- projected: bfloat16 [1024, 6144], P(('abl', 'head', 'ctx')), parts along dimension 0
There are 2 independent parts, one for each index of `abl`. A program takes and returns all parts, laid end to end along the dimension named above; an argument that names none is the same for every part. Nothing has to cross between parts.
Inputs may be any that keep to these rules, and one draw needn't show every extreme that they name: `kept_rows`: in every part the first row of each block of 16 consecutive rows is kept.
All inputs are finite; a program needn't handle non-finite values.
Results may differ from a plain program's by a relative error of at most 0.028.
Values may be sent and summed in bfloat16 or wider, within the bound.
No kernel may reach another device: no remote copies, remote signals or barrier semaphores. Data moves between devices by JAX's collectives and lax.ppermute only.
A program may use at most 128 MiB of HBM per device.

v0:
```python
import math

import jax
import jax.numpy as jnp
from jax import lax
from jax.sharding import PartitionSpec as P

HD = 128


def shards(queries, keys, values, kept_rows, out_weight):
    score_scale = 1.0 / math.sqrt(HD)
    local_heads = keys.shape[1] // HD
    key_count = keys.shape[0]
    key_heads = keys.reshape(key_count, local_heads, HD)
    value_heads = values.reshape(key_count, local_heads, HD)
    visible = jnp.repeat(kept_rows, 128) > 0
    query_block = lax.all_to_all(queries, "head", split_axis=1, concat_axis=0, tiled=True)
    all_queries = lax.all_gather(query_block, "ctx", axis=0, tiled=True)
    row_count = all_queries.shape[0]
    zeros_sum = jnp.zeros((row_count, local_heads * HD), jnp.float32)
    lowest = jnp.full((local_heads, row_count), -1e30, jnp.float32)
    summed = zeros_sum
    row_count = all_queries.shape[0]
    shaped = all_queries.reshape(row_count, local_heads, HD)
    scores = (
        jnp.einsum("qhd,khd->hqk", shaped, key_heads, preferred_element_type=jnp.float32)
        * score_scale
    )
    scores = jnp.where(visible[None, None, :], scores, -jnp.inf)
    highest = jnp.maximum(lowest, jnp.max(scores, axis=-1))
    rescale = jnp.exp(lowest - highest)
    softened = jnp.exp(scores - highest[..., None])
    normal_sum = jnp.sum(softened, axis=-1)
    mixed = jnp.einsum(
        "hqk,khd->qhd",
        softened.astype(jnp.bfloat16),
        value_heads,
        preferred_element_type=jnp.float32,
    )
    summed = summed * jnp.repeat(rescale.T, HD, axis=1) + mixed.reshape(row_count, local_heads * HD)
    summed, running, normal_sum = (summed, highest, normal_sum)
    highest = lax.pmax(running, "ctx")
    rescale = jnp.exp(running - highest)
    summed = summed * jnp.repeat(rescale.T, HD, axis=1)
    normal_sum = normal_sum * rescale
    summed, normal_sum = (
        lax.psum_scatter(
            summed.astype(jnp.bfloat16), "ctx", scatter_dimension=0, tiled=True
        ).astype(jnp.float32),
        lax.psum_scatter(
            normal_sum.astype(jnp.bfloat16), "ctx", scatter_dimension=1, tiled=True
        ).astype(jnp.float32),
    )
    attended = (summed / jnp.repeat(normal_sum.T, HD, axis=1)).astype(jnp.bfloat16)
    return lax.psum_scatter(
        jnp.dot(attended, out_weight, preferred_element_type=jnp.float32).astype(jnp.bfloat16),
        "head",
        scatter_dimension=0,
        tiled=True,
    )


def solution(mesh):
    placed = (
        P(("abl", "head", "ctx"), None),
        P(("abl", "ctx"), "head"),
        P(("abl", "ctx"), "head"),
        P(("abl", "ctx")),
        P("head", None),
    )
    return jax.shard_map(
        shards,
        mesh=mesh,
        in_specs=placed,
        out_specs=P(("abl", "head", "ctx"), None),
        check_vma=False,
    )
```

profile of v0, /device:TPU:0, one launch (start us, length us, event | category | flops | bytes accessed | tf_op | source)
XLA Modules:
  0.0 223.1 jit_solution(14071060724346164999)
XLA Ops:
  6.5 0.0 copy-start
  6.5 0.0 all-gather.2.cloned.1.call-start
  6.5 1.0 copy.33
  7.6 11.6 %all_to_all.19 = bf16[32,4,1536]{2,0,1:T(8,128)(2,1)} all-to-all(bf16[32,4,1536]{2,0,1:T(8,128)(2,1)S(1)} %bitcast.42), channel_id=1, replica_groups=mesh['abl'=2,'head'=4,'ctx'=4] {'head'}, dimensions={1} | all-to-all | bytes 786432 | tf_op jit(solution)/shard_map/all_to_all | solution.py:18
  19.1 0.0 all-gather.2.cloned.1.call-update
  19.2 0.0 reduce-scatter.12.cloned.1.call-start
  19.2 8.8 %copy.21 = bf16[2048,1536]{0,1:T(8,128)(2,1)} copy(bf16[2048,1536]{1,0:T(8,128)(2,1)} %param.6) | data formatting | bytes 12582912 | tf_op args[1]
  28.0 8.8 %copy.24 = bf16[2048,1536]{0,1:T(8,128)(2,1)} copy(bf16[2048,1536]{1,0:T(8,128)(2,1)} %param.7) | data formatting | bytes 12582912 | tf_op args[2]
  36.7 0.0 copy-done
  36.7 0.1 broadcast_bitcast_fusion
  36.8 20.3 %all-gather.2.cloned.1.call-done = bf16[512,1536]{1,0:T(8,128)(2,1)} async-done(((bf16[128,1536]{1,0:T(8,128)(2,1)}), bf16[512,1536]{1,0:T(8,128)(2,1)}) %all-gather.2.cloned.1.call-update) | async-done | bytes 1572880 | tf_op jit(solution)/shard_map/all_gather | solution.py:19
  57.1 1.7 copy.20
  58.8 22.6 %fusion = (f32[12,512]{1,0:T(8,128)S(1)}, f32[12,512,2048]{2,1,0:T(8,128)}) fusion(pred[2048]{0:T(1024)(128)(4,1)S(1)} %broadcast_bitcast_fusion, bf16[512,12,128]{0,2,1:T(8,128)(2,1)S(1)} %bitcast.38, bf16[2048,12,128]{0,2,1:T(8,128)(2,1)} %bitcast.37), kind=kOutput, calls=%fused_computation.2 | convolution fusion | flops 3258968064 | bytes 58222592 | tf_op jit(solution)/shard_map/qhd,khd->hqk/dot_general | solution.py:27
  81.4 16.9 %pmax.7 = f32[12,512]{1,0:T(8,128)S(1)} all-reduce(f32[12,512]{1,0:T(8,128)S(1)} %broadcast_maximum_fusion), channel_id=1, replica_groups=mesh['abl'=2,'head'=4,'ctx'=4] {'ctx'}, use_global_device_ids=true, to_apply=%region_1.2 | all-reduce | flops 6144 | bytes 49152 | tf_op jit(solution)/shard_map/pmax | solution.py:43
  98.4 21.1 %fusion.1 = f32[12,512]{1,0:T(8,128)S(1)} fusion(f32[12,512,2048]{2,1,0:T(8,128)} %get-tuple-element.9, f32[12,512]{1,0:T(8,128)S(1)} %broadcast_maximum_fusion, pred[2048]{0:T(1024)(128)(4,1)S(1)} %broadcast_bitcast_fusion), kind=kLoop, calls=%fused_computation.3 | loop fusion | flops 50325504 | bytes 50382848 | tf_op jit(solution)/shard_map/reduce_sum | solution.py:34
  119.5 0.8 copy.29
  120.3 0.0 reduce-scatter.12.cloned.1.call-update
  120.3 0.0 reduce-scatter.10.cloned.1.call-start
  120.4 22.0 %fusion.7 = bf16[512,12,128]{0,2,1:T(8,128)(2,1)S(1)} fusion(bf16[2048,12,128]{0,2,1:T(8,128)(2,1)} %bitcast.39, f32[12,512,2048]{2,1,0:T(8,128)} %get-tuple-element.9, f32[12,512]{1,0:T(8,128)S(1)} %broadcast_maximum_fusion, pred[2048]{0:T(1024)(128)(4,1)S(1)} %broadcast_bitcast_fusion, f32[512,12]{0,1:T(8,128)S(1)} %get-tuple-element.6, ...), kind=kOutput, calls=%fused_computation.10 | convolution fusion | flops 3273916416 | bytes 58271744 | tf_op jit(solution)/shard_map/hqk,khd->qhd/dot_general | solution.py:35
  142.4 1.6 copy.27
  144.0 0.0 reduce-scatter.10.cloned.1.call-update
  144.0 0.2 reduce-scatter.8.cloned.1.call-start
  144.2 0.0 reduce-scatter.12.cloned.1.call-done
  144.3 0.8 copy.30
  145.1 32.7 %reduce-scatter.10.cloned.1.call-done = bf16[128,1536]{1,0:T(8,128)(2,1)} async-done(((bf16[512,1536]{1,0:T(8,128)(2,1)}), bf16[128,1536]{1,0:T(8,128)(2,1)}) %reduce-scatter.10.cloned.1.call-update) | async-done | bytes 393232
  177.7 1.2 copy.28
  179.0 0.1 fusion.10
  179.1 10.2 %convolution_convert_fusion = bf16[128,6144]{1,0:T(8,128)(2,1)} fusion(bf16[128,1536]{0,1:T(8,128)(2,1)S(1)} %fusion.10, bf16[1536,6144]{1,0:T(8,128)(2,1)} %param.9), kind=kOutput, calls=%fused_computation.7 | convolution fusion | flops 2416705536 | bytes 20840448 | tf_op jit(solution)/shard_map/dot_general | solution.py:57
  189.3 0.0 reduce-scatter.8.cloned.1.call-update
  189.3 27.3 %reduce-scatter.8.cloned.1.call-done = bf16[32,6144]{1,0:T(8,128)(2,1)} async-done(((bf16[128,6144]{1,0:T(8,128)(2,1)}), bf16[32,6144]{1,0:T(8,128)(2,1)}) %reduce-scatter.8.cloned.1.call-update) | async-done | bytes 393232 | tf_op jit(solution)/shard_map/reduce_scatter | solution.py:56
  (4 shorter events, 0.0 us)
Async XLA Ops:
  6.5 30.2 %copy-start = (s32[16]{0:T(128)S(1)}, s32[16]{0:T(128)}, u32[]{:S(2)}) copy-start(s32[16]{0:T(128)} %param.8) | copy-start | bytes 196
  6.5 50.6 %all-gather.2.cloned.1.call-start = ((), (), s32[]{:S(2)}) async-start(), calls=%async_computation.4 | async-start | bytes 1966080 | tf_op jit(solution)/shard_map/all_gather | solution.py:19
  19.2 125.1 %reduce-scatter.12.cloned.1.call-start = ((), (), s32[]{:S(2)}) async-start(), calls=%async_computation.7 | async-start | bytes 163840
  120.3 57.4 %reduce-scatter.10.cloned.1.call-start = ((), (), s32[]{:S(2)}) async-start(), calls=%async_computation.6 | async-start | bytes 1966080
  144.0 72.6 %reduce-scatter.8.cloned.1.call-start = ((), (), s32[]{:S(2)}) async-start(), calls=%async_computation.5 | async-start | bytes 1966080 | tf_op jit(solution)/shard_map/reduce_scatter | solution.py:56
Sparse Core Ops, SparseCore 0:
  19.3 37.8 all-gather.1
  120.4 17.4 reduce-scatter.11
  144.1 33.5 reduce-scatter.9
  189.4 27.1 reduce-scatter.7
where the time goes:
time: 224 us; the launch traced here: 223 us
  waiting for transfers between devices  80.4 us (36%)
  matrix products  54.9 us (25%)
  blocking collectives  28.5 us (13%)
  local copies, waits for them, and re-layouts  24.7 us (11%)
  other arithmetic  21.2 us (9%)
  between operations  13.2 us (6%)
    unnamed x6, waiting for transfers between devices  32.7 us
    reduce_scatter x1, waiting for transfers between devices, shards(): lax.psum_scatter(jnp.dot(attended, out_weight, preferred_element_type=jnp...  27.3 us
    dot_general x1, matrix products, shards(): jnp.einsum('qhd,khd->hqk', shaped, key_heads, preferred_element_type=jnp....  22.6 us
    dot_general x1, matrix products, shards(): jnp.einsum('hqk,khd->qhd', softened.astype(jnp.bfloat16), value_heads, pr...  22 us
    unnamed x8, local copies, waits for them, and re-layouts  21.9 us
    reduce_sum x1, other arithmetic, shards(): normal_sum = jnp.sum(softened, axis=-1)  21.1 us
    all_gather x1, waiting for transfers between devices, shards(): all_queries = lax.all_gather(query_block, 'ctx', axis=0, tiled=True)  20.3 us
    pmax x1, blocking collectives, shards(): highest = lax.pmax(running, 'ctx')  16.9 us
  transfers between devices with their start and end apart: 4, of which 3 were waited for; matrix products, arithmetic and copies ran while one was open for 19% of the time, Pallas kernels for 0%

commit v1 on v0

v1 whole, which is shorter than its diff:
```python
import functools
import math

import jax
import jax.numpy as jnp
from jax import lax
from jax.experimental import pallas as pl
from jax.experimental.pallas import tpu as pltpu
from jax.sharding import PartitionSpec as P

HD = 128
LANES = 128
ROW = 128
LOW = -1e30
SCALE2 = math.log2(math.e) / math.sqrt(HD)
STEP = 32
CHUNKS = 2
TAILS = 1
VMEM = 56 << 20


def swap(x, axis, size, bit):
    return lax.ppermute(x, axis, [(i, i ^ bit) for i in range(size)])


def split_stats(stats):
    lane = lax.broadcasted_iota(jnp.int32, stats.shape, 1)
    high = stats.astype(jnp.bfloat16)
    rest = stats - high.astype(jnp.float32)
    middle = rest.astype(jnp.bfloat16)
    low = (rest - middle.astype(jnp.float32)).astype(jnp.bfloat16)
    return jnp.where(
        lane < STEP,
        high.astype(jnp.float32),
        jnp.where(lane < 2 * STEP, middle.astype(jnp.float32), low.astype(jnp.float32)),
    ).astype(jnp.bfloat16)


def join_stats(packed):
    x = packed.astype(jnp.float32)
    return x + pltpu.roll(x, LANES - STEP, 1) + pltpu.roll(x, LANES - 2 * STEP, 1)


def attend_body(kept_ref, *refs, pieces, heads, per_step):
    q_refs, (k_ref, v_ref) = refs[:pieces], refs[pieces : pieces + 2]
    o_refs, stat_ref = refs[pieces + 2 : 2 * pieces + 2], refs[-1]
    step = pl.program_id(0)
    keys = k_ref.shape[0]
    rows = q_refs[0].shape[0]
    key_row = lax.broadcasted_iota(jnp.int32, (1, keys), 1) // ROW
    bias = jnp.zeros((1, keys), jnp.float32)
    for j in range(keys // ROW):
        bias = jnp.where(key_row == j, jnp.where(kept_ref[j] > 0, 0.0, LOW), bias)
    lane = lax.broadcasted_iota(jnp.int32, (rows, LANES), 1)

    @pl.when(step == 0)
    def _():
        stat_ref[...] = jnp.zeros_like(stat_ref)

    for i in range(per_step):
        head = step * per_step + i
        columns = slice(i * HD, i * HD + HD)
        k = k_ref[:, columns]
        v = v_ref[:, columns]
        v = jnp.concatenate([v, jnp.ones_like(v)], axis=1)
        for d in range(pieces):
            scores = lax.dot_general(
                q_refs[d][:, columns], k, (((1,), (1,)), ((), ())), preferred_element_type=jnp.float32
            )
            scores = scores + bias
            highest = jnp.max(scores, axis=1, keepdims=True)
            probs = jnp.exp2((scores - highest) * SCALE2)
            both = jnp.dot(probs.astype(jnp.bfloat16), v, preferred_element_type=jnp.float32)
            total = both[:, HD:]
            o_refs[d][:, pl.ds(pl.multiple_of(head * HD, HD), HD)] = (both[:, :HD] / total).astype(jnp.bfloat16)
            stat = highest * SCALE2 + jnp.log2(total)
            stat_ref[d] = jnp.where(lane % STEP == head, stat, stat_ref[d])

    @pl.when(step == pl.num_programs(0) - 1)
    def _():
        for d in range(pieces):
            o_refs[d][:, heads * HD :] = split_stats(stat_ref[d])


def attend(kept, q_pieces, keys, values, first, heads):
    pieces = len(q_pieces)
    rows = q_pieces[0].shape[0]
    count = keys.shape[0]
    per_step = 2 if heads % 2 == 0 and first % 2 == 0 else 1
    width = (heads + 1) * HD
    offset = first // per_step
    return pl.pallas_call(
        functools.partial(attend_body, pieces=pieces, heads=heads, per_step=per_step),
        grid=(heads // per_step,),
        in_specs=[pl.BlockSpec(memory_space=pltpu.SMEM)]
        + [pl.BlockSpec((rows, per_step * HD), lambda h: (0, h))] * pieces
        + [pl.BlockSpec((count, per_step * HD), lambda h: (0, h + offset))] * 2,
        out_specs=[pl.BlockSpec((rows, width), lambda h: (0, 0))] * pieces,
        out_shape=[jax.ShapeDtypeStruct((rows, width), jnp.bfloat16)] * pieces,
        scratch_shapes=[pltpu.VMEM((pieces, rows, LANES), jnp.float32)],
        compiler_params=pltpu.CompilerParams(vmem_limit_bytes=VMEM),
        name="attend",
    )(kept, *q_pieces, keys, values)


def shares(parts, heads):
    stats = [join_stats(part[:, heads * HD :]) for part in parts]
    top = functools.reduce(jnp.maximum, stats)
    weights = [jnp.exp2(stat - top) for stat in stats]
    total = functools.reduce(jnp.add, weights)
    return [w / total for w in weights], top + jnp.log2(total)


def mix(parts, weights, h):
    columns = slice(h * HD, h * HD + HD)
    return functools.reduce(
        jnp.add, [w[:, h : h + 1] * part[:, columns].astype(jnp.float32) for w, part in zip(weights, parts)]
    )


def merge_body(*refs, heads):
    parts = [ref[...] for ref in refs[:-1]]
    weights, total = shares(parts, heads)
    for h in range(heads):
        refs[-1][:, h * HD : h * HD + HD] = mix(parts, weights, h).astype(jnp.bfloat16)
    lane = lax.broadcasted_iota(jnp.int32, total.shape, 1)
    spread = jnp.where(
        lane < STEP, total, jnp.where(lane < 2 * STEP, pltpu.roll(total, STEP, 1), pltpu.roll(total, 2 * STEP, 1))
    )
    refs[-1][:, heads * HD :] = split_stats(spread)


def merge(parts, heads):
    if len(parts) == 1:
        return parts[0]
    return pl.pallas_call(
        functools.partial(merge_body, heads=heads),
        out_shape=jax.ShapeDtypeStruct(parts[0].shape, parts[0].dtype),
        compiler_params=pltpu.CompilerParams(vmem_limit_bytes=VMEM),
        name="merge",
    )(*parts)


def project_body(*refs, counts, heads, group):
    part_refs = refs[: sum(counts)]
    w_ref, keep_ref, send_ref, attended_ref = refs[sum(counts) :]

    @pl.when(pl.program_id(0) == 0)
    def _():
        start, column = 0, 0
        for count, some in zip(counts, heads):
            parts = [ref[...] for ref in part_refs[start : start + count]]
            weights, _ = shares(parts, some)
            for h in range(some):
                attended_ref[:, column : column + HD] = mix(parts, weights, h).astype(jnp.bfloat16)
                column += HD
            start += count

    product = jnp.dot(attended_ref[...], w_ref[...], preferred_element_type=jnp.float32)
    for e in range(product.shape[0] // group):
        target = send_ref if e % 2 else keep_ref
        half = e // 2
        target[half * group : half * group + group, :] = product[e * group : e * group + group, :].astype(jnp.bfloat16)


def project(chunks, heads, weight, group, first, width):
    flat = [part for parts in chunks for part in parts]
    rows = flat[0].shape[0]
    depth = weight.shape[0]
    block = 512
    offset = first // block
    half = jax.ShapeDtypeStruct((rows // 2, width), jnp.bfloat16)
    return pl.pallas_call(
        functools.partial(project_body, counts=[len(parts) for parts in chunks], heads=heads, group=group),
        grid=(width // block,),
        in_specs=[pl.BlockSpec(part.shape, lambda n: (0, 0)) for part in flat]
        + [pl.BlockSpec((depth, block), lambda n: (0, n + offset))],
        out_specs=[pl.BlockSpec((rows // 2, block), lambda n: (0, n))] * 2,
        out_shape=[half, half],
        scratch_shapes=[pltpu.VMEM((rows, depth), jnp.bfloat16)],
        compiler_params=pltpu.CompilerParams(vmem_limit_bytes=VMEM),
        name="project",
    )(*flat, weight)


def shards(queries, keys, values, kept_rows, out_weight, *, n_head, n_ctx):
    local_heads = keys.shape[1] // HD
    group = queries.shape[0]
    rank = lax.axis_index("head")
    edges = [local_heads * i // CHUNKS for i in range(CHUNKS + 1)]
    spans = [(a, b - a) for a, b in zip(edges, edges[1:]) if b > a]

    chunks = []
    for first, heads in spans:
        mine = []
        for e in range(n_head):
            start = (rank ^ e) * (local_heads * HD) + first * HD
            part = lax.dynamic_slice(queries, (0, start), (group, heads * HD))
            mine.append(swap(part, "head", n_head, e) if e else part)
        pieces = {0: jnp.concatenate(mine, axis=0)}
        bit = n_ctx // 2
        while bit:
            pieces.update({d ^ bit: swap(x, "ctx", n_ctx, bit) for d, x in list(pieces.items())})
            bit //= 2
        chunks.append([pieces[d] for d in range(n_ctx)])

    gathered = []
    for (first, heads), q_pieces in zip(spans, chunks):
        partial = attend(kept_rows, q_pieces, keys, values, first, heads)
        waiting = {d: [x] for d, x in enumerate(partial)}
        bit = 1
        while bit < n_ctx:
            for d in reversed(sorted(d for d in waiting if d & bit)):
                waiting[d ^ bit].append(swap(merge(waiting.pop(d), heads), "ctx", n_ctx, bit))
            bit *= 2
        gathered.append(waiting[0])

    width = out_weight.shape[1]
    done = []
    for t in range(TAILS):
        size = width // TAILS
        keep, send = project(gathered, [h for _, h in spans], out_weight, group, t * size, size)
        keep = keep.astype(jnp.float32) + swap(send, "head", n_head, 1).astype(jnp.float32)
        blocks = [keep[i * group : (i + 1) * group] for i in range(n_head // 2)]
        bit = 2
        while bit < n_head:
            sent = blocks[1::2]
            blocks = [
                a + swap(b.astype(jnp.bfloat16), "head", n_head, bit).astype(jnp.float32)
                for a, b in zip(blocks[::2], sent)
            ]
            bit *= 2
        done.append(blocks[0].astype(jnp.bfloat16))
    return jnp.concatenate(done, axis=1)


def solution(mesh):
    placed = (
        P(("abl", "head", "ctx"), None),
        P(("abl", "ctx"), "head"),
        P(("abl", "ctx"), "head"),
        P(("abl", "ctx")),
        P("head", None),
    )
    return jax.shard_map(
        functools.partial(shards, n_head=mesh.shape["head"], n_ctx=mesh.shape["ctx"]),
        mesh=mesh,
        in_specs=placed,
        out_specs=P(("abl", "head", "ctx"), None),
        check_vma=False,
    )
```

time: 224 us -> 118 us (0.53)
  matrix products: 54.9 us -> 0 us
  Pallas kernels: 0 us -> 42.4 us
  waiting for transfers between devices: 80.4 us -> 39 us
  blocking collectives: 28.5 us -> 0 us
  starting transfers between devices: 0.31 us -> 27.4 us
  local copies, waits for them, and re-layouts: 24.7 us -> 5.31 us
  other arithmetic: 21.2 us -> 2.13 us
  between operations: 13.2 us -> 0.16 us
    dot_general x3 -> x0, matrix products: 54.9 us -> none  [the longest x1 22.6 us: shards(): jnp.einsum('qhd,khd->hqk', shaped, key_heads, preferred_element_type=jnp....]
    pallas_call x0 -> x5, Pallas kernels: none -> 42.4 us  [the longest x2 23.7 us: attend(): pl.pallas_call(functools.partial(attend_body, pieces=pieces, heads=heads,...]
    ppermute x0 -> x20, waiting for transfers between devices: none -> 39 us  [swap(): return lax.ppermute(x, axis, [(i, i ^ bit) for i in range(size)])]
    unnamed x6 -> x0, waiting for transfers between devices: 32.7 us -> none
    ppermute x0 -> x20, starting transfers between devices: none -> 27.4 us  [swap(): return lax.ppermute(x, axis, [(i, i ^ bit) for i in range(size)])]
    reduce_scatter x1 -> x0, waiting for transfers between devices: 27.3 us -> none  [shards(): lax.psum_scatter(jnp.dot(attended, out_weight, preferred_element_type=jnp...]
    reduce_sum x1 -> x0, other arithmetic: 21.1 us -> none  [shards(): normal_sum = jnp.sum(softened, axis=-1)]
    all_gather x1 -> x0, waiting for transfers between devices: 20.3 us -> none  [shards(): all_queries = lax.all_gather(query_block, 'ctx', axis=0, tiled=True)]
  transfers between devices with their start and end apart: 4 -> 20, of which waited for: 3 -> 8; matrix products, arithmetic and copies ran while one was open for 19% -> 0% of each run, Pallas kernels for 0% -> 24%
where the time goes in v1:
time: 118 us; the launch traced here: 116 us
  Pallas kernels  42.4 us (36%)
  waiting for transfers between devices  39 us (33%)
  starting transfers between devices  27.4 us (23%)
  local copies, waits for them, and re-layouts  5.31 us (4%)
  other arithmetic  2.13 us (2%)
    ppermute x20, waiting for transfers between devices, swap(): return lax.ppermute(x, axis, [(i, i ^ bit) for i in range(size)])  39 us
    ppermute x20, starting transfers between devices, swap(): return lax.ppermute(x, axis, [(i, i ^ bit) for i in range(size)])  27.4 us
    pallas_call x2, Pallas kernels, attend(): pl.pallas_call(functools.partial(attend_body, pieces=pieces, heads=heads,...  23.7 us
    pallas_call x1, Pallas kernels, project(): pl.pallas_call(functools.partial(project_body, counts=[len(parts) for par...  14.4 us
    pallas_call x2, Pallas kernels, merge(): pl.pallas_call(functools.partial(merge_body, heads=heads), out_shape=jax....  4.34 us
    unnamed x30, local copies, waits for them, and re-layouts  4.27 us
  transfers between devices with their start and end apart: 20, of which 8 were waited for; matrix products, arithmetic and copies ran while one was open for 0% of the time, Pallas kernels for 24%

profile of v1, /device:TPU:0, one launch (start us, length us, event | category | flops | bytes accessed | tf_op | source)
XLA Modules:
  0.0 116.4 jit_solution(4108614706079390486)
XLA Ops:
  0.0 1.0 constant_dynamic-slice_fusion.3
  1.0 2.4 %collective-permute-start.2 = (bf16[32,768]{1,0:T(8,128)(2,1)S(1)}, bf16[32,768]{1,0:T(8,128)(2,1)S(1)}, u32[]{:S(2)}, u32[]{:S(2)}) collective-permute-start(bf16[32,768]{1,0:T(8,128)(2,1)S(1)} %get-tuple-element.27), channel_id=1, source_target_pairs={{0,12},{4,8},{8,4},{12,0},{1,13},{5,9},{9,5},{13,1},{2,14},{6,10},... | collective-permute-start | bytes 147464 | tf_op jit(solution)/shard_map/ppermute | solution.py:23
  3.4 0.6 collective-permute-start.1
  4.1 0.0 collective-permute-start
  4.1 0.5 collective-permute-start.9
  4.6 1.4 %collective-permute-start.11 = (bf16[32,768]{1,0:T(8,128)(2,1)S(1)}, bf16[32,768]{1,0:T(8,128)(2,1)S(1)}, u32[]{:S(2)}, u32[]{:S(2)}) collective-permute-start(bf16[32,768]{1,0:T(8,128)(2,1)S(1)} %get-tuple-element.31), channel_id=1, source_target_pairs={{0,12},{4,8},{8,4},{12,0},{1,13},{5,9},{9,5},{13,1},{2,14},{6,10},... | collective-permute-start | bytes 147464 | tf_op jit(solution)/shard_map/ppermute | solution.py:23
  6.0 0.0 collective-permute-done.2
  6.0 2.0 %collective-permute-start.10 = (bf16[32,768]{1,0:T(8,128)(2,1)S(1)}, bf16[32,768]{1,0:T(8,128)(2,1)S(1)}, u32[]{:S(2)}, u32[]{:S(2)}) collective-permute-start(bf16[32,768]{1,0:T(8,128)(2,1)S(1)} %get-tuple-element.32), channel_id=1, source_target_pairs={{0,8},{4,12},{8,0},{12,4},{1,9},{5,13},{9,1},{13,5},{2,10},{6,14},... | collective-permute-start | bytes 147464 | tf_op jit(solution)/shard_map/ppermute | solution.py:23
  8.0 0.0 collective-permute-done.1
  8.0 0.0 collective-permute-done
  8.1 0.0 copy-start
  8.1 2.7 %collective-permute-start.4 = (bf16[128,768]{1,0:T(8,128)(2,1)S(1)}, bf16[128,768]{1,0:T(8,128)(2,1)S(1)}, u32[]{:S(2)}, u32[]{:S(2)}) collective-permute-start(bf16[128,768]{1,0:T(8,128)(2,1)S(1)} %pad_maximum_fusion.refs_0_), channel_id=1, source_target_pairs={{0,2},{1,3},{2,0},{3,1},{4,6},{5,7},{6,4},{7,5},{8,10},{9,11},{10,... | collective-permute-start | bytes 589832 | tf_op jit(solution)/shard_map/ppermute | solution.py:23
  10.7 0.0 collective-permute-done.9
  10.7 0.0 collective-permute-done.11
  10.7 0.0 collective-permute-done.10
  10.8 0.0 copy-start.1
  10.8 2.5 %collective-permute-start.13 = (bf16[128,768]{1,0:T(8,128)(2,1)S(1)}, bf16[128,768]{1,0:T(8,128)(2,1)S(1)}, u32[]{:S(2)}, u32[]{:S(2)}) collective-permute-start(bf16[128,768]{1,0:T(8,128)(2,1)S(1)} %pad_maximum_fusion.1.refs_0_), channel_id=1, source_target_pairs={{0,2},{1,3},{2,0},{3,1},{4,6},{5,7},{6,4},{7,5},{8,10},{9,11},{10,... | collective-permute-start | bytes 589832 | tf_op jit(solution)/shard_map/ppermute | solution.py:23
  13.3 1.6 %collective-permute-start.3 = (bf16[128,768]{1,0:T(8,128)(2,1)S(1)}, bf16[128,768]{1,0:T(8,128)(2,1)S(1)}, u32[]{:S(2)}, u32[]{:S(2)}) collective-permute-start(bf16[128,768]{1,0:T(8,128)(2,1)S(1)} %pad_maximum_fusion.refs_0_), channel_id=1, source_target_pairs={{0,1},{1,0},{2,3},{3,2},{4,5},{5,4},{6,7},{7,6},{8,9},{9,8},{10,11... | collective-permute-start | bytes 589832 | tf_op jit(solution)/shard_map/ppermute | solution.py:23
  14.9 10.4 %collective-permute-done.4.refs_2_ = bf16[128,768]{1,0:T(8,128)(2,1)S(1)} collective-permute-done((bf16[128,768]{1,0:T(8,128)(2,1)S(1)}, bf16[128,768]{1,0:T(8,128)(2,1)S(1)}, u32[]{:S(2)}, u32[]{:S(2)}) %collective-permute-start.4) | collective-permute-done | bytes 196640 | tf_op jit(solution)/shard_map/ppermute | solution.py:23
  25.2 0.0 collective-permute-start.5
  25.2 2.0 %collective-permute-start.12 = (bf16[128,768]{1,0:T(8,128)(2,1)S(1)}, bf16[128,768]{1,0:T(8,128)(2,1)S(1)}, u32[]{:S(2)}, u32[]{:S(2)}) collective-permute-start(bf16[128,768]{1,0:T(8,128)(2,1)S(1)} %pad_maximum_fusion.1.refs_0_), channel_id=1, source_target_pairs={{0,1},{1,0},{2,3},{3,2},{4,5},{5,4},{6,7},{7,6},{8,9},{9,8},{10,11... | collective-permute-start | bytes 589832 | tf_op jit(solution)/shard_map/ppermute | solution.py:23
  27.3 1.2 collective-permute-done.13.refs_2_
  28.4 0.6 collective-permute-start.14
  29.0 0.0 collective-permute-done.3.refs_1_
  29.0 4.1 %collective-permute-done.5.refs_3_ = bf16[128,768]{1,0:T(8,128)(2,1)S(1)} collective-permute-done((bf16[128,768]{1,0:T(8,128)(2,1)S(1)}, bf16[128,768]{1,0:T(8,128)(2,1)S(1)}, u32[]{:S(2)}, u32[]{:S(2)}) %collective-permute-start.5) | collective-permute-done | bytes 196640 | tf_op jit(solution)/shard_map/ppermute | solution.py:23
  33.1 0.0 copy-done
  33.1 0.0 copy-done.8
  33.1 0.0 copy-done.12
  33.1 0.0 copy-start.13
  33.1 0.7 copy-done.13
  33.7 11.8 %attend.2 = (bf16[128,896]{1,0:T(8,128)(2,1)}, bf16[128,896]{1,0:T(8,128)(2,1)}, bf16[128,896]{1,0:T(8,128)(2,1)}, bf16[128,896]{1,0:T(8,128)(2,1)}) custom-call(s32[16]{0:T(128)} %kept_ref.3, bf16[128,768]{1,0:T(8,128)(2,1)} %copy-done, bf16[128,768]{1,0:T(8,128)(2,1)} %copy-done.12, bf16[128,768]{1,0:T(8,128)(2,1)} %copy-done.8, ...), custom_call_target="tpu_custom_call" | custom-call | tf_op jit(solution)/shard_map/attend/pallas_call | solution.py:92
  45.6 0.1 collective-permute-start.7
  45.7 0.0 collective-permute-done.12.refs_1_
  45.7 0.0 copy-start.10
  45.7 0.0 collective-permute-done.14.refs_3_
  45.7 0.7 copy-done.10
  46.4 0.7 copy-done.11
  47.0 11.9 %attend.3 = (bf16[128,896]{1,0:T(8,128)(2,1)}, bf16[128,896]{1,0:T(8,128)(2,1)}, bf16[128,896]{1,0:T(8,128)(2,1)}, bf16[128,896]{1,0:T(8,128)(2,1)}) custom-call(s32[16]{0:T(128)} %kept_ref.3, bf16[128,768]{1,0:T(8,128)(2,1)} %copy-done.1, bf16[128,768]{1,0:T(8,128)(2,1)} %copy-done.10, bf16[128,768]{1,0:T(8,128)(2,1)} %copy-done.9, ...), custom_call_target="tpu_custom_call" | custom-call | tf_op jit(solution)/shard_map/attend/pallas_call | solution.py:92
  58.9 2.0 %collective-permute-start.16 = (bf16[128,896]{1,0:T(8,128)(2,1)}, bf16[128,896]{1,0:T(8,128)(2,1)S(1)}, u32[]{:S(2)}, u32[]{:S(2)}) collective-permute-start(bf16[128,896]{1,0:T(8,128)(2,1)} %get-tuple-element.22), channel_id=1, source_target_pairs={{0,1},{1,0},{2,3},{3,2},{4,5},{5,4},{6,7},{7,6},{8,9},{9,8},{10,11... | collective-permute-start | bytes 688136 | tf_op jit(solution)/shard_map/ppermute | solution.py:23
  60.9 0.0 copy-done.14
  60.9 0.1 collective-permute-start.6
  61.0 1.9 %collective-permute-start.15 = (bf16[128,896]{1,0:T(8,128)(2,1)}, bf16[128,896]{1,0:T(8,128)(2,1)S(1)}, u32[]{:S(2)}, u32[]{:S(2)}) collective-permute-start(bf16[128,896]{1,0:T(8,128)(2,1)} %get-tuple-element.20), channel_id=1, source_target_pairs={{0,1},{1,0},{2,3},{3,2},{4,5},{5,4},{6,7},{7,6},{8,9},{9,8},{10,11... | collective-permute-start | bytes 688136 | tf_op jit(solution)/shard_map/ppermute | solution.py:23
  62.9 0.0 collective-permute-done.7.refs_1_
  62.9 0.7 copy-done.6
  63.6 2.2 %merge.2 = bf16[128,896]{1,0:T(8,128)(2,1)} custom-call(bf16[128,896]{1,0:T(8,128)(2,1)} %get-tuple-element.17.refs_0_, bf16[128,896]{1,0:T(8,128)(2,1)} %copy-done.6), custom_call_target="tpu_custom_call" | custom-call | tf_op jit(solution)/shard_map/merge/pallas_call | solution.py:136
  65.8 1.7 %collective-permute-start.8 = (bf16[128,896]{1,0:T(8,128)(2,1)}, bf16[128,896]{1,0:T(8,128)(2,1)S(1)}, u32[]{:S(2)}, u32[]{:S(2)}) collective-permute-start(bf16[128,896]{1,0:T(8,128)(2,1)} %merge.2), channel_id=1, source_target_pairs={{0,2},{1,3},{2,0},{3,1},{4,6},{5,7},{6,4},{7,5},{8,10},{9,11},{10,... | collective-permute-start | bytes 688136 | tf_op jit(solution)/shard_map/ppermute | solution.py:23
  67.5 0.2 collective-permute-done.16.refs_1_
  67.7 0.7 copy-done.7
  68.4 2.2 %merge.3 = bf16[128,896]{1,0:T(8,128)(2,1)} custom-call(bf16[128,896]{1,0:T(8,128)(2,1)} %get-tuple-element.21.refs_0_, bf16[128,896]{1,0:T(8,128)(2,1)} %copy-done.7), custom_call_target="tpu_custom_call" | custom-call | tf_op jit(solution)/shard_map/merge/pallas_call | solution.py:136
  70.5 3.5 %collective-permute-start.17 = (bf16[128,896]{1,0:T(8,128)(2,1)}, bf16[128,896]{1,0:T(8,128)(2,1)S(1)}, u32[]{:S(2)}, u32[]{:S(2)}) collective-permute-start(bf16[128,896]{1,0:T(8,128)(2,1)} %merge.3), channel_id=1, source_target_pairs={{0,2},{1,3},{2,0},{3,1},{4,6},{5,7},{6,4},{7,5},{8,10},{9,11},{10,... | collective-permute-start | bytes 688136 | tf_op jit(solution)/shard_map/ppermute | solution.py:23
  74.1 8.3 %collective-permute-done.6.refs_1_ = bf16[128,896]{1,0:T(8,128)(2,1)S(1)} collective-permute-done((bf16[128,896]{1,0:T(8,128)(2,1)S(1)}, bf16[128,896]{1,0:T(8,128)(2,1)S(1)}, u32[]{:S(2)}, u32[]{:S(2)}) %collective-permute-start.6) | collective-permute-done | bytes 229408 | tf_op jit(solution)/shard_map/ppermute | solution.py:23
  82.4 2.9 %collective-permute-done.15.refs_4_ = bf16[128,896]{1,0:T(8,128)(2,1)S(1)} collective-permute-done((bf16[128,896]{1,0:T(8,128)(2,1)}, bf16[128,896]{1,0:T(8,128)(2,1)S(1)}, u32[]{:S(2)}, u32[]{:S(2)}) %collective-permute-start.15) | collective-permute-done | bytes 229408 | tf_op jit(solution)/shard_map/ppermute | solution.py:23
  85.3 0.0 collective-permute-done.8.refs_2_
  85.3 0.0 collective-permute-done.17.refs_5_
  85.3 0.7 copy-done.3
  86.0 0.1 copy-done.4
  86.1 0.1 copy-done.5
  86.2 14.4 %project.1 = (bf16[64,6144]{1,0:T(8,128)(2,1)}, bf16[64,6144]{1,0:T(8,128)(2,1)}) custom-call(bf16[128,896]{1,0:T(8,128)(2,1)} %get-tuple-element.15.refs_0_, bf16[128,896]{1,0:T(8,128)(2,1)} %copy-done.2, bf16[128,896]{1,0:T(8,128)(2,1)} %copy-done.4, bf16[128,896]{1,0:T(8,128)(2,1)} %get-tuple-element.19.refs_3_, bf16[128,896]{1,0:T(8,128)(2,1)} %copy-done.3, ...), custom_call_target="tpu_custom_call" | custom-call | tf_op jit(solution)/shard_map/project/pallas_call | solution.py:173
  100.6 0.0 collective-permute-start.18
  100.6 2.5 %collective-permute-done.18 = bf16[64,6144]{1,0:T(8,128)(2,1)S(1)} collective-permute-done((bf16[64,6144]{1,0:T(8,128)(2,1)}, bf16[64,6144]{1,0:T(8,128)(2,1)S(1)}, u32[]{:S(2)}, u32[]{:S(2)}) %collective-permute-start.18) | collective-permute-done | bytes 786464 | tf_op jit(solution)/shard_map/ppermute | solution.py:23
  103.1 1.3 %convert_add_fusion = f32[64,6144]{1,0:T(8,128)S(1)} fusion(bf16[64,6144]{1,0:T(8,128)(2,1)S(1)} %collective-permute-done.18, bf16[64,6144]{1,0:T(8,128)(2,1)} %get-tuple-element.23), kind=kLoop, calls=%fused_computation | loop fusion | flops 1179648 | bytes 3145728 | tf_op jit(solution)/shard_map/add | solution.py:223
  104.4 1.7 %collective-permute-start.19 = (bf16[32,6144]{1,0:T(8,128)(2,1)S(1)}, bf16[32,6144]{1,0:T(8,128)(2,1)S(1)}, u32[]{:S(2)}, u32[]{:S(2)}) collective-permute-start(bf16[32,6144]{1,0:T(8,128)(2,1)S(1)} %slice.15), channel_id=1, source_target_pairs={{0,8},{4,12},{8,0},{12,4},{1,9},{5,13},{9,1},{13,5},{2,10},{6,14},... | collective-permute-start | bytes 1179656 | tf_op jit(solution)/shard_map/ppermute | solution.py:23
  106.1 9.5 %collective-permute-done.19 = bf16[32,6144]{1,0:T(8,128)(2,1)S(1)} collective-permute-done((bf16[32,6144]{1,0:T(8,128)(2,1)S(1)}, bf16[32,6144]{1,0:T(8,128)(2,1)S(1)}, u32[]{:S(2)}, u32[]{:S(2)}) %collective-permute-start.19) | collective-permute-done | bytes 393248 | tf_op jit(solution)/shard_map/ppermute | solution.py:23
  115.6 0.8 fusion
  (17 shorter events, 0.1 us)
Async XLA Ops:
  1.0 5.0 %collective-permute-start.2 = (bf16[32,768]{1,0:T(8,128)(2,1)S(1)}, bf16[32,768]{1,0:T(8,128)(2,1)S(1)}, u32[]{:S(2)}, u32[]{:S(2)}) collective-permute-start(bf16[32,768]{1,0:T(8,128)(2,1)S(1)} %get-tuple-element.27), channel_id=1, source_target_pairs={{0,12},{4,8},{8,4},{12,0},{1,13},{5,9},{9,5},{13,1},{2,14},{6,10},... | collective-permute-start | bytes 147464 | tf_op jit(solution)/shard_map/ppermute | solution.py:23
  3.4 4.6 %collective-permute-start.1 = (bf16[32,768]{1,0:T(8,128)(2,1)S(1)}, bf16[32,768]{1,0:T(8,128)(2,1)S(1)}, u32[]{:S(2)}, u32[]{:S(2)}) collective-permute-start(bf16[32,768]{1,0:T(8,128)(2,1)S(1)} %get-tuple-element.28), channel_id=1, source_target_pairs={{0,8},{4,12},{8,0},{12,4},{1,9},{5,13},{9,1},{13,5},{2,10},{6,14},... | collective-permute-start | bytes 147464 | tf_op jit(solution)/shard_map/ppermute | solution.py:23
  4.1 4.0 %collective-permute-start = (bf16[32,768]{1,0:T(8,128)(2,1)S(1)}, bf16[32,768]{1,0:T(8,128)(2,1)S(1)}, u32[]{:S(2)}, u32[]{:S(2)}) collective-permute-start(bf16[32,768]{1,0:T(8,128)(2,1)S(1)} %get-tuple-element.29), channel_id=1, source_target_pairs={{0,4},{4,0},{8,12},{12,8},{1,5},{5,1},{9,13},{13,9},{2,6},{6,2},{1... | collective-permute-start | bytes 147464 | tf_op jit(solution)/shard_map/ppermute | solution.py:23
  4.1 6.6 %collective-permute-start.9 = (bf16[32,768]{1,0:T(8,128)(2,1)S(1)}, bf16[32,768]{1,0:T(8,128)(2,1)S(1)}, u32[]{:S(2)}, u32[]{:S(2)}) collective-permute-start(bf16[32,768]{1,0:T(8,128)(2,1)S(1)} %get-tuple-element.26), channel_id=1, source_target_pairs={{0,4},{4,0},{8,12},{12,8},{1,5},{5,1},{9,13},{13,9},{2,6},{6,2},{1... | collective-permute-start | bytes 147464 | tf_op jit(solution)/shard_map/ppermute | solution.py:23
  4.6 6.1 %collective-permute-start.11 = (bf16[32,768]{1,0:T(8,128)(2,1)S(1)}, bf16[32,768]{1,0:T(8,128)(2,1)S(1)}, u32[]{:S(2)}, u32[]{:S(2)}) collective-permute-start(bf16[32,768]{1,0:T(8,128)(2,1)S(1)} %get-tuple-element.31), channel_id=1, source_target_pairs={{0,12},{4,8},{8,4},{12,0},{1,13},{5,9},{9,5},{13,1},{2,14},{6,10},... | collective-permute-start | bytes 147464 | tf_op jit(solution)/shard_map/ppermute | solution.py:23
  6.0 4.7 %collective-permute-start.10 = (bf16[32,768]{1,0:T(8,128)(2,1)S(1)}, bf16[32,768]{1,0:T(8,128)(2,1)S(1)}, u32[]{:S(2)}, u32[]{:S(2)}) collective-permute-start(bf16[32,768]{1,0:T(8,128)(2,1)S(1)} %get-tuple-element.32), channel_id=1, source_target_pairs={{0,8},{4,12},{8,0},{12,4},{1,9},{5,13},{9,1},{13,5},{2,10},{6,14},... | collective-permute-start | bytes 147464 | tf_op jit(solution)/shard_map/ppermute | solution.py:23
  8.1 25.0 %copy-start = (bf16[128,768]{1,0:T(8,128)(2,1)}, bf16[128,768]{1,0:T(8,128)(2,1)S(1)}, u32[]{:S(2)}) copy-start(bf16[128,768]{1,0:T(8,128)(2,1)S(1)} %pad_maximum_fusion.refs_0_) | copy-start | bytes 589828
  8.1 17.2 %collective-permute-start.4 = (bf16[128,768]{1,0:T(8,128)(2,1)S(1)}, bf16[128,768]{1,0:T(8,128)(2,1)S(1)}, u32[]{:S(2)}, u32[]{:S(2)}) collective-permute-start(bf16[128,768]{1,0:T(8,128)(2,1)S(1)} %pad_maximum_fusion.refs_0_), channel_id=1, source_target_pairs={{0,2},{1,3},{2,0},{3,1},{4,6},{5,7},{6,4},{7,5},{8,10},{9,11},{10,... | collective-permute-start | bytes 589832 | tf_op jit(solution)/shard_map/ppermute | solution.py:23
  10.8 34.8 %copy-start.1 = (bf16[128,768]{1,0:T(8,128)(2,1)}, bf16[128,768]{1,0:T(8,128)(2,1)S(1)}, u32[]{:S(2)}) copy-start(bf16[128,768]{1,0:T(8,128)(2,1)S(1)} %pad_maximum_fusion.1.refs_0_) | copy-start | bytes 589828
  10.8 17.6 %collective-permute-start.13 = (bf16[128,768]{1,0:T(8,128)(2,1)S(1)}, bf16[128,768]{1,0:T(8,128)(2,1)S(1)}, u32[]{:S(2)}, u32[]{:S(2)}) collective-permute-start(bf16[128,768]{1,0:T(8,128)(2,1)S(1)} %pad_maximum_fusion.1.refs_0_), channel_id=1, source_target_pairs={{0,2},{1,3},{2,0},{3,1},{4,6},{5,7},{6,4},{7,5},{8,10},{9,11},{10,... | collective-permute-start | bytes 589832 | tf_op jit(solution)/shard_map/ppermute | solution.py:23
  13.3 15.7 %collective-permute-start.3 = (bf16[128,768]{1,0:T(8,128)(2,1)S(1)}, bf16[128,768]{1,0:T(8,128)(2,1)S(1)}, u32[]{:S(2)}, u32[]{:S(2)}) collective-permute-start(bf16[128,768]{1,0:T(8,128)(2,1)S(1)} %pad_maximum_fusion.refs_0_), channel_id=1, source_target_pairs={{0,1},{1,0},{2,3},{3,2},{4,5},{5,4},{6,7},{7,6},{8,9},{9,8},{10,11... | collective-permute-start | bytes 589832 | tf_op jit(solution)/shard_map/ppermute | solution.py:23
  25.2 7.8 %copy-start.8 = (bf16[128,768]{1,0:T(8,128)(2,1)}, bf16[128,768]{1,0:T(8,128)(2,1)S(1)}, u32[]{:S(2)}) copy-start(bf16[128,768]{1,0:T(8,128)(2,1)S(1)} %collective-permute-done.4.refs_2_) | copy-start | bytes 589828
  25.2 7.8 %collective-permute-start.5 = (bf16[128,768]{1,0:T(8,128)(2,1)S(1)}, bf16[128,768]{1,0:T(8,128)(2,1)S(1)}, u32[]{:S(2)}, u32[]{:S(2)}) collective-permute-start(bf16[128,768]{1,0:T(8,128)(2,1)S(1)} %collective-permute-done.4.refs_2_), channel_id=1, source_target_pairs={{0,1},{1,0},{2,3},{3,2},{4,5},{5,4},{6,7},{7,6},{8,9},{9,8},{10,11... | collective-permute-start | bytes 589832 | tf_op jit(solution)/shard_map/ppermute | solution.py:23
  25.2 20.4 %collective-permute-start.12 = (bf16[128,768]{1,0:T(8,128)(2,1)S(1)}, bf16[128,768]{1,0:T(8,128)(2,1)S(1)}, u32[]{:S(2)}, u32[]{:S(2)}) collective-permute-start(bf16[128,768]{1,0:T(8,128)(2,1)S(1)} %pad_maximum_fusion.1.refs_0_), channel_id=1, source_target_pairs={{0,1},{1,0},{2,3},{3,2},{4,5},{5,4},{6,7},{7,6},{8,9},{9,8},{10,11... | collective-permute-start | bytes 589832 | tf_op jit(solution)/shard_map/ppermute | solution.py:23
  28.4 17.2 %copy-start.9 = (bf16[128,768]{1,0:T(8,128)(2,1)}, bf16[128,768]{1,0:T(8,128)(2,1)S(1)}, u32[]{:S(2)}) copy-start(bf16[128,768]{1,0:T(8,128)(2,1)S(1)} %collective-permute-done.13.refs_2_) | copy-start | bytes 589828
  28.4 17.3 %collective-permute-start.14 = (bf16[128,768]{1,0:T(8,128)(2,1)S(1)}, bf16[128,768]{1,0:T(8,128)(2,1)S(1)}, u32[]{:S(2)}, u32[]{:S(2)}) collective-permute-start(bf16[128,768]{1,0:T(8,128)(2,1)S(1)} %collective-permute-done.13.refs_2_), channel_id=1, source_target_pairs={{0,1},{1,0},{2,3},{3,2},{4,5},{5,4},{6,7},{7,6},{8,9},{9,8},{10,11... | collective-permute-start | bytes 589832 | tf_op jit(solution)/shard_map/ppermute | solution.py:23
  29.0 4.1 %copy-start.12 = (bf16[128,768]{1,0:T(8,128)(2,1)}, bf16[128,768]{1,0:T(8,128)(2,1)S(1)}, u32[]{:S(2)}) copy-start(bf16[128,768]{1,0:T(8,128)(2,1)S(1)} %collective-permute-done.3.refs_1_) | copy-start | bytes 589828
  33.1 0.7 copy-start.13
  45.6 15.3 %copy-start.14 = (bf16[128,896]{1,0:T(8,128)(2,1)S(1)}, bf16[128,896]{1,0:T(8,128)(2,1)}, u32[]{:S(2)}) copy-start(bf16[128,896]{1,0:T(8,128)(2,1)} %get-tuple-element.16) | copy-start | bytes 688132
  45.6 17.3 %collective-permute-start.7 = (bf16[128,896]{1,0:T(8,128)(2,1)}, bf16[128,896]{1,0:T(8,128)(2,1)S(1)}, u32[]{:S(2)}, u32[]{:S(2)}) collective-permute-start(bf16[128,896]{1,0:T(8,128)(2,1)} %get-tuple-element.18), channel_id=1, source_target_pairs={{0,1},{1,0},{2,3},{3,2},{4,5},{5,4},{6,7},{7,6},{8,9},{9,8},{10,11... | collective-permute-start | bytes 688136 | tf_op jit(solution)/shard_map/ppermute | solution.py:23
  45.7 0.7 copy-start.10
  46.4 0.7 copy-start.11
  58.9 8.8 %collective-permute-start.16 = (bf16[128,896]{1,0:T(8,128)(2,1)}, bf16[128,896]{1,0:T(8,128)(2,1)S(1)}, u32[]{:S(2)}, u32[]{:S(2)}) collective-permute-start(bf16[128,896]{1,0:T(8,128)(2,1)} %get-tuple-element.22), channel_id=1, source_target_pairs={{0,1},{1,0},{2,3},{3,2},{4,5},{5,4},{6,7},{7,6},{8,9},{9,8},{10,11... | collective-permute-start | bytes 688136 | tf_op jit(solution)/shard_map/ppermute | solution.py:23
  60.9 21.5 %collective-permute-start.6 = (bf16[128,896]{1,0:T(8,128)(2,1)S(1)}, bf16[128,896]{1,0:T(8,128)(2,1)S(1)}, u32[]{:S(2)}, u32[]{:S(2)}) collective-permute-start(bf16[128,896]{1,0:T(8,128)(2,1)S(1)} %copy-done.14), channel_id=1, source_target_pairs={{0,1},{1,0},{2,3},{3,2},{4,5},{5,4},{6,7},{7,6},{8,9},{9,8},{10,11... | collective-permute-start | bytes 688136 | tf_op jit(solution)/shard_map/ppermute | solution.py:23
  61.0 24.3 %collective-permute-start.15 = (bf16[128,896]{1,0:T(8,128)(2,1)}, bf16[128,896]{1,0:T(8,128)(2,1)S(1)}, u32[]{:S(2)}, u32[]{:S(2)}) collective-permute-start(bf16[128,896]{1,0:T(8,128)(2,1)} %get-tuple-element.20), channel_id=1, source_target_pairs={{0,1},{1,0},{2,3},{3,2},{4,5},{5,4},{6,7},{7,6},{8,9},{9,8},{10,11... | collective-permute-start | bytes 688136 | tf_op jit(solution)/shard_map/ppermute | solution.py:23
  62.9 0.7 copy-start.6
  65.8 19.5 %collective-permute-start.8 = (bf16[128,896]{1,0:T(8,128)(2,1)}, bf16[128,896]{1,0:T(8,128)(2,1)S(1)}, u32[]{:S(2)}, u32[]{:S(2)}) collective-permute-start(bf16[128,896]{1,0:T(8,128)(2,1)} %merge.2), channel_id=1, source_target_pairs={{0,2},{1,3},{2,0},{3,1},{4,6},{5,7},{6,4},{7,5},{8,10},{9,11},{10,... | collective-permute-start | bytes 688136 | tf_op jit(solution)/shard_map/ppermute | solution.py:23
  67.7 0.7 copy-start.7
  70.5 14.8 %collective-permute-start.17 = (bf16[128,896]{1,0:T(8,128)(2,1)}, bf16[128,896]{1,0:T(8,128)(2,1)S(1)}, u32[]{:S(2)}, u32[]{:S(2)}) collective-permute-start(bf16[128,896]{1,0:T(8,128)(2,1)} %merge.3), channel_id=1, source_target_pairs={{0,2},{1,3},{2,0},{3,1},{4,6},{5,7},{6,4},{7,5},{8,10},{9,11},{10,... | collective-permute-start | bytes 688136 | tf_op jit(solution)/shard_map/ppermute | solution.py:23
  82.4 2.9 %copy-start.2 = (bf16[128,896]{1,0:T(8,128)(2,1)}, bf16[128,896]{1,0:T(8,128)(2,1)S(1)}, u32[]{:S(2)}) copy-start(bf16[128,896]{1,0:T(8,128)(2,1)S(1)} %collective-permute-done.6.refs_1_) | copy-start | bytes 688132
  85.3 0.7 copy-start.3
  85.3 0.8 copy-start.4
  85.3 0.8 copy-start.5
  100.6 2.5 %collective-permute-start.18 = (bf16[64,6144]{1,0:T(8,128)(2,1)}, bf16[64,6144]{1,0:T(8,128)(2,1)S(1)}, u32[]{:S(2)}, u32[]{:S(2)}) collective-permute-start(bf16[64,6144]{1,0:T(8,128)(2,1)} %get-tuple-element.24), channel_id=1, source_target_pairs={{0,4},{4,0},{8,12},{12,8},{1,5},{5,1},{9,13},{13,9},{2,6},{6,2},{1... | collective-permute-start | bytes 2359304 | tf_op jit(solution)/shard_map/ppermute | solution.py:23
  104.4 11.2 %collective-permute-start.19 = (bf16[32,6144]{1,0:T(8,128)(2,1)S(1)}, bf16[32,6144]{1,0:T(8,128)(2,1)S(1)}, u32[]{:S(2)}, u32[]{:S(2)}) collective-permute-start(bf16[32,6144]{1,0:T(8,128)(2,1)S(1)} %slice.15), channel_id=1, source_target_pairs={{0,8},{4,12},{8,0},{12,4},{1,9},{5,13},{9,1},{13,5},{2,10},{6,14},... | collective-permute-start | bytes 1179656 | tf_op jit(solution)/shard_map/ppermute | solution.py:23

commit v2 on v0

v2 whole, which is shorter than its diff:
```python
import functools
import math

import jax
import jax.numpy as jnp
from jax import lax
from jax.experimental import pallas as pl
from jax.experimental.pallas import tpu as pltpu
from jax.sharding import PartitionSpec as P

HD = 128
LANES = 128
ROW = 128
LOW = -1e30
SCALE2 = math.log2(math.e) / math.sqrt(HD)
STEP = 32
BLOCK = 512
CUTS = 2
TILE = 128
VMEM = 10 << 20


WHOLE = pl.BlockSpec(memory_space=pltpu.VMEM)


def near(x):
    return pltpu.with_memory_space_constraint(x, pltpu.VMEM)


def swap(x, axis, size, bit):
    return lax.ppermute(x, axis, [(i, i ^ bit) for i in range(size)])


def split_stats(stats):
    lane = lax.broadcasted_iota(jnp.int32, stats.shape, 1)
    high = stats.astype(jnp.bfloat16)
    rest = stats - high.astype(jnp.float32)
    middle = rest.astype(jnp.bfloat16)
    low = (rest - middle.astype(jnp.float32)).astype(jnp.bfloat16)
    return jnp.where(
        lane < STEP,
        high.astype(jnp.float32),
        jnp.where(lane < 2 * STEP, middle.astype(jnp.float32), low.astype(jnp.float32)),
    ).astype(jnp.bfloat16)


def join_stats(packed):
    x = packed.astype(jnp.float32)
    return x + pltpu.roll(x, LANES - STEP, 1) + pltpu.roll(x, LANES - 2 * STEP, 1)


def attend_body(kept_ref, *refs, pieces, heads, loads):
    q_refs, (k_ref, v_ref) = refs[:pieces], refs[pieces : pieces + 2]
    o_refs = refs[pieces + 2 : 2 * pieces + 2]
    copies = []
    if loads:
        sources, (k_ref, v_ref, sems) = (k_ref, v_ref), refs[2 * pieces + 2 :]
        for i in range(heads):
            here = pl.ds(i * HD, HD)
            for n, (source, target) in enumerate(zip(sources, (k_ref, v_ref))):
                copies.append(pltpu.make_async_copy(source.at[:, here], target.at[:, here], sems.at[n, i]))
                copies[-1].start()
    keys = k_ref.shape[0]
    rows = q_refs[0].shape[0]
    key_row = lax.broadcasted_iota(jnp.int32, (1, keys), 1) // ROW
    bias = jnp.zeros((1, keys), jnp.float32)
    for j in range(keys // ROW):
        bias = jnp.where(key_row == j, jnp.where(kept_ref[j] > 0, 0.0, LOW), bias)
    together = max(1, min(pieces, TILE // rows))
    tiles = [range(d, min(d + together, pieces)) for d in range(0, pieces, together)]
    work = [(i, tile) for i in range(heads) for tile in tiles]
    lane = lax.broadcasted_iota(jnp.int32, (together * rows, LANES), 1)
    stats = {tile: jnp.zeros((len(tile) * rows, LANES), jnp.float32) for tile in tiles}

    def score(i, tile):
        if loads and tile is tiles[0]:
            copies[2 * i].wait()
            copies[2 * i + 1].wait()
        here = slice(i * HD, i * HD + HD)
        q = [q_refs[d][:, here] for d in tile]
        q = q[0] if len(q) == 1 else jnp.concatenate(q, axis=0)
        return lax.dot_general(q, k_ref[:, here], (((1,), (1,)), ((), ())), preferred_element_type=jnp.float32) + bias

    scores = score(*work[0])
    for at, (i, tile) in enumerate(work):
        following = score(*work[at + 1]) if at + 1 < len(work) else None
        here = slice(i * HD, i * HD + HD)
        v = v_ref[:, here]
        v = jnp.concatenate([v, jnp.ones_like(v)], axis=1)
        highest = jnp.max(scores, axis=1, keepdims=True)
        probs = jnp.exp2((scores - highest) * SCALE2)
        both = jnp.dot(probs.astype(jnp.bfloat16), v, preferred_element_type=jnp.float32)
        total = both[:, HD:]
        mixed = (both[:, :HD] / total).astype(jnp.bfloat16)
        stat = highest * SCALE2 + jnp.log2(total)
        for n, d in enumerate(tile):
            o_refs[d][:, here] = mixed[n * rows : n * rows + rows]
        stats[tile] = jnp.where(lane[: len(tile) * rows] % STEP == i, stat, stats[tile])
        scores = following
    for tile in tiles:
        packed = split_stats(stats[tile])
        for n, d in enumerate(tile):
            o_refs[d][:, heads * HD :] = packed[n * rows : n * rows + rows]


def attend(kept, q_pieces, keys, values, loads):
    pieces = len(q_pieces)
    rows = q_pieces[0].shape[0]
    count = keys.shape[0]
    heads = keys.shape[1] // HD
    source = pl.BlockSpec(memory_space=pltpu.HBM) if loads else WHOLE
    out = [jax.ShapeDtypeStruct((rows, (heads + 1) * HD), jnp.bfloat16)] * pieces
    if loads:
        out += [pltpu.VMEM(keys.shape, keys.dtype), pltpu.VMEM(values.shape, values.dtype)]
    return pl.pallas_call(
        functools.partial(attend_body, pieces=pieces, heads=heads, loads=loads),
        in_specs=[pl.BlockSpec(memory_space=pltpu.SMEM)] + [WHOLE] * pieces + [source] * 2,
        out_specs=[WHOLE] * len(out),
        out_shape=out,
        scratch_shapes=[pltpu.SemaphoreType.DMA((2, heads))] if loads else [],
        compiler_params=pltpu.CompilerParams(vmem_limit_bytes=10 << 20),
        cost_estimate=pl.CostEstimate(
            flops=16 * pieces * rows * count * HD * heads,
            transcendentals=pieces * rows * count * heads,
            bytes_accessed=4 * count * HD * heads,
        ),
        name="attend",
    )(kept, *map(near, q_pieces), keys, values)


def shares(parts, heads):
    stats = [join_stats(part[:, heads * HD :]) for part in parts]
    top = functools.reduce(jnp.maximum, stats)
    weights = [jnp.exp2(stat - top) for stat in stats]
    total = functools.reduce(jnp.add, weights)
    return [w / total for w in weights], top + jnp.log2(total)


def mix(parts, weights, h):
    columns = slice(h * HD, h * HD + HD)
    return functools.reduce(
        jnp.add, [w[:, h : h + 1] * part[:, columns].astype(jnp.float32) for w, part in zip(weights, parts)]
    )


def project_body(*refs, count, heads, group):
    parts = [ref[...] for ref in refs[:count]]
    w_ref, *out_refs = refs[count:]
    weights, _ = shares(parts, heads)
    mixed = [mix(parts, weights, h).astype(jnp.bfloat16) for h in range(heads)]
    attended = mixed[0] if heads == 1 else jnp.concatenate(mixed, axis=1)
    for n in range(0, w_ref.shape[1], BLOCK):
        here = slice(n, n + BLOCK)
        product = jnp.dot(attended, w_ref[:, here], preferred_element_type=jnp.float32)
        for e in range(product.shape[0] // group):
            half = e // 2 * group
            out_refs[e % 2][half : half + group, here] = product[e * group : e * group + group].astype(jnp.bfloat16)


def project(parts, weight, group):
    rows = parts[0].shape[0]
    width = weight.shape[1]
    half = jax.ShapeDtypeStruct((rows // 2, width), jnp.bfloat16)
    return pl.pallas_call(
        functools.partial(project_body, count=len(parts), heads=weight.shape[0] // HD, group=group),
        in_specs=[WHOLE] * (len(parts) + 1),
        out_specs=[WHOLE] * 2,
        out_shape=[half, half],
        compiler_params=pltpu.CompilerParams(vmem_limit_bytes=VMEM),
        cost_estimate=pl.CostEstimate(flops=0, transcendentals=0, bytes_accessed=0),
        name="project",
    )(*map(near, parts), weight)


def exchange(blocks, size, bit):
    out = [t for t in sorted(blocks) if t & bit]
    rows = blocks[0].shape[0]
    got = swap(jnp.concatenate([blocks[t] for t in out], axis=0), "head", size, bit)
    kept = {t: x for t, x in blocks.items() if not t & bit}
    for i, t in enumerate(out):
        kept[t ^ bit] = jnp.concatenate([kept[t ^ bit], got[i * rows : i * rows + rows]], axis=0)
    return kept


def far(x, size):
    return {0: x, size // 2: swap(x, "ctx", size, size // 2)}


def near_side(pieces, size):
    return {1: swap(pieces[0], "ctx", size, 1), **pieces}


def rest(pieces, size):
    pieces = dict(pieces)
    bit = size // 4
    while bit:
        for d, piece in list(pieces.items()):
            if d ^ bit not in pieces:
                pieces[d ^ bit] = swap(piece, "ctx", size, bit)
        bit //= 2
    return pieces


def fold(keep, send, size, top, group):
    bit = 1
    while bit < top:
        wide = send.shape[1] // CUTS
        got = [swap(send[:, n * wide : n * wide + wide], "head", size, bit) for n in range(CUTS)]
        got = jnp.concatenate(got, axis=1)
        total = keep.astype(jnp.float32) + got.astype(jnp.float32)
        bit *= 2
        if bit < top:
            blocks = [total[i : i + group] for i in range(0, total.shape[0], group)]
            keep = jnp.concatenate(blocks[::2], axis=0)
            send = jnp.concatenate(blocks[1::2], axis=0).astype(jnp.bfloat16)
    return total.astype(jnp.bfloat16)


def shards(queries, keys, values, kept_rows, out_weight, *, n_head, n_ctx):
    local_heads = keys.shape[1] // HD
    columns = local_heads * HD
    group = queries.shape[0]
    rank = lax.axis_index("head")
    out_weight = near(out_weight)
    keys = pltpu.with_memory_space_constraint(keys, pltpu.HBM)
    values = pltpu.with_memory_space_constraint(values, pltpu.HBM)
    top = n_head // 2

    blocks = {t: lax.dynamic_slice(queries, (0, (rank ^ t) * columns), (group, columns)) for t in range(n_head)}
    bit = 1
    while bit < top:
        blocks = exchange(blocks, n_head, bit)
        bit *= 2
    own, other = {0: blocks[0]}, {0: swap(blocks[top], "head", n_head, top)}
    own[1] = swap(own[0], "ctx", n_ctx, 1)
    other = near_side(far(other[0], n_ctx), n_ctx)

    def run(side, pieces, need):
        nonlocal kept_rows, keys, values
        loads = not need
        q = [side[d] for d in pieces]
        q, kept_rows, _ = lax.optimization_barrier((q, kept_rows, need))
        out = attend(kept_rows, q, keys, values, loads)
        if loads:
            *out, keys, values = out
            keys, values = near(keys), near(values)
        kept_rows, out = lax.optimization_barrier((kept_rows, out))
        return dict(zip(pieces, out))

    def send(pieces):
        return [x if d == 0 else swap(x, "ctx", n_ctx, d) for d, x in sorted(pieces.items(), reverse=True)]

    low, high = (0, 1), tuple(range(2, n_ctx))
    made = run(own, low, [])
    mine = send(made)
    other_far, gate = lax.optimization_barrier((other[n_ctx // 2], made[0]))
    other[n_ctx // 2] = other_far
    other = rest(other, n_ctx)
    own[0] = lax.optimization_barrier((own[0], gate))[0]
    own[n_ctx // 2] = swap(own[0], "ctx", n_ctx, n_ctx // 2)
    made = run(other, low, [made[0]])
    theirs = send(made)
    own[n_ctx // 2] = lax.optimization_barrier((own[n_ctx // 2], made[0]))[0]
    own = rest(own, n_ctx)
    made = run(other, high, mine)
    theirs += send(made)
    made = run(own, high, theirs[:2])
    mine += send(made)

    theirs, _ = lax.optimization_barrier((theirs, made[2]))
    done = project(theirs, out_weight, group)
    done = fold(*done, n_head, top, group)
    mine, done = lax.optimization_barrier((mine, done))
    other = swap(done, "head", n_head, top)
    done = project(mine, out_weight, group)
    done = fold(*done, n_head, top, group)
    return (done.astype(jnp.float32) + other.astype(jnp.float32)).astype(jnp.bfloat16)


def solution(mesh):
    placed = (
        P(("abl", "head", "ctx"), None),
        P(("abl", "ctx"), "head"),
        P(("abl", "ctx"), "head"),
        P(("abl", "ctx")),
        P("head", None),
    )
    return jax.shard_map(
        functools.partial(shards, n_head=mesh.shape["head"], n_ctx=mesh.shape["ctx"]),
        mesh=mesh,
        in_specs=placed,
        out_specs=P(("abl", "head", "ctx"), None),
        check_vma=False,
    )
```

time: 224 us -> 96 us (0.43)
  the two profiles are of different devices: /device:TPU:0 before, /device:TPU:8 now
where the time goes in v2:
time: 96 us; the launch traced here: 95.9 us
  waiting for transfers between devices  36.9 us (38%)
  Pallas kernels  30.4 us (32%)
  starting transfers between devices  25.5 us (27%)
  local copies, waits for them, and re-layouts  1.81 us (2%)
  other arithmetic  1.03 us (1%)
    ppermute x19, waiting for transfers between devices, swap(): return lax.ppermute(x, axis, [(i, i ^ bit) for i in range(size)])  36.9 us
    ppermute x19, starting transfers between devices, swap(): return lax.ppermute(x, axis, [(i, i ^ bit) for i in range(size)])  25.5 us
    pallas_call x4, Pallas kernels, attend(): pl.pallas_call(functools.partial(attend_body, pieces=pieces, heads=heads,...  22.7 us
    pallas_call x2, Pallas kernels, project(): pl.pallas_call(functools.partial(project_body, count=len(parts), heads=we...  7.75 us
  transfers between devices with their start and end apart: 19, of which 9 were waited for; matrix products, arithmetic and copies ran while one was open for 0% of the time, Pallas kernels for 28%

profile of v2, /device:TPU:8, one launch (start us, length us, event | category | flops | bytes accessed | tf_op | source)
XLA Modules:
  0.0 95.9 jit_solution(11535175137025319354)
XLA Ops:
  0.0 1.1 %constant_dynamic-slice_fusion = (bf16[32,1536]{1,0:T(8,128)(2,1)S(1)}, bf16[32,1536]{1,0:T(8,128)(2,1)S(1)}, bf16[32,1536]{1,0:T(8,128)(2,1)S(1)}, bf16[32,1536]{1,0:T(8,128)(2,1)S(1)}) fusion(bf16[32,6144]{1,0:T(8,128)(2,1)} %param.5, s32[]{:T(128)S(6)} %select_n.15, s32[]{:T(128)S(6)} %select_n.13, s32[]{:T(128)S(6)} %select_n.12, s32[]{:T(128)S(6)} %select_n.14), kind=kLoop, calls=%fused_computation.6 | loop fusion | bytes 786448 | tf_op jit(solution)/shard_map/dynamic_slice | solution.py:229
  1.1 0.1 collective-permute-start
  1.2 1.4 %collective-permute-done = bf16[64,1536]{1,0:T(8,128)(2,1)S(1)} collective-permute-done((bf16[64,1536]{1,0:T(8,128)(2,1)S(1)}, bf16[64,1536]{1,0:T(8,128)(2,1)S(1)}, u32[]{:S(2)}, u32[]{:S(2)}) %collective-permute-start) | collective-permute-done | bytes 196640 | tf_op jit(solution)/shard_map/ppermute | solution.py:31
  2.6 0.1 collective-permute-start.1
  2.7 2.0 %collective-permute-start.4 = (bf16[64,1536]{1,0:T(8,128)(2,1)S(1)}, bf16[64,1536]{1,0:T(8,128)(2,1)S(1)}, u32[]{:S(2)}, u32[]{:S(2)}) collective-permute-start(bf16[64,1536]{1,0:T(8,128)(2,1)S(1)} %pad_maximum_fusion.2), channel_id=1, source_target_pairs={{0,8},{4,12},{8,0},{12,4},{1,9},{5,13},{9,1},{13,5},{2,10},{6,14},... | collective-permute-start | bytes 589832 | tf_op jit(solution)/shard_map/ppermute | solution.py:31
  4.7 2.6 %collective-permute-start.3 = (bf16[64,1536]{1,0:T(8,128)(2,1)S(1)}, bf16[64,1536]{1,0:T(8,128)(2,1)S(1)}, u32[]{:S(2)}, u32[]{:S(2)}) collective-permute-start(bf16[64,1536]{1,0:T(8,128)(2,1)S(1)} %pad_maximum_fusion.1.refs_0_), channel_id=1, source_target_pairs={{0,2},{1,3},{2,0},{3,1},{4,6},{5,7},{6,4},{7,5},{8,10},{9,11},{10,... | collective-permute-start | bytes 589832 | tf_op jit(solution)/shard_map/ppermute | solution.py:31
  7.3 2.9 %collective-permute-done.1.refs_1_ = bf16[64,1536]{1,0:T(8,128)(2,1)S(1)} collective-permute-done((bf16[64,1536]{1,0:T(8,128)(2,1)S(1)}, bf16[64,1536]{1,0:T(8,128)(2,1)S(1)}, u32[]{:S(2)}, u32[]{:S(2)}) %collective-permute-start.1) | collective-permute-done | bytes 196640 | tf_op jit(solution)/shard_map/ppermute | solution.py:31
  10.2 0.0 collective-permute-done.4.refs_0_
  10.2 3.7 %collective-permute-start.7 = (bf16[64,1536]{1,0:T(8,128)(2,1)S(1)}, bf16[64,1536]{1,0:T(8,128)(2,1)S(1)}, u32[]{:S(2)}, u32[]{:S(2)}) collective-permute-start(bf16[64,1536]{1,0:T(8,128)(2,1)S(1)} %collective-permute-done.4.refs_0_), channel_id=1, source_target_pairs={{0,2},{1,3},{2,0},{3,1},{4,6},{5,7},{6,4},{7,5},{8,10},{9,11},{10,... | collective-permute-start | bytes 589832 | tf_op jit(solution)/shard_map/ppermute | solution.py:31
  13.9 0.1 collective-permute-start.5
  14.1 0.0 copy-start
  14.1 0.7 copy-done
  14.7 8.4 %attend.4 = (bf16[64,1664]{1,0:T(8,128)(2,1)S(1)}, bf16[64,1664]{1,0:T(8,128)(2,1)S(1)}, bf16[2048,1536]{1,0:T(8,128)(2,1)S(1)}, bf16[2048,1536]{1,0:T(8,128)(2,1)S(1)}) custom-call(s32[16]{0:T(128)S(1)} %copy-done, bf16[64,1536]{1,0:T(8,128)(2,1)S(1)} %pad_maximum_fusion.1.refs_0_, bf16[64,1536]{1,0:T(8,128)(2,1)S(1)} %collective-permute-done.1.refs_1_, ...), custom_call_target="tpu_custom_call" | custom-call | flops 6442450944 | bytes 12582912 | tf_op jit(solution)/shard_map/attend/pallas_call | solution.py:115
  23.2 1.9 %collective-permute-start.2 = (bf16[64,1664]{1,0:T(8,128)(2,1)S(1)}, bf16[64,1664]{1,0:T(8,128)(2,1)S(1)}, u32[]{:S(2)}, u32[]{:S(2)}) collective-permute-start(bf16[64,1664]{1,0:T(8,128)(2,1)S(1)} %get-tuple-element.58), channel_id=1, source_target_pairs={{0,1},{1,0},{2,3},{3,2},{4,5},{5,4},{6,7},{7,6},{8,9},{9,8},{10,11... | collective-permute-start | bytes 638984 | tf_op jit(solution)/shard_map/ppermute | solution.py:31
  25.1 0.0 collective-permute-done.5.refs_1_
  25.1 0.0 collective-permute-done.7.refs_0_
  25.1 1.2 %collective-permute-start.8 = (bf16[64,1536]{1,0:T(8,128)(2,1)S(1)}, bf16[64,1536]{1,0:T(8,128)(2,1)S(1)}, u32[]{:S(2)}, u32[]{:S(2)}) collective-permute-start(bf16[64,1536]{1,0:T(8,128)(2,1)S(1)} %collective-permute-done.7.refs_0_), channel_id=1, source_target_pairs={{0,1},{1,0},{2,3},{3,2},{4,5},{5,4},{6,7},{7,6},{8,9},{9,8},{10,11... | collective-permute-start | bytes 589832 | tf_op jit(solution)/shard_map/ppermute | solution.py:31
  26.3 0.0 copy-start.1
  26.3 4.7 %attend.5 = (bf16[64,1664]{1,0:T(8,128)(2,1)S(1)}, bf16[64,1664]{1,0:T(8,128)(2,1)S(1)}) custom-call(s32[16]{0:T(128)S(1)} %copy-done, bf16[64,1536]{1,0:T(8,128)(2,1)S(1)} %collective-permute-done.4.refs_0_, bf16[64,1536]{1,0:T(8,128)(2,1)S(1)} %collective-permute-done.5.refs_1_, bf16[2048,1536]{1,0:T(8,128)(2,1)S(1)} %get-tuple-element.64.refs_2_, ...), custom_call_target="tpu_custom_call" | custom-call | flops 6442450944 | bytes 12582912 | tf_op jit(solution)/shard_map/attend/pallas_call | solution.py:115
  31.0 0.0 collective-permute-done.3.refs_0_
  31.0 0.9 collective-permute-start.6
  31.9 1.2 %collective-permute-start.9 = (bf16[64,1664]{1,0:T(8,128)(2,1)S(1)}, bf16[64,1664]{1,0:T(8,128)(2,1)S(1)}, u32[]{:S(2)}, u32[]{:S(2)}) collective-permute-start(bf16[64,1664]{1,0:T(8,128)(2,1)S(1)} %get-tuple-element.78), channel_id=1, source_target_pairs={{0,1},{1,0},{2,3},{3,2},{4,5},{5,4},{6,7},{7,6},{8,9},{9,8},{10,11... | collective-permute-start | bytes 638984 | tf_op jit(solution)/shard_map/ppermute | solution.py:31
  33.1 0.0 collective-permute-done.2.refs_0_
  33.1 2.0 %collective-permute-done.8.refs_1_ = bf16[64,1536]{1,0:T(8,128)(2,1)S(1)} collective-permute-done((bf16[64,1536]{1,0:T(8,128)(2,1)S(1)}, bf16[64,1536]{1,0:T(8,128)(2,1)S(1)}, u32[]{:S(2)}, u32[]{:S(2)}) %collective-permute-start.8) | collective-permute-done | bytes 196640 | tf_op jit(solution)/shard_map/ppermute | solution.py:31
  35.0 0.0 copy-done.1
  35.0 0.0 slice-start
  35.0 0.0 slice-start.1
  35.0 0.0 slice-start.2
  35.0 4.9 %attend.6 = (bf16[64,1664]{1,0:T(8,128)(2,1)S(1)}, bf16[64,1664]{1,0:T(8,128)(2,1)S(1)}) custom-call(s32[16]{0:T(128)S(1)} %copy-done.1, bf16[64,1536]{1,0:T(8,128)(2,1)S(1)} %collective-permute-done.7.refs_0_, bf16[64,1536]{1,0:T(8,128)(2,1)S(1)} %collective-permute-done.8.refs_1_, bf16[2048,1536]{1,0:T(8,128)(2,1)S(1)} %get-tuple-element.64.refs_2_, ...), custom_call_target="tpu_custom_call" | custom-call | flops 6442450944 | bytes 12582912 | tf_op jit(solution)/shard_map/attend/pallas_call | solution.py:115
  39.9 0.0 slice-start.3
  39.9 0.0 slice-start.4
  39.9 0.1 collective-permute-start.12
  40.0 4.8 %collective-permute-start.13 = (bf16[64,1664]{1,0:T(8,128)(2,1)S(1)}, bf16[64,1664]{1,0:T(8,128)(2,1)S(1)}, u32[]{:S(2)}, u32[]{:S(2)}) collective-permute-start(bf16[64,1664]{1,0:T(8,128)(2,1)S(1)} %get-tuple-element.87), channel_id=1, source_target_pairs={{0,2},{1,3},{2,0},{3,1},{4,6},{5,7},{6,4},{7,5},{8,10},{9,11},{10,... | collective-permute-start | bytes 638984 | tf_op jit(solution)/shard_map/ppermute | solution.py:31
  44.9 0.0 collective-permute-done.6.refs_1_
  44.9 0.0 collective-permute-done.9.refs_0_
  44.9 4.7 %attend.7 = (bf16[64,1664]{1,0:T(8,128)(2,1)S(1)}, bf16[64,1664]{1,0:T(8,128)(2,1)S(1)}) custom-call(s32[16]{0:T(128)S(1)} %copy-done.1, bf16[64,1536]{1,0:T(8,128)(2,1)S(1)} %collective-permute-done.3.refs_0_, bf16[64,1536]{1,0:T(8,128)(2,1)S(1)} %collective-permute-done.6.refs_1_, bf16[2048,1536]{1,0:T(8,128)(2,1)S(1)} %get-tuple-element.64.refs_2_, ...), custom_call_target="tpu_custom_call" | custom-call | flops 6442450944 | bytes 12582912 | tf_op jit(solution)/shard_map/attend/pallas_call | solution.py:115
  49.6 6.4 %collective-permute-done.12.refs_2_ = bf16[64,1664]{1,0:T(8,128)(2,1)S(1)} collective-permute-done((bf16[64,1664]{1,0:T(8,128)(2,1)S(1)}, bf16[64,1664]{1,0:T(8,128)(2,1)S(1)}, u32[]{:S(2)}, u32[]{:S(2)}) %collective-permute-start.12) | collective-permute-done | bytes 213024 | tf_op jit(solution)/shard_map/ppermute | solution.py:31
  56.0 0.9 collective-permute-done.13.refs_3_
  56.8 0.0 slice-done
  56.8 0.0 slice-done.1
  56.8 0.0 slice-done.2
  56.9 0.0 slice-done.3
  56.9 0.0 slice-done.4
  56.9 3.9 %project.2 = (bf16[32,6144]{1,0:T(8,128)(2,1)S(1)}, bf16[32,6144]{1,0:T(8,128)(2,1)S(1)}) custom-call(bf16[64,1664]{1,0:T(8,128)(2,1)S(1)} %collective-permute-done.9.refs_0_, bf16[64,1664]{1,0:T(8,128)(2,1)S(1)} %get-tuple-element.89.refs_1_, bf16[64,1664]{1,0:T(8,128)(2,1)S(1)} %collective-permute-done.12.refs_2_, ...), custom_call_target="tpu_custom_call" | custom-call | tf_op jit(solution)/shard_map/project/pallas_call | solution.py:164
  60.8 0.1 collective-permute-start.14
  60.9 0.5 collective-permute-start.15
  61.4 3.4 %collective-permute-start.11 = (bf16[64,1664]{1,0:T(8,128)(2,1)S(1)}, bf16[64,1664]{1,0:T(8,128)(2,1)S(1)}, u32[]{:S(2)}, u32[]{:S(2)}) collective-permute-start(bf16[64,1664]{1,0:T(8,128)(2,1)S(1)} %get-tuple-element.85), channel_id=1, source_target_pairs={{0,2},{1,3},{2,0},{3,1},{4,6},{5,7},{6,4},{7,5},{8,10},{9,11},{10,... | collective-permute-start | bytes 638984 | tf_op jit(solution)/shard_map/ppermute | solution.py:31
  64.8 0.9 collective-permute-start.10
  65.7 0.0 collective-permute-done.14
  65.7 0.0 collective-permute-done.15
  65.7 0.1 add_convert_fusion.2
  65.8 18.1 %collective-permute-done.10.refs_2_ = bf16[64,1664]{1,0:T(8,128)(2,1)S(1)} collective-permute-done((bf16[64,1664]{1,0:T(8,128)(2,1)S(1)}, bf16[64,1664]{1,0:T(8,128)(2,1)S(1)}, u32[]{:S(2)}, u32[]{:S(2)}) %collective-permute-start.10) | collective-permute-done | bytes 213024 | tf_op jit(solution)/shard_map/ppermute | solution.py:31
  83.9 0.0 collective-permute-done.11.refs_3_
  83.9 1.4 %collective-permute-start.18 = (bf16[32,6144]{1,0:T(8,128)(2,1)S(1)}, bf16[32,6144]{1,0:T(8,128)(2,1)S(1)}, u32[]{:S(2)}, u32[]{:S(2)}) collective-permute-start(bf16[32,6144]{1,0:T(8,128)(2,1)S(1)} %add_convert_fusion.2), channel_id=1, source_target_pairs={{0,8},{4,12},{8,0},{12,4},{1,9},{5,13},{9,1},{13,5},{2,10},{6,14},... | collective-permute-start | bytes 1179656 | tf_op jit(solution)/shard_map/ppermute | solution.py:31
  85.3 3.9 %project.3 = (bf16[32,6144]{1,0:T(8,128)(2,1)S(1)}, bf16[32,6144]{1,0:T(8,128)(2,1)S(1)}) custom-call(bf16[64,1664]{1,0:T(8,128)(2,1)S(1)} %collective-permute-done.2.refs_0_, bf16[64,1664]{1,0:T(8,128)(2,1)S(1)} %get-tuple-element.95.refs_1_, bf16[64,1664]{1,0:T(8,128)(2,1)S(1)} %collective-permute-done.10.refs_2_, ...), custom_call_target="tpu_custom_call" | custom-call | tf_op jit(solution)/shard_map/project/pallas_call | solution.py:164
  89.2 0.1 collective-permute-start.16
  89.3 0.5 collective-permute-start.17
  89.8 0.9 collective-permute-done.16
  90.7 0.3 collective-permute-done.17
  91.0 4.0 %collective-permute-done.18 = bf16[32,6144]{1,0:T(8,128)(2,1)S(1)} collective-permute-done((bf16[32,6144]{1,0:T(8,128)(2,1)S(1)}, bf16[32,6144]{1,0:T(8,128)(2,1)S(1)}, u32[]{:S(2)}, u32[]{:S(2)}) %collective-permute-start.18) | collective-permute-done | bytes 393248 | tf_op jit(solution)/shard_map/ppermute | solution.py:31
  95.0 0.9 add_convert_fusion
  (7 shorter events, 0.1 us)
Async XLA Ops:
  1.1 1.5 %collective-permute-start = (bf16[64,1536]{1,0:T(8,128)(2,1)S(1)}, bf16[64,1536]{1,0:T(8,128)(2,1)S(1)}, u32[]{:S(2)}, u32[]{:S(2)}) collective-permute-start(bf16[64,1536]{1,0:T(8,128)(2,1)S(1)} %pad_maximum_fusion), channel_id=1, source_target_pairs={{0,4},{4,0},{8,12},{12,8},{1,5},{5,1},{9,13},{13,9},{2,6},{6,2},{1... | collective-permute-start | bytes 589832 | tf_op jit(solution)/shard_map/ppermute | solution.py:31
  2.6 7.6 %collective-permute-start.1 = (bf16[64,1536]{1,0:T(8,128)(2,1)S(1)}, bf16[64,1536]{1,0:T(8,128)(2,1)S(1)}, u32[]{:S(2)}, u32[]{:S(2)}) collective-permute-start(bf16[64,1536]{1,0:T(8,128)(2,1)S(1)} %pad_maximum_fusion.1.refs_0_), channel_id=1, source_target_pairs={{0,1},{1,0},{2,3},{3,2},{4,5},{5,4},{6,7},{7,6},{8,9},{9,8},{10,11... | collective-permute-start | bytes 589832 | tf_op jit(solution)/shard_map/ppermute | solution.py:31
  2.7 7.5 %collective-permute-start.4 = (bf16[64,1536]{1,0:T(8,128)(2,1)S(1)}, bf16[64,1536]{1,0:T(8,128)(2,1)S(1)}, u32[]{:S(2)}, u32[]{:S(2)}) collective-permute-start(bf16[64,1536]{1,0:T(8,128)(2,1)S(1)} %pad_maximum_fusion.2), channel_id=1, source_target_pairs={{0,8},{4,12},{8,0},{12,4},{1,9},{5,13},{9,1},{13,5},{2,10},{6,14},... | collective-permute-start | bytes 589832 | tf_op jit(solution)/shard_map/ppermute | solution.py:31
  4.7 26.2 %collective-permute-start.3 = (bf16[64,1536]{1,0:T(8,128)(2,1)S(1)}, bf16[64,1536]{1,0:T(8,128)(2,1)S(1)}, u32[]{:S(2)}, u32[]{:S(2)}) collective-permute-start(bf16[64,1536]{1,0:T(8,128)(2,1)S(1)} %pad_maximum_fusion.1.refs_0_), channel_id=1, source_target_pairs={{0,2},{1,3},{2,0},{3,1},{4,6},{5,7},{6,4},{7,5},{8,10},{9,11},{10,... | collective-permute-start | bytes 589832 | tf_op jit(solution)/shard_map/ppermute | solution.py:31
  10.2 14.9 %collective-permute-start.7 = (bf16[64,1536]{1,0:T(8,128)(2,1)S(1)}, bf16[64,1536]{1,0:T(8,128)(2,1)S(1)}, u32[]{:S(2)}, u32[]{:S(2)}) collective-permute-start(bf16[64,1536]{1,0:T(8,128)(2,1)S(1)} %collective-permute-done.4.refs_0_), channel_id=1, source_target_pairs={{0,2},{1,3},{2,0},{3,1},{4,6},{5,7},{6,4},{7,5},{8,10},{9,11},{10,... | collective-permute-start | bytes 589832 | tf_op jit(solution)/shard_map/ppermute | solution.py:31
  13.9 11.2 %collective-permute-start.5 = (bf16[64,1536]{1,0:T(8,128)(2,1)S(1)}, bf16[64,1536]{1,0:T(8,128)(2,1)S(1)}, u32[]{:S(2)}, u32[]{:S(2)}) collective-permute-start(bf16[64,1536]{1,0:T(8,128)(2,1)S(1)} %collective-permute-done.4.refs_0_), channel_id=1, source_target_pairs={{0,1},{1,0},{2,3},{3,2},{4,5},{5,4},{6,7},{7,6},{8,9},{9,8},{10,11... | collective-permute-start | bytes 589832 | tf_op jit(solution)/shard_map/ppermute | solution.py:31
  14.1 0.7 copy-start
  23.2 9.9 %collective-permute-start.2 = (bf16[64,1664]{1,0:T(8,128)(2,1)S(1)}, bf16[64,1664]{1,0:T(8,128)(2,1)S(1)}, u32[]{:S(2)}, u32[]{:S(2)}) collective-permute-start(bf16[64,1664]{1,0:T(8,128)(2,1)S(1)} %get-tuple-element.58), channel_id=1, source_target_pairs={{0,1},{1,0},{2,3},{3,2},{4,5},{5,4},{6,7},{7,6},{8,9},{9,8},{10,11... | collective-permute-start | bytes 638984 | tf_op jit(solution)/shard_map/ppermute | solution.py:31
  25.1 9.9 %collective-permute-start.8 = (bf16[64,1536]{1,0:T(8,128)(2,1)S(1)}, bf16[64,1536]{1,0:T(8,128)(2,1)S(1)}, u32[]{:S(2)}, u32[]{:S(2)}) collective-permute-start(bf16[64,1536]{1,0:T(8,128)(2,1)S(1)} %collective-permute-done.7.refs_0_), channel_id=1, source_target_pairs={{0,1},{1,0},{2,3},{3,2},{4,5},{5,4},{6,7},{7,6},{8,9},{9,8},{10,11... | collective-permute-start | bytes 589832 | tf_op jit(solution)/shard_map/ppermute | solution.py:31
  26.3 8.8 %copy-start.1 = (s32[16]{0:T(128)S(1)}, s32[16]{0:T(128)}, u32[]{:S(2)}) copy-start(s32[16]{0:T(128)} %kept_ref.3) | copy-start | bytes 196
  31.0 13.9 %collective-permute-start.6 = (bf16[64,1536]{1,0:T(8,128)(2,1)S(1)}, bf16[64,1536]{1,0:T(8,128)(2,1)S(1)}, u32[]{:S(2)}, u32[]{:S(2)}) collective-permute-start(bf16[64,1536]{1,0:T(8,128)(2,1)S(1)} %collective-permute-done.3.refs_0_), channel_id=1, source_target_pairs={{0,1},{1,0},{2,3},{3,2},{4,5},{5,4},{6,7},{7,6},{8,9},{9,8},{10,11... | collective-permute-start | bytes 589832 | tf_op jit(solution)/shard_map/ppermute | solution.py:31
  31.9 13.0 %collective-permute-start.9 = (bf16[64,1664]{1,0:T(8,128)(2,1)S(1)}, bf16[64,1664]{1,0:T(8,128)(2,1)S(1)}, u32[]{:S(2)}, u32[]{:S(2)}) collective-permute-start(bf16[64,1664]{1,0:T(8,128)(2,1)S(1)} %get-tuple-element.78), channel_id=1, source_target_pairs={{0,1},{1,0},{2,3},{3,2},{4,5},{5,4},{6,7},{7,6},{8,9},{9,8},{10,11... | collective-permute-start | bytes 638984 | tf_op jit(solution)/shard_map/ppermute | solution.py:31
  35.0 21.8 %slice-start = ((s8[18874368]{0:T(1024)(128)(4,1)}), s8[4194304]{0:T(1024)(128)(4,1)S(1)}, s32[]{:S(2)}) async-start(s8[18874368]{0:T(1024)(128)(4,1)} %bitcast), calls=%async_computation | async-start | bytes 8388608
  35.0 21.8 %slice-start.1 = ((s8[18874368]{0:T(1024)(128)(4,1)}), s8[4194304]{0:T(1024)(128)(4,1)S(1)}, s32[]{:S(2)}) async-start(s8[18874368]{0:T(1024)(128)(4,1)} %bitcast), calls=%async_computation.1 | async-start | bytes 8388608
  35.0 21.8 %slice-start.2 = ((s8[18874368]{0:T(1024)(128)(4,1)}), s8[4194304]{0:T(1024)(128)(4,1)S(1)}, s32[]{:S(2)}) async-start(s8[18874368]{0:T(1024)(128)(4,1)} %bitcast), calls=%async_computation.2 | async-start | bytes 8388608
  39.9 16.9 %slice-start.3 = ((s8[18874368]{0:T(1024)(128)(4,1)}), s8[4194304]{0:T(1024)(128)(4,1)S(1)}, s32[]{:S(2)}) async-start(s8[18874368]{0:T(1024)(128)(4,1)} %bitcast), calls=%async_computation.3 | async-start | bytes 8388608
  39.9 16.9 %slice-start.4 = ((s8[18874368]{0:T(1024)(128)(4,1)}), s8[2097152]{0:T(1024)(128)(4,1)S(1)}, s32[]{:S(2)}) async-start(s8[18874368]{0:T(1024)(128)(4,1)} %bitcast), calls=%async_computation.4 | async-start | bytes 4194304
  39.9 16.0 %collective-permute-start.12 = (bf16[64,1664]{1,0:T(8,128)(2,1)S(1)}, bf16[64,1664]{1,0:T(8,128)(2,1)S(1)}, u32[]{:S(2)}, u32[]{:S(2)}) collective-permute-start(bf16[64,1664]{1,0:T(8,128)(2,1)S(1)} %get-tuple-element.86), channel_id=1, source_target_pairs={{0,3},{1,2},{2,1},{3,0},{4,7},{5,6},{6,5},{7,4},{8,11},{9,10},{10,... | collective-permute-start | bytes 638984 | tf_op jit(solution)/shard_map/ppermute | solution.py:31
  40.0 16.8 %collective-permute-start.13 = (bf16[64,1664]{1,0:T(8,128)(2,1)S(1)}, bf16[64,1664]{1,0:T(8,128)(2,1)S(1)}, u32[]{:S(2)}, u32[]{:S(2)}) collective-permute-start(bf16[64,1664]{1,0:T(8,128)(2,1)S(1)} %get-tuple-element.87), channel_id=1, source_target_pairs={{0,2},{1,3},{2,0},{3,1},{4,6},{5,7},{6,4},{7,5},{8,10},{9,11},{10,... | collective-permute-start | bytes 638984 | tf_op jit(solution)/shard_map/ppermute | solution.py:31
  60.8 4.9 %collective-permute-start.14 = (bf16[32,3072]{1,0:T(8,128)(2,1)S(1)}, bf16[32,3072]{1,0:T(8,128)(2,1)S(1)}, u32[]{:S(2)}, u32[]{:S(2)}) collective-permute-start(bf16[32,3072]{1,0:T(8,128)(2,1)S(1)} %get-tuple-element.103), channel_id=1, source_target_pairs={{0,4},{4,0},{8,12},{12,8},{1,5},{5,1},{9,13},{13,9},{2,6},{6,2},{1... | collective-permute-start | bytes 589832 | tf_op jit(solution)/shard_map/ppermute | solution.py:31
  60.9 4.8 %collective-permute-start.15 = (bf16[32,3072]{1,0:T(8,128)(2,1)S(1)}, bf16[32,3072]{1,0:T(8,128)(2,1)S(1)}, u32[]{:S(2)}, u32[]{:S(2)}) collective-permute-start(bf16[32,3072]{1,0:T(8,128)(2,1)S(1)} %get-tuple-element.104), channel_id=1, source_target_pairs={{0,4},{4,0},{8,12},{12,8},{1,5},{5,1},{9,13},{13,9},{2,6},{6,2},{1... | collective-permute-start | bytes 589832 | tf_op jit(solution)/shard_map/ppermute | solution.py:31
  61.4 22.6 %collective-permute-start.11 = (bf16[64,1664]{1,0:T(8,128)(2,1)S(1)}, bf16[64,1664]{1,0:T(8,128)(2,1)S(1)}, u32[]{:S(2)}, u32[]{:S(2)}) collective-permute-start(bf16[64,1664]{1,0:T(8,128)(2,1)S(1)} %get-tuple-element.85), channel_id=1, source_target_pairs={{0,2},{1,3},{2,0},{3,1},{4,6},{5,7},{6,4},{7,5},{8,10},{9,11},{10,... | collective-permute-start | bytes 638984 | tf_op jit(solution)/shard_map/ppermute | solution.py:31
  64.8 19.2 %collective-permute-start.10 = (bf16[64,1664]{1,0:T(8,128)(2,1)S(1)}, bf16[64,1664]{1,0:T(8,128)(2,1)S(1)}, u32[]{:S(2)}, u32[]{:S(2)}) collective-permute-start(bf16[64,1664]{1,0:T(8,128)(2,1)S(1)} %get-tuple-element.84), channel_id=1, source_target_pairs={{0,3},{1,2},{2,1},{3,0},{4,7},{5,6},{6,5},{7,4},{8,11},{9,10},{10,... | collective-permute-start | bytes 638984 | tf_op jit(solution)/shard_map/ppermute | solution.py:31
  83.9 11.0 %collective-permute-start.18 = (bf16[32,6144]{1,0:T(8,128)(2,1)S(1)}, bf16[32,6144]{1,0:T(8,128)(2,1)S(1)}, u32[]{:S(2)}, u32[]{:S(2)}) collective-permute-start(bf16[32,6144]{1,0:T(8,128)(2,1)S(1)} %add_convert_fusion.2), channel_id=1, source_target_pairs={{0,8},{4,12},{8,0},{12,4},{1,9},{5,13},{9,1},{13,5},{2,10},{6,14},... | collective-permute-start | bytes 1179656 | tf_op jit(solution)/shard_map/ppermute | solution.py:31
  89.2 1.5 %collective-permute-start.16 = (bf16[32,3072]{1,0:T(8,128)(2,1)S(1)}, bf16[32,3072]{1,0:T(8,128)(2,1)S(1)}, u32[]{:S(2)}, u32[]{:S(2)}) collective-permute-start(bf16[32,3072]{1,0:T(8,128)(2,1)S(1)} %get-tuple-element.101), channel_id=1, source_target_pairs={{0,4},{4,0},{8,12},{12,8},{1,5},{5,1},{9,13},{13,9},{2,6},{6,2},{1... | collective-permute-start | bytes 589832 | tf_op jit(solution)/shard_map/ppermute | solution.py:31
  89.3 1.7 %collective-permute-start.17 = (bf16[32,3072]{1,0:T(8,128)(2,1)S(1)}, bf16[32,3072]{1,0:T(8,128)(2,1)S(1)}, u32[]{:S(2)}, u32[]{:S(2)}) collective-permute-start(bf16[32,3072]{1,0:T(8,128)(2,1)S(1)} %get-tuple-element.102), channel_id=1, source_target_pairs={{0,4},{4,0},{8,12},{12,8},{1,5},{5,1},{9,13},{13,9},{2,6},{6,2},{1... | collective-permute-start | bytes 589832 | tf_op jit(solution)/shard_map/ppermute | solution.py:31

commit v3 on v2

--- a/solution.py
+++ b/solution.py
@@ -23,8 +23,15 @@
 WHOLE = pl.BlockSpec(memory_space=pltpu.VMEM)
 
 
+SMALL = pl.CostEstimate(flops=1, transcendentals=1, bytes_accessed=1)
+
+
 def near(x):
     return pltpu.with_memory_space_constraint(x, pltpu.VMEM)
+
+
+def after(x, first):
+    return lax.optimization_barrier((x, first))[0]
 
 
 def swap(x, axis, size, bit):
@@ -143,6 +150,30 @@
     )
 
 
+def merge_body(*refs, heads):
+    parts = [ref[...] for ref in refs[:-1]]
+    weights, total = shares(parts, heads)
+    for h in range(heads):
+        refs[-1][:, h * HD : h * HD + HD] = mix(parts, weights, h).astype(jnp.bfloat16)
+    lane = lax.broadcasted_iota(jnp.int32, total.shape, 1)
+    spread = jnp.where(
+        lane < STEP, total, jnp.where(lane < 2 * STEP, pltpu.roll(total, STEP, 1), pltpu.roll(total, 2 * STEP, 1))
+    )
+    refs[-1][:, heads * HD :] = split_stats(spread)
+
+
+def merge(parts, heads):
+    return pl.pallas_call(
+        functools.partial(merge_body, heads=heads),
+        in_specs=[WHOLE] * len(parts),
+        out_specs=WHOLE,
+        out_shape=jax.ShapeDtypeStruct(parts[0].shape, parts[0].dtype),
+        compiler_params=pltpu.CompilerParams(vmem_limit_bytes=VMEM),
+        cost_estimate=SMALL,
+        name="merge",
+    )(*map(near, parts))
+
+
 def project_body(*refs, count, heads, group):
     parts = [ref[...] for ref in refs[:count]]
     w_ref, *out_refs = refs[count:]
@@ -167,7 +198,7 @@
         out_specs=[WHOLE] * 2,
         out_shape=[half, half],
         compiler_params=pltpu.CompilerParams(vmem_limit_bytes=VMEM),
-        cost_estimate=pl.CostEstimate(flops=0, transcendentals=0, bytes_accessed=0),
+        cost_estimate=SMALL,
         name="project",
     )(*map(near, parts), weight)
 
@@ -231,49 +262,61 @@
     while bit < top:
         blocks = exchange(blocks, n_head, bit)
         bit *= 2
+    far_off = n_ctx // 2
     own, other = {0: blocks[0]}, {0: swap(blocks[top], "head", n_head, top)}
     own[1] = swap(own[0], "ctx", n_ctx, 1)
-    other = near_side(far(other[0], n_ctx), n_ctx)
-
-    def run(side, pieces, need):
+    others = [d for d in range(n_ctx) if d not in (0, 1, far_off)]
+    sides = [own, other]
+    parts = [{}, {}]
+
+    def run(pieces, need):
         nonlocal kept_rows, keys, values
-        loads = not need
-        q = [side[d] for d in pieces]
+        loads = not parts[0]
+        q = [sides[side][d] for side, d in pieces]
         q, kept_rows, _ = lax.optimization_barrier((q, kept_rows, need))
         out = attend(kept_rows, q, keys, values, loads)
         if loads:
             *out, keys, values = out
             keys, values = near(keys), near(values)
         kept_rows, out = lax.optimization_barrier((kept_rows, out))
-        return dict(zip(pieces, out))
-
-    def send(pieces):
-        return [x if d == 0 else swap(x, "ctx", n_ctx, d) for d, x in sorted(pieces.items(), reverse=True)]
-
-    low, high = (0, 1), tuple(range(2, n_ctx))
-    made = run(own, low, [])
-    mine = send(made)
-    other_far, gate = lax.optimization_barrier((other[n_ctx // 2], made[0]))
-    other[n_ctx // 2] = other_far
-    other = rest(other, n_ctx)
-    own[0] = lax.optimization_barrier((own[0], gate))[0]
-    own[n_ctx // 2] = swap(own[0], "ctx", n_ctx, n_ctx // 2)
-    made = run(other, low, [made[0]])
-    theirs = send(made)
-    own[n_ctx // 2] = lax.optimization_barrier((own[n_ctx // 2], made[0]))[0]
-    own = rest(own, n_ctx)
-    made = run(other, high, mine)
-    theirs += send(made)
-    made = run(own, high, theirs[:2])
-    mine += send(made)
-
-    theirs, _ = lax.optimization_barrier((theirs, made[2]))
-    done = project(theirs, out_weight, group)
-    done = fold(*done, n_head, top, group)
+        for (side, d), x in zip(pieces, out):
+            parts[side][d] = x
+
+    def send(side, d):
+        parts[side][d] = swap(parts[side][d], "ctx", n_ctx, d)
+
+    sides[1] = other = near_side(far(other[0], n_ctx), n_ctx)
+    own[far_off] = swap(own[0], "ctx", n_ctx, far_off)
+    last = far_off ^ 1
+
+    def passed(side):
+        for d in others:
+            if d != last:
+                send(side, d)
+        return [parts[side].pop(far_off), swap(parts[side].pop(last), "ctx", n_ctx, 1)]
+
+    run([(0, 0), (0, 1)], [])
+    sides[1] = rest(other, n_ctx)
+    run([(1, 0), (1, 1)], [])
+    own[far_off] = after(own[far_off], parts[1][0])
+    sides[0] = rest(own, n_ctx)
+    run([(1, d) for d in [far_off] + others], [])
+    for side in (0, 1):
+        parts[side][1] = after(parts[side][1], parts[1][far_off])
+        send(side, 1)
+    relay = passed(1)
+    run([(0, d) for d in [far_off] + others], [])
+    theirs_through = merge(relay, local_heads)
+    parts[1][far_off] = swap(theirs_through, "ctx", n_ctx, far_off)
+    through = merge(passed(0), local_heads)
+    theirs, mine = list(parts[1].values()), list(parts[0].values())
+
+    theirs, through = lax.optimization_barrier((theirs, through))
+    mine.append(swap(through, "ctx", n_ctx, far_off))
+    done = fold(*project(theirs, out_weight, group), n_head, top, group)
     mine, done = lax.optimization_barrier((mine, done))
     other = swap(done, "head", n_head, top)
-    done = project(mine, out_weight, group)
-    done = fold(*done, n_head, top, group)
+    done = fold(*project(mine, out_weight, group), n_head, top, group)
     return (done.astype(jnp.float32) + other.astype(jnp.float32)).astype(jnp.bfloat16)
 
 

time: 96 us -> 89.1 us (0.928)
  the two profiles are of different devices: /device:TPU:8 before, /device:TPU:0 now
where the time goes in v3:
time: 89.1 us; the launch traced here: 88.9 us
  waiting for transfers between devices  31.5 us (35%)
  Pallas kernels  31 us (35%)
  starting transfers between devices  23.4 us (26%)
  local copies, waits for them, and re-layouts  1.82 us (2%)
  other arithmetic  1.03 us (1%)
    ppermute x19, waiting for transfers between devices, swap(): return lax.ppermute(x, axis, [(i, i ^ bit) for i in range(size)])  31.5 us
    ppermute x19, starting transfers between devices, swap(): return lax.ppermute(x, axis, [(i, i ^ bit) for i in range(size)])  23.4 us
    pallas_call x4, Pallas kernels, attend(): pl.pallas_call(functools.partial(attend_body, pieces=pieces, heads=heads,...  22.7 us
    pallas_call x2, Pallas kernels, project(): pl.pallas_call(functools.partial(project_body, count=len(parts), heads=we...  7.47 us
  transfers between devices with their start and end apart: 19, of which 10 were waited for; matrix products, arithmetic and copies ran while one was open for 0% of the time, Pallas kernels for 31%

profile of v3, /device:TPU:0, one launch (start us, length us, event | category | flops | bytes accessed | tf_op | source)
XLA Modules:
  0.0 88.9 jit_solution(5279746084324308569)
XLA Ops:
  0.0 1.1 %constant_dynamic-slice_fusion = (bf16[32,1536]{1,0:T(8,128)(2,1)S(1)}, bf16[32,1536]{1,0:T(8,128)(2,1)S(1)}, bf16[32,1536]{1,0:T(8,128)(2,1)S(1)}, bf16[32,1536]{1,0:T(8,128)(2,1)S(1)}) fusion(bf16[32,6144]{1,0:T(8,128)(2,1)} %param.5, s32[]{:T(128)S(6)} %select_n.15, s32[]{:T(128)S(6)} %select_n.13, s32[]{:T(128)S(6)} %select_n.12, s32[]{:T(128)S(6)} %select_n.14), kind=kLoop, calls=%fused_computation.6 | loop fusion | bytes 786448 | tf_op jit(solution)/shard_map/dynamic_slice | solution.py:260
  1.1 0.5 collective-permute-start
  1.6 1.1 %collective-permute-done = bf16[64,1536]{1,0:T(8,128)(2,1)S(1)} collective-permute-done((bf16[64,1536]{1,0:T(8,128)(2,1)S(1)}, bf16[64,1536]{1,0:T(8,128)(2,1)S(1)}, u32[]{:S(2)}, u32[]{:S(2)}) %collective-permute-start) | collective-permute-done | bytes 196640 | tf_op jit(solution)/shard_map/ppermute | solution.py:38
  2.7 3.0 %collective-permute-start.1 = (bf16[64,1536]{1,0:T(8,128)(2,1)S(1)}, bf16[64,1536]{1,0:T(8,128)(2,1)S(1)}, u32[]{:S(2)}, u32[]{:S(2)}) collective-permute-start(bf16[64,1536]{1,0:T(8,128)(2,1)S(1)} %pad_maximum_fusion.1.refs_0_), channel_id=1, source_target_pairs={{0,1},{1,0},{2,3},{3,2},{4,5},{5,4},{6,7},{7,6},{8,9},{9,8},{10,11... | collective-permute-start | bytes 589832 | tf_op jit(solution)/shard_map/ppermute | solution.py:38
  5.7 1.6 %collective-permute-start.2 = (bf16[64,1536]{1,0:T(8,128)(2,1)S(1)}, bf16[64,1536]{1,0:T(8,128)(2,1)S(1)}, u32[]{:S(2)}, u32[]{:S(2)}) collective-permute-start(bf16[64,1536]{1,0:T(8,128)(2,1)S(1)} %pad_maximum_fusion.2), channel_id=1, source_target_pairs={{0,8},{4,12},{8,0},{12,4},{1,9},{5,13},{9,1},{13,5},{2,10},{6,14},... | collective-permute-start | bytes 589832 | tf_op jit(solution)/shard_map/ppermute | solution.py:38
  7.3 2.6 %collective-permute-start.10 = (bf16[64,1536]{1,0:T(8,128)(2,1)S(1)}, bf16[64,1536]{1,0:T(8,128)(2,1)S(1)}, u32[]{:S(2)}, u32[]{:S(2)}) collective-permute-start(bf16[64,1536]{1,0:T(8,128)(2,1)S(1)} %pad_maximum_fusion.1.refs_0_), channel_id=1, source_target_pairs={{0,2},{1,3},{2,0},{3,1},{4,6},{5,7},{6,4},{7,5},{8,10},{9,11},{10,... | collective-permute-start | bytes 589832 | tf_op jit(solution)/shard_map/ppermute | solution.py:38
  9.9 3.5 %collective-permute-done.1.refs_1_ = bf16[64,1536]{1,0:T(8,128)(2,1)S(1)} collective-permute-done((bf16[64,1536]{1,0:T(8,128)(2,1)S(1)}, bf16[64,1536]{1,0:T(8,128)(2,1)S(1)}, u32[]{:S(2)}, u32[]{:S(2)}) %collective-permute-start.1) | collective-permute-done | bytes 196640 | tf_op jit(solution)/shard_map/ppermute | solution.py:38
  13.4 0.0 collective-permute-done.2.refs_0_
  13.4 1.7 %collective-permute-start.3 = (bf16[64,1536]{1,0:T(8,128)(2,1)S(1)}, bf16[64,1536]{1,0:T(8,128)(2,1)S(1)}, u32[]{:S(2)}, u32[]{:S(2)}) collective-permute-start(bf16[64,1536]{1,0:T(8,128)(2,1)S(1)} %collective-permute-done.2.refs_0_), channel_id=1, source_target_pairs={{0,2},{1,3},{2,0},{3,1},{4,6},{5,7},{6,4},{7,5},{8,10},{9,11},{10,... | collective-permute-start | bytes 589832 | tf_op jit(solution)/shard_map/ppermute | solution.py:38
  15.1 1.9 %collective-permute-start.5 = (bf16[64,1536]{1,0:T(8,128)(2,1)S(1)}, bf16[64,1536]{1,0:T(8,128)(2,1)S(1)}, u32[]{:S(2)}, u32[]{:S(2)}) collective-permute-start(bf16[64,1536]{1,0:T(8,128)(2,1)S(1)} %collective-permute-done.2.refs_0_), channel_id=1, source_target_pairs={{0,1},{1,0},{2,3},{3,2},{4,5},{5,4},{6,7},{7,6},{8,9},{9,8},{10,11... | collective-permute-start | bytes 589832 | tf_op jit(solution)/shard_map/ppermute | solution.py:38
  16.9 0.0 copy-start
  16.9 0.7 copy-done
  17.6 8.4 %attend.4 = (bf16[64,1664]{1,0:T(8,128)(2,1)S(1)}, bf16[64,1664]{1,0:T(8,128)(2,1)S(1)}, bf16[2048,1536]{1,0:T(8,128)(2,1)S(1)}, bf16[2048,1536]{1,0:T(8,128)(2,1)S(1)}) custom-call(s32[16]{0:T(128)S(1)} %copy-done, bf16[64,1536]{1,0:T(8,128)(2,1)S(1)} %pad_maximum_fusion.1.refs_0_, bf16[64,1536]{1,0:T(8,128)(2,1)S(1)} %collective-permute-done.1.refs_1_, ...), custom_call_target="tpu_custom_call" | custom-call | flops 6442450944 | bytes 12582912 | tf_op jit(solution)/shard_map/attend/pallas_call | solution.py:122
  26.0 0.0 collective-permute-done.5.refs_1_
  26.0 1.2 %collective-permute-done.3.refs_0_ = bf16[64,1536]{1,0:T(8,128)(2,1)S(1)} collective-permute-done((bf16[64,1536]{1,0:T(8,128)(2,1)S(1)}, bf16[64,1536]{1,0:T(8,128)(2,1)S(1)}, u32[]{:S(2)}, u32[]{:S(2)}) %collective-permute-start.3) | collective-permute-done | bytes 196640 | tf_op jit(solution)/shard_map/ppermute | solution.py:38
  27.3 0.0 collective-permute-start.4
  27.3 0.0 copy-start.1
  27.3 4.7 %attend.5 = (bf16[64,1664]{1,0:T(8,128)(2,1)S(1)}, bf16[64,1664]{1,0:T(8,128)(2,1)S(1)}) custom-call(s32[16]{0:T(128)S(1)} %copy-done, bf16[64,1536]{1,0:T(8,128)(2,1)S(1)} %collective-permute-done.2.refs_0_, bf16[64,1536]{1,0:T(8,128)(2,1)S(1)} %collective-permute-done.5.refs_1_, bf16[2048,1536]{1,0:T(8,128)(2,1)S(1)} %get-tuple-element.64.refs_2_, ...), custom_call_target="tpu_custom_call" | custom-call | flops 6442450944 | bytes 12582912 | tf_op jit(solution)/shard_map/attend/pallas_call | solution.py:122
  32.0 0.0 collective-permute-done.10.refs_0_
  32.0 2.1 %collective-permute-start.11 = (bf16[64,1536]{1,0:T(8,128)(2,1)S(1)}, bf16[64,1536]{1,0:T(8,128)(2,1)S(1)}, u32[]{:S(2)}, u32[]{:S(2)}) collective-permute-start(bf16[64,1536]{1,0:T(8,128)(2,1)S(1)} %collective-permute-done.10.refs_0_), channel_id=1, source_target_pairs={{0,1},{1,0},{2,3},{3,2},{4,5},{5,4},{6,7},{7,6},{8,9},{9,8},{10,11... | collective-permute-start | bytes 589832 | tf_op jit(solution)/shard_map/ppermute | solution.py:38
  34.1 0.0 collective-permute-done.4.refs_1_
  34.1 0.0 copy-done.1
  34.1 0.0 slice-start
  34.1 0.0 slice-start.1
  34.1 0.0 slice-start.2
  34.1 4.9 %attend.6 = (bf16[64,1664]{1,0:T(8,128)(2,1)S(1)}, bf16[64,1664]{1,0:T(8,128)(2,1)S(1)}) custom-call(s32[16]{0:T(128)S(1)} %copy-done.1, bf16[64,1536]{1,0:T(8,128)(2,1)S(1)} %collective-permute-done.3.refs_0_, bf16[64,1536]{1,0:T(8,128)(2,1)S(1)} %collective-permute-done.4.refs_1_, bf16[2048,1536]{1,0:T(8,128)(2,1)S(1)} %get-tuple-element.64.refs_2_, ...), custom_call_target="tpu_custom_call" | custom-call | flops 6442450944 | bytes 12582912 | tf_op jit(solution)/shard_map/attend/pallas_call | solution.py:122
  39.0 0.0 slice-start.3
  39.0 0.0 slice-start.4
  39.0 0.1 collective-permute-start.8
  39.1 0.0 collective-permute-done.11.refs_1_
  39.1 4.7 %attend.7 = (bf16[64,1664]{1,0:T(8,128)(2,1)S(1)}, bf16[64,1664]{1,0:T(8,128)(2,1)S(1)}) custom-call(s32[16]{0:T(128)S(1)} %copy-done.1, bf16[64,1536]{1,0:T(8,128)(2,1)S(1)} %collective-permute-done.10.refs_0_, bf16[64,1536]{1,0:T(8,128)(2,1)S(1)} %collective-permute-done.11.refs_1_, bf16[2048,1536]{1,0:T(8,128)(2,1)S(1)} %get-tuple-element.64.refs_2_, ...), custom_call_target="tpu_custom_call" | custom-call | flops 6442450944 | bytes 12582912 | tf_op jit(solution)/shard_map/attend/pallas_call | solution.py:122
  43.8 2.0 %collective-permute-start.12 = (bf16[64,1664]{1,0:T(8,128)(2,1)S(1)}, bf16[64,1664]{1,0:T(8,128)(2,1)S(1)}, u32[]{:S(2)}, u32[]{:S(2)}) collective-permute-start(bf16[64,1664]{1,0:T(8,128)(2,1)S(1)} %get-tuple-element.88), channel_id=1, source_target_pairs={{0,1},{1,0},{2,3},{3,2},{4,5},{5,4},{6,7},{7,6},{8,9},{9,8},{10,11... | collective-permute-start | bytes 638984 | tf_op jit(solution)/shard_map/ppermute | solution.py:38
  45.8 0.1 collective-permute-start.7
  45.9 0.0 collective-permute-done.8.refs_1_
  45.9 0.4 merge.2
  46.3 3.0 %collective-permute-start.9 = (bf16[64,1664]{1,0:T(8,128)(2,1)S(1)}, bf16[64,1664]{1,0:T(8,128)(2,1)S(1)}, u32[]{:S(2)}, u32[]{:S(2)}) collective-permute-start(bf16[64,1664]{1,0:T(8,128)(2,1)S(1)} %merge.2), channel_id=1, source_target_pairs={{0,2},{1,3},{2,0},{3,1},{4,6},{5,7},{6,4},{7,5},{8,10},{9,11},{10,... | collective-permute-start | bytes 638984 | tf_op jit(solution)/shard_map/ppermute | solution.py:38
  49.4 7.0 %collective-permute-done.12.refs_1_ = bf16[64,1664]{1,0:T(8,128)(2,1)S(1)} collective-permute-done((bf16[64,1664]{1,0:T(8,128)(2,1)S(1)}, bf16[64,1664]{1,0:T(8,128)(2,1)S(1)}, u32[]{:S(2)}, u32[]{:S(2)}) %collective-permute-start.12) | collective-permute-done | bytes 213024 | tf_op jit(solution)/shard_map/ppermute | solution.py:38
  56.3 0.4 merge.3
  56.7 1.9 %collective-permute-done.7.refs_1_ = bf16[64,1664]{1,0:T(8,128)(2,1)S(1)} collective-permute-done((bf16[64,1664]{1,0:T(8,128)(2,1)S(1)}, bf16[64,1664]{1,0:T(8,128)(2,1)S(1)}, u32[]{:S(2)}, u32[]{:S(2)}) %collective-permute-start.7) | collective-permute-done | bytes 213024 | tf_op jit(solution)/shard_map/ppermute | solution.py:38
  58.6 0.0 collective-permute-done.9.refs_2_
  58.6 0.0 slice-done
  58.6 0.0 slice-done.1
  58.6 0.0 slice-done.2
  58.6 0.0 slice-done.3
  58.6 0.0 slice-done.4
  58.6 3.7 %project.2 = (bf16[32,6144]{1,0:T(8,128)(2,1)S(1)}, bf16[32,6144]{1,0:T(8,128)(2,1)S(1)}) custom-call(bf16[64,1664]{1,0:T(8,128)(2,1)S(1)} %get-tuple-element.90.refs_0_, bf16[64,1664]{1,0:T(8,128)(2,1)S(1)} %collective-permute-done.7.refs_1_, bf16[64,1664]{1,0:T(8,128)(2,1)S(1)} %collective-permute-done.9.refs_2_, bf16[1536,6144]{1,0:T(8,128)(2,1)S(1)} %bitcast.1), custom_call_target="tpu_custom_call" | custom-call | flops 1 | bytes 1 | tf_op jit(solution)/shard_map/project/pallas_call | solution.py:195
  62.4 0.1 collective-permute-start.15
  62.5 0.5 collective-permute-start.14
  63.0 2.6 %collective-permute-start.6 = (bf16[64,1664]{1,0:T(8,128)(2,1)S(1)}, bf16[64,1664]{1,0:T(8,128)(2,1)S(1)}, u32[]{:S(2)}, u32[]{:S(2)}) collective-permute-start(bf16[64,1664]{1,0:T(8,128)(2,1)S(1)} %get-tuple-element.75), channel_id=1, source_target_pairs={{0,1},{1,0},{2,3},{3,2},{4,5},{5,4},{6,7},{7,6},{8,9},{9,8},{10,11... | collective-permute-start | bytes 638984 | tf_op jit(solution)/shard_map/ppermute | solution.py:38
  65.6 0.5 collective-permute-start.13
  66.0 0.0 collective-permute-done.15
  66.0 0.0 collective-permute-done.14
  66.0 0.1 add_convert_fusion.2
  66.1 8.1 %collective-permute-done.6.refs_1_ = bf16[64,1664]{1,0:T(8,128)(2,1)S(1)} collective-permute-done((bf16[64,1664]{1,0:T(8,128)(2,1)S(1)}, bf16[64,1664]{1,0:T(8,128)(2,1)S(1)}, u32[]{:S(2)}, u32[]{:S(2)}) %collective-permute-start.6) | collective-permute-done | bytes 213024 | tf_op jit(solution)/shard_map/ppermute | solution.py:38
  74.3 3.8 %collective-permute-done.13.refs_2_ = bf16[64,1664]{1,0:T(8,128)(2,1)S(1)} collective-permute-done((bf16[64,1664]{1,0:T(8,128)(2,1)S(1)}, bf16[64,1664]{1,0:T(8,128)(2,1)S(1)}, u32[]{:S(2)}, u32[]{:S(2)}) %collective-permute-start.13) | collective-permute-done | bytes 213024 | tf_op jit(solution)/shard_map/ppermute | solution.py:38
  78.0 0.6 collective-permute-start.18
  78.7 3.7 %project.3 = (bf16[32,6144]{1,0:T(8,128)(2,1)S(1)}, bf16[32,6144]{1,0:T(8,128)(2,1)S(1)}) custom-call(bf16[64,1664]{1,0:T(8,128)(2,1)S(1)} %get-tuple-element.95.refs_0_, bf16[64,1664]{1,0:T(8,128)(2,1)S(1)} %collective-permute-done.6.refs_1_, bf16[64,1664]{1,0:T(8,128)(2,1)S(1)} %collective-permute-done.13.refs_2_, bf16[1536,6144]{1,0:T(8,128)(2,1)S(1)} %bitcast.1), custom_call_target="tpu_custom_call" | custom-call | flops 1 | bytes 1 | tf_op jit(solution)/shard_map/project/pallas_call | solution.py:195
  82.5 0.1 collective-permute-start.17
  82.5 0.5 collective-permute-start.16
  83.0 0.9 %collective-permute-done.17 = bf16[32,3072]{1,0:T(8,128)(2,1)S(1)} collective-permute-done((bf16[32,3072]{1,0:T(8,128)(2,1)S(1)}, bf16[32,3072]{1,0:T(8,128)(2,1)S(1)}, u32[]{:S(2)}, u32[]{:S(2)}) %collective-permute-start.17) | collective-permute-done | bytes 196640 | tf_op jit(solution)/shard_map/ppermute | solution.py:38
  84.0 0.3 collective-permute-done.16
  84.2 3.8 %collective-permute-done.18 = bf16[32,6144]{1,0:T(8,128)(2,1)S(1)} collective-permute-done((bf16[32,6144]{1,0:T(8,128)(2,1)S(1)}, bf16[32,6144]{1,0:T(8,128)(2,1)S(1)}, u32[]{:S(2)}, u32[]{:S(2)}) %collective-permute-start.18) | collective-permute-done | bytes 393248 | tf_op jit(solution)/shard_map/ppermute | solution.py:38
  88.0 0.9 %add_convert_fusion = bf16[32,6144]{1,0:T(8,128)(2,1)} fusion(bf16[32,6144]{1,0:T(8,128)(2,1)S(1)} %collective-permute-done.18, bf16[32,6144]{1,0:T(8,128)(2,1)S(1)} %get-tuple-element.98, bf16[32,3072]{1,0:T(8,128)(2,1)S(1)} %collective-permute-done.17, bf16[32,3072]{1,0:T(8,128)(2,1)S(1)} %collective-permute-done.16), kind=kLoop, calls=%fused_computation | loop fusion | flops 2162688 | bytes 1572864 | tf_op jit(solution)/shard_map/convert_element_type | solution.py:320
  (7 shorter events, 0.1 us)
Async XLA Ops:
  1.1 1.6 %collective-permute-start = (bf16[64,1536]{1,0:T(8,128)(2,1)S(1)}, bf16[64,1536]{1,0:T(8,128)(2,1)S(1)}, u32[]{:S(2)}, u32[]{:S(2)}) collective-permute-start(bf16[64,1536]{1,0:T(8,128)(2,1)S(1)} %pad_maximum_fusion), channel_id=1, source_target_pairs={{0,4},{4,0},{8,12},{12,8},{1,5},{5,1},{9,13},{13,9},{2,6},{6,2},{1... | collective-permute-start | bytes 589832 | tf_op jit(solution)/shard_map/ppermute | solution.py:38
  2.7 10.6 %collective-permute-start.1 = (bf16[64,1536]{1,0:T(8,128)(2,1)S(1)}, bf16[64,1536]{1,0:T(8,128)(2,1)S(1)}, u32[]{:S(2)}, u32[]{:S(2)}) collective-permute-start(bf16[64,1536]{1,0:T(8,128)(2,1)S(1)} %pad_maximum_fusion.1.refs_0_), channel_id=1, source_target_pairs={{0,1},{1,0},{2,3},{3,2},{4,5},{5,4},{6,7},{7,6},{8,9},{9,8},{10,11... | collective-permute-start | bytes 589832 | tf_op jit(solution)/shard_map/ppermute | solution.py:38
  5.7 7.6 %collective-permute-start.2 = (bf16[64,1536]{1,0:T(8,128)(2,1)S(1)}, bf16[64,1536]{1,0:T(8,128)(2,1)S(1)}, u32[]{:S(2)}, u32[]{:S(2)}) collective-permute-start(bf16[64,1536]{1,0:T(8,128)(2,1)S(1)} %pad_maximum_fusion.2), channel_id=1, source_target_pairs={{0,8},{4,12},{8,0},{12,4},{1,9},{5,13},{9,1},{13,5},{2,10},{6,14},... | collective-permute-start | bytes 589832 | tf_op jit(solution)/shard_map/ppermute | solution.py:38
  7.3 24.7 %collective-permute-start.10 = (bf16[64,1536]{1,0:T(8,128)(2,1)S(1)}, bf16[64,1536]{1,0:T(8,128)(2,1)S(1)}, u32[]{:S(2)}, u32[]{:S(2)}) collective-permute-start(bf16[64,1536]{1,0:T(8,128)(2,1)S(1)} %pad_maximum_fusion.1.refs_0_), channel_id=1, source_target_pairs={{0,2},{1,3},{2,0},{3,1},{4,6},{5,7},{6,4},{7,5},{8,10},{9,11},{10,... | collective-permute-start | bytes 589832 | tf_op jit(solution)/shard_map/ppermute | solution.py:38
  13.4 13.9 %collective-permute-start.3 = (bf16[64,1536]{1,0:T(8,128)(2,1)S(1)}, bf16[64,1536]{1,0:T(8,128)(2,1)S(1)}, u32[]{:S(2)}, u32[]{:S(2)}) collective-permute-start(bf16[64,1536]{1,0:T(8,128)(2,1)S(1)} %collective-permute-done.2.refs_0_), channel_id=1, source_target_pairs={{0,2},{1,3},{2,0},{3,1},{4,6},{5,7},{6,4},{7,5},{8,10},{9,11},{10,... | collective-permute-start | bytes 589832 | tf_op jit(solution)/shard_map/ppermute | solution.py:38
  15.1 11.0 %collective-permute-start.5 = (bf16[64,1536]{1,0:T(8,128)(2,1)S(1)}, bf16[64,1536]{1,0:T(8,128)(2,1)S(1)}, u32[]{:S(2)}, u32[]{:S(2)}) collective-permute-start(bf16[64,1536]{1,0:T(8,128)(2,1)S(1)} %collective-permute-done.2.refs_0_), channel_id=1, source_target_pairs={{0,1},{1,0},{2,3},{3,2},{4,5},{5,4},{6,7},{7,6},{8,9},{9,8},{10,11... | collective-permute-start | bytes 589832 | tf_op jit(solution)/shard_map/ppermute | solution.py:38
  16.9 0.7 copy-start
  27.3 6.8 %collective-permute-start.4 = (bf16[64,1536]{1,0:T(8,128)(2,1)S(1)}, bf16[64,1536]{1,0:T(8,128)(2,1)S(1)}, u32[]{:S(2)}, u32[]{:S(2)}) collective-permute-start(bf16[64,1536]{1,0:T(8,128)(2,1)S(1)} %collective-permute-done.3.refs_0_), channel_id=1, source_target_pairs={{0,1},{1,0},{2,3},{3,2},{4,5},{5,4},{6,7},{7,6},{8,9},{9,8},{10,11... | collective-permute-start | bytes 589832 | tf_op jit(solution)/shard_map/ppermute | solution.py:38
  27.3 6.8 %copy-start.1 = (s32[16]{0:T(128)S(1)}, s32[16]{0:T(128)}, u32[]{:S(2)}) copy-start(s32[16]{0:T(128)} %kept_ref.3) | copy-start | bytes 196
  32.0 7.1 %collective-permute-start.11 = (bf16[64,1536]{1,0:T(8,128)(2,1)S(1)}, bf16[64,1536]{1,0:T(8,128)(2,1)S(1)}, u32[]{:S(2)}, u32[]{:S(2)}) collective-permute-start(bf16[64,1536]{1,0:T(8,128)(2,1)S(1)} %collective-permute-done.10.refs_0_), channel_id=1, source_target_pairs={{0,1},{1,0},{2,3},{3,2},{4,5},{5,4},{6,7},{7,6},{8,9},{9,8},{10,11... | collective-permute-start | bytes 589832 | tf_op jit(solution)/shard_map/ppermute | solution.py:38
  34.1 24.5 %slice-start = ((s8[18874368]{0:T(1024)(128)(4,1)}), s8[4194304]{0:T(1024)(128)(4,1)S(1)}, s32[]{:S(2)}) async-start(s8[18874368]{0:T(1024)(128)(4,1)} %bitcast), calls=%async_computation | async-start | bytes 8388608
  34.1 24.5 %slice-start.1 = ((s8[18874368]{0:T(1024)(128)(4,1)}), s8[4194304]{0:T(1024)(128)(4,1)S(1)}, s32[]{:S(2)}) async-start(s8[18874368]{0:T(1024)(128)(4,1)} %bitcast), calls=%async_computation.1 | async-start | bytes 8388608
  34.1 24.5 %slice-start.2 = ((s8[18874368]{0:T(1024)(128)(4,1)}), s8[4194304]{0:T(1024)(128)(4,1)S(1)}, s32[]{:S(2)}) async-start(s8[18874368]{0:T(1024)(128)(4,1)} %bitcast), calls=%async_computation.2 | async-start | bytes 8388608
  39.0 19.7 %slice-start.3 = ((s8[18874368]{0:T(1024)(128)(4,1)}), s8[4194304]{0:T(1024)(128)(4,1)S(1)}, s32[]{:S(2)}) async-start(s8[18874368]{0:T(1024)(128)(4,1)} %bitcast), calls=%async_computation.3 | async-start | bytes 8388608
  39.0 19.6 %slice-start.4 = ((s8[18874368]{0:T(1024)(128)(4,1)}), s8[2097152]{0:T(1024)(128)(4,1)S(1)}, s32[]{:S(2)}) async-start(s8[18874368]{0:T(1024)(128)(4,1)} %bitcast), calls=%async_computation.4 | async-start | bytes 4194304
  39.0 6.9 %collective-permute-start.8 = (bf16[64,1664]{1,0:T(8,128)(2,1)S(1)}, bf16[64,1664]{1,0:T(8,128)(2,1)S(1)}, u32[]{:S(2)}, u32[]{:S(2)}) collective-permute-start(bf16[64,1664]{1,0:T(8,128)(2,1)S(1)} %get-tuple-element.79), channel_id=1, source_target_pairs={{0,1},{1,0},{2,3},{3,2},{4,5},{5,4},{6,7},{7,6},{8,9},{9,8},{10,11... | collective-permute-start | bytes 638984 | tf_op jit(solution)/shard_map/ppermute | solution.py:38
  43.8 12.5 %collective-permute-start.12 = (bf16[64,1664]{1,0:T(8,128)(2,1)S(1)}, bf16[64,1664]{1,0:T(8,128)(2,1)S(1)}, u32[]{:S(2)}, u32[]{:S(2)}) collective-permute-start(bf16[64,1664]{1,0:T(8,128)(2,1)S(1)} %get-tuple-element.88), channel_id=1, source_target_pairs={{0,1},{1,0},{2,3},{3,2},{4,5},{5,4},{6,7},{7,6},{8,9},{9,8},{10,11... | collective-permute-start | bytes 638984 | tf_op jit(solution)/shard_map/ppermute | solution.py:38
  45.8 12.8 %collective-permute-start.7 = (bf16[64,1664]{1,0:T(8,128)(2,1)S(1)}, bf16[64,1664]{1,0:T(8,128)(2,1)S(1)}, u32[]{:S(2)}, u32[]{:S(2)}) collective-permute-start(bf16[64,1664]{1,0:T(8,128)(2,1)S(1)} %get-tuple-element.78), channel_id=1, source_target_pairs={{0,1},{1,0},{2,3},{3,2},{4,5},{5,4},{6,7},{7,6},{8,9},{9,8},{10,11... | collective-permute-start | bytes 638984 | tf_op jit(solution)/shard_map/ppermute | solution.py:38
  46.3 12.3 %collective-permute-start.9 = (bf16[64,1664]{1,0:T(8,128)(2,1)S(1)}, bf16[64,1664]{1,0:T(8,128)(2,1)S(1)}, u32[]{:S(2)}, u32[]{:S(2)}) collective-permute-start(bf16[64,1664]{1,0:T(8,128)(2,1)S(1)} %merge.2), channel_id=1, source_target_pairs={{0,2},{1,3},{2,0},{3,1},{4,6},{5,7},{6,4},{7,5},{8,10},{9,11},{10,... | collective-permute-start | bytes 638984 | tf_op jit(solution)/shard_map/ppermute | solution.py:38
  62.4 3.6 %collective-permute-start.15 = (bf16[32,3072]{1,0:T(8,128)(2,1)S(1)}, bf16[32,3072]{1,0:T(8,128)(2,1)S(1)}, u32[]{:S(2)}, u32[]{:S(2)}) collective-permute-start(bf16[32,3072]{1,0:T(8,128)(2,1)S(1)} %get-tuple-element.104), channel_id=1, source_target_pairs={{0,4},{4,0},{8,12},{12,8},{1,5},{5,1},{9,13},{13,9},{2,6},{6,2},{1... | collective-permute-start | bytes 589832 | tf_op jit(solution)/shard_map/ppermute | solution.py:38
  62.5 3.5 %collective-permute-start.14 = (bf16[32,3072]{1,0:T(8,128)(2,1)S(1)}, bf16[32,3072]{1,0:T(8,128)(2,1)S(1)}, u32[]{:S(2)}, u32[]{:S(2)}) collective-permute-start(bf16[32,3072]{1,0:T(8,128)(2,1)S(1)} %get-tuple-element.103), channel_id=1, source_target_pairs={{0,4},{4,0},{8,12},{12,8},{1,5},{5,1},{9,13},{13,9},{2,6},{6,2},{1... | collective-permute-start | bytes 589832 | tf_op jit(solution)/shard_map/ppermute | solution.py:38
  63.0 11.3 %collective-permute-start.6 = (bf16[64,1664]{1,0:T(8,128)(2,1)S(1)}, bf16[64,1664]{1,0:T(8,128)(2,1)S(1)}, u32[]{:S(2)}, u32[]{:S(2)}) collective-permute-start(bf16[64,1664]{1,0:T(8,128)(2,1)S(1)} %get-tuple-element.75), channel_id=1, source_target_pairs={{0,1},{1,0},{2,3},{3,2},{4,5},{5,4},{6,7},{7,6},{8,9},{9,8},{10,11... | collective-permute-start | bytes 638984 | tf_op jit(solution)/shard_map/ppermute | solution.py:38
  65.6 12.5 %collective-permute-start.13 = (bf16[64,1664]{1,0:T(8,128)(2,1)S(1)}, bf16[64,1664]{1,0:T(8,128)(2,1)S(1)}, u32[]{:S(2)}, u32[]{:S(2)}) collective-permute-start(bf16[64,1664]{1,0:T(8,128)(2,1)S(1)} %merge.3), channel_id=1, source_target_pairs={{0,2},{1,3},{2,0},{3,1},{4,6},{5,7},{6,4},{7,5},{8,10},{9,11},{10,... | collective-permute-start | bytes 638984 | tf_op jit(solution)/shard_map/ppermute | solution.py:38
  78.0 10.0 %collective-permute-start.18 = (bf16[32,6144]{1,0:T(8,128)(2,1)S(1)}, bf16[32,6144]{1,0:T(8,128)(2,1)S(1)}, u32[]{:S(2)}, u32[]{:S(2)}) collective-permute-start(bf16[32,6144]{1,0:T(8,128)(2,1)S(1)} %add_convert_fusion.2), channel_id=1, source_target_pairs={{0,8},{4,12},{8,0},{12,4},{1,9},{5,13},{9,1},{13,5},{2,10},{6,14},... | collective-permute-start | bytes 1179656 | tf_op jit(solution)/shard_map/ppermute | solution.py:38
  82.5 1.5 %collective-permute-start.17 = (bf16[32,3072]{1,0:T(8,128)(2,1)S(1)}, bf16[32,3072]{1,0:T(8,128)(2,1)S(1)}, u32[]{:S(2)}, u32[]{:S(2)}) collective-permute-start(bf16[32,3072]{1,0:T(8,128)(2,1)S(1)} %get-tuple-element.102), channel_id=1, source_target_pairs={{0,4},{4,0},{8,12},{12,8},{1,5},{5,1},{9,13},{13,9},{2,6},{6,2},{1... | collective-permute-start | bytes 589832 | tf_op jit(solution)/shard_map/ppermute | solution.py:38
  82.5 1.7 %collective-permute-start.16 = (bf16[32,3072]{1,0:T(8,128)(2,1)S(1)}, bf16[32,3072]{1,0:T(8,128)(2,1)S(1)}, u32[]{:S(2)}, u32[]{:S(2)}) collective-permute-start(bf16[32,3072]{1,0:T(8,128)(2,1)S(1)} %get-tuple-element.101), channel_id=1, source_target_pairs={{0,4},{4,0},{8,12},{12,8},{1,5},{5,1},{9,13},{13,9},{2,6},{6,2},{1... | collective-permute-start | bytes 589832 | tf_op jit(solution)/shard_map/ppermute | solution.py:38

commit v4 on v3

--- a/solution.py
+++ b/solution.py
@@ -14,7 +14,7 @@
 LOW = -1e30
 SCALE2 = math.log2(math.e) / math.sqrt(HD)
 STEP = 32
-BLOCK = 512
+BLOCK = 1536
 CUTS = 2
 TILE = 128
 VMEM = 10 << 20
@@ -314,8 +314,8 @@
     theirs, through = lax.optimization_barrier((theirs, through))
     mine.append(swap(through, "ctx", n_ctx, far_off))
     done = fold(*project(theirs, out_weight, group), n_head, top, group)
-    mine, done = lax.optimization_barrier((mine, done))
     other = swap(done, "head", n_head, top)
+    mine = after(mine, done)
     done = fold(*project(mine, out_weight, group), n_head, top, group)
     return (done.astype(jnp.float32) + other.astype(jnp.float32)).astype(jnp.bfloat16)
 

time: 89.1 us -> 84.7 us (0.951)
  waiting for transfers between devices: 31.5 us -> 27.2 us
    ppermute x19, waiting for transfers between devices: 31.5 us -> 27.2 us  [swap(): return lax.ppermute(x, axis, [(i, i ^ bit) for i in range(size)])]
  transfers between devices with their start and end apart: 19 -> 19, of which waited for: 10 -> 9; matrix products, arithmetic and copies ran while one was open for 0% -> 0% of each run, Pallas kernels for 31% -> 32%
where the time goes in v4:
time: 84.7 us; the launch traced here: 84.5 us
  Pallas kernels  31 us (37%)
  waiting for transfers between devices  27.2 us (32%)
  starting transfers between devices  23.4 us (28%)
  local copies, waits for them, and re-layouts  1.82 us (2%)
  other arithmetic  1.03 us (1%)
    ppermute x19, waiting for transfers between devices, swap(): return lax.ppermute(x, axis, [(i, i ^ bit) for i in range(size)])  27.2 us
    ppermute x19, starting transfers between devices, swap(): return lax.ppermute(x, axis, [(i, i ^ bit) for i in range(size)])  23.4 us
    pallas_call x4, Pallas kernels, attend(): pl.pallas_call(functools.partial(attend_body, pieces=pieces, heads=heads,...  22.7 us
    pallas_call x2, Pallas kernels, project(): pl.pallas_call(functools.partial(project_body, count=len(parts), heads=we...  7.47 us
  transfers between devices with their start and end apart: 19, of which 9 were waited for; matrix products, arithmetic and copies ran while one was open for 0% of the time, Pallas kernels for 32%

profile of v4, /device:TPU:0, one launch (start us, length us, event | category | flops | bytes accessed | tf_op | source)
XLA Modules:
  0.0 84.5 jit_solution(15498055316703380830)
XLA Ops:
  0.0 1.1 %constant_dynamic-slice_fusion.3 = (bf16[32,1536]{1,0:T(8,128)(2,1)S(1)}, bf16[32,1536]{1,0:T(8,128)(2,1)S(1)}, bf16[32,1536]{1,0:T(8,128)(2,1)S(1)}, bf16[32,1536]{1,0:T(8,128)(2,1)S(1)}) fusion(bf16[32,6144]{1,0:T(8,128)(2,1)} %param.5, s32[]{:T(128)S(6)} %select_n.12, s32[]{:T(128)S(6)} %select_n.13, s32[]{:T(128)S(6)} %select_n.15, s32[]{:T(128)S(6)} %select_n.14), kind=kLoop, calls=%fused_computation.9 | loop fusion | bytes 786448 | tf_op jit(solution)/shard_map/dynamic_slice | solution.py:260
  1.1 0.5 collective-permute-start
  1.6 1.1 %collective-permute-done = bf16[64,1536]{1,0:T(8,128)(2,1)S(1)} collective-permute-done((bf16[64,1536]{1,0:T(8,128)(2,1)S(1)}, bf16[64,1536]{1,0:T(8,128)(2,1)S(1)}, u32[]{:S(2)}, u32[]{:S(2)}) %collective-permute-start) | collective-permute-done | bytes 196640 | tf_op jit(solution)/shard_map/ppermute | solution.py:38
  2.7 3.0 %collective-permute-start.1 = (bf16[64,1536]{1,0:T(8,128)(2,1)S(1)}, bf16[64,1536]{1,0:T(8,128)(2,1)S(1)}, u32[]{:S(2)}, u32[]{:S(2)}) collective-permute-start(bf16[64,1536]{1,0:T(8,128)(2,1)S(1)} %pad_maximum_fusion.1.refs_0_), channel_id=1, source_target_pairs={{0,1},{1,0},{2,3},{3,2},{4,5},{5,4},{6,7},{7,6},{8,9},{9,8},{10,11... | collective-permute-start | bytes 589832 | tf_op jit(solution)/shard_map/ppermute | solution.py:38
  5.7 1.6 %collective-permute-start.2 = (bf16[64,1536]{1,0:T(8,128)(2,1)S(1)}, bf16[64,1536]{1,0:T(8,128)(2,1)S(1)}, u32[]{:S(2)}, u32[]{:S(2)}) collective-permute-start(bf16[64,1536]{1,0:T(8,128)(2,1)S(1)} %pad_maximum_fusion.2), channel_id=1, source_target_pairs={{0,8},{4,12},{8,0},{12,4},{1,9},{5,13},{9,1},{13,5},{2,10},{6,14},... | collective-permute-start | bytes 589832 | tf_op jit(solution)/shard_map/ppermute | solution.py:38
  7.3 2.6 %collective-permute-start.10 = (bf16[64,1536]{1,0:T(8,128)(2,1)S(1)}, bf16[64,1536]{1,0:T(8,128)(2,1)S(1)}, u32[]{:S(2)}, u32[]{:S(2)}) collective-permute-start(bf16[64,1536]{1,0:T(8,128)(2,1)S(1)} %pad_maximum_fusion.1.refs_0_), channel_id=1, source_target_pairs={{0,2},{1,3},{2,0},{3,1},{4,6},{5,7},{6,4},{7,5},{8,10},{9,11},{10,... | collective-permute-start | bytes 589832 | tf_op jit(solution)/shard_map/ppermute | solution.py:38
  9.9 3.5 %collective-permute-done.1.refs_1_ = bf16[64,1536]{1,0:T(8,128)(2,1)S(1)} collective-permute-done((bf16[64,1536]{1,0:T(8,128)(2,1)S(1)}, bf16[64,1536]{1,0:T(8,128)(2,1)S(1)}, u32[]{:S(2)}, u32[]{:S(2)}) %collective-permute-start.1) | collective-permute-done | bytes 196640 | tf_op jit(solution)/shard_map/ppermute | solution.py:38
  13.4 0.0 collective-permute-done.2.refs_0_
  13.4 0.0 collective-permute-start.5
  13.4 3.6 %collective-permute-start.3 = (bf16[64,1536]{1,0:T(8,128)(2,1)S(1)}, bf16[64,1536]{1,0:T(8,128)(2,1)S(1)}, u32[]{:S(2)}, u32[]{:S(2)}) collective-permute-start(bf16[64,1536]{1,0:T(8,128)(2,1)S(1)} %collective-permute-done.2.refs_0_), channel_id=1, source_target_pairs={{0,2},{1,3},{2,0},{3,1},{4,6},{5,7},{6,4},{7,5},{8,10},{9,11},{10,... | collective-permute-start | bytes 589832 | tf_op jit(solution)/shard_map/ppermute | solution.py:38
  16.9 0.0 copy-start
  16.9 0.7 copy-done
  17.6 8.4 %attend.4 = (bf16[64,1664]{1,0:T(8,128)(2,1)S(1)}, bf16[64,1664]{1,0:T(8,128)(2,1)S(1)}, bf16[2048,1536]{1,0:T(8,128)(2,1)S(1)}, bf16[2048,1536]{1,0:T(8,128)(2,1)S(1)}) custom-call(s32[16]{0:T(128)S(1)} %copy-done, bf16[64,1536]{1,0:T(8,128)(2,1)S(1)} %pad_maximum_fusion.1.refs_0_, bf16[64,1536]{1,0:T(8,128)(2,1)S(1)} %collective-permute-done.1.refs_1_, ...), custom_call_target="tpu_custom_call" | custom-call | flops 6442450944 | bytes 12582912 | tf_op jit(solution)/shard_map/attend/pallas_call | solution.py:122
  26.0 0.0 collective-permute-done.5.refs_1_
  26.0 1.3 %collective-permute-done.3.refs_0_ = bf16[64,1536]{1,0:T(8,128)(2,1)S(1)} collective-permute-done((bf16[64,1536]{1,0:T(8,128)(2,1)S(1)}, bf16[64,1536]{1,0:T(8,128)(2,1)S(1)}, u32[]{:S(2)}, u32[]{:S(2)}) %collective-permute-start.3) | collective-permute-done | bytes 196640 | tf_op jit(solution)/shard_map/ppermute | solution.py:38
  27.3 0.0 collective-permute-start.4
  27.3 0.0 copy-start.1
  27.3 4.7 %attend.5 = (bf16[64,1664]{1,0:T(8,128)(2,1)S(1)}, bf16[64,1664]{1,0:T(8,128)(2,1)S(1)}) custom-call(s32[16]{0:T(128)S(1)} %copy-done, bf16[64,1536]{1,0:T(8,128)(2,1)S(1)} %collective-permute-done.2.refs_0_, bf16[64,1536]{1,0:T(8,128)(2,1)S(1)} %collective-permute-done.5.refs_1_, bf16[2048,1536]{1,0:T(8,128)(2,1)S(1)} %get-tuple-element.63.refs_2_, ...), custom_call_target="tpu_custom_call" | custom-call | flops 6442450944 | bytes 12582912 | tf_op jit(solution)/shard_map/attend/pallas_call | solution.py:122
  32.0 0.0 collective-permute-done.10.refs_0_
  32.0 2.1 %collective-permute-start.11 = (bf16[64,1536]{1,0:T(8,128)(2,1)S(1)}, bf16[64,1536]{1,0:T(8,128)(2,1)S(1)}, u32[]{:S(2)}, u32[]{:S(2)}) collective-permute-start(bf16[64,1536]{1,0:T(8,128)(2,1)S(1)} %collective-permute-done.10.refs_0_), channel_id=1, source_target_pairs={{0,1},{1,0},{2,3},{3,2},{4,5},{5,4},{6,7},{7,6},{8,9},{9,8},{10,11... | collective-permute-start | bytes 589832 | tf_op jit(solution)/shard_map/ppermute | solution.py:38
  34.1 0.0 collective-permute-done.4.refs_1_
  34.1 0.0 copy-done.1
  34.1 0.0 slice-start
  34.1 0.0 slice-start.1
  34.1 0.0 slice-start.2
  34.1 4.9 %attend.6 = (bf16[64,1664]{1,0:T(8,128)(2,1)S(1)}, bf16[64,1664]{1,0:T(8,128)(2,1)S(1)}) custom-call(s32[16]{0:T(128)S(1)} %copy-done.1, bf16[64,1536]{1,0:T(8,128)(2,1)S(1)} %collective-permute-done.3.refs_0_, bf16[64,1536]{1,0:T(8,128)(2,1)S(1)} %collective-permute-done.4.refs_1_, bf16[2048,1536]{1,0:T(8,128)(2,1)S(1)} %get-tuple-element.63.refs_2_, ...), custom_call_target="tpu_custom_call" | custom-call | flops 6442450944 | bytes 12582912 | tf_op jit(solution)/shard_map/attend/pallas_call | solution.py:122
  39.0 0.0 slice-start.3
  39.0 0.0 slice-start.4
  39.0 0.0 collective-permute-done.11.refs_1_
  39.0 0.7 collective-permute-start.8
  39.8 4.7 %attend.7 = (bf16[64,1664]{1,0:T(8,128)(2,1)S(1)}, bf16[64,1664]{1,0:T(8,128)(2,1)S(1)}) custom-call(s32[16]{0:T(128)S(1)} %copy-done.1, bf16[64,1536]{1,0:T(8,128)(2,1)S(1)} %collective-permute-done.10.refs_0_, bf16[64,1536]{1,0:T(8,128)(2,1)S(1)} %collective-permute-done.11.refs_1_, bf16[2048,1536]{1,0:T(8,128)(2,1)S(1)} %get-tuple-element.63.refs_2_, ...), custom_call_target="tpu_custom_call" | custom-call | flops 6442450944 | bytes 12582912 | tf_op jit(solution)/shard_map/attend/pallas_call | solution.py:122
  44.5 1.4 %collective-permute-start.12 = (bf16[64,1664]{1,0:T(8,128)(2,1)S(1)}, bf16[64,1664]{1,0:T(8,128)(2,1)S(1)}, u32[]{:S(2)}, u32[]{:S(2)}) collective-permute-start(bf16[64,1664]{1,0:T(8,128)(2,1)S(1)} %get-tuple-element.87), channel_id=1, source_target_pairs={{0,1},{1,0},{2,3},{3,2},{4,5},{5,4},{6,7},{7,6},{8,9},{9,8},{10,11... | collective-permute-start | bytes 638984 | tf_op jit(solution)/shard_map/ppermute | solution.py:38
  45.9 0.7 collective-permute-start.7
  46.6 0.0 collective-permute-done.8.refs_1_
  46.6 0.4 merge.2
  47.0 2.4 %collective-permute-start.9 = (bf16[64,1664]{1,0:T(8,128)(2,1)S(1)}, bf16[64,1664]{1,0:T(8,128)(2,1)S(1)}, u32[]{:S(2)}, u32[]{:S(2)}) collective-permute-start(bf16[64,1664]{1,0:T(8,128)(2,1)S(1)} %merge.2), channel_id=1, source_target_pairs={{0,2},{1,3},{2,0},{3,1},{4,6},{5,7},{6,4},{7,5},{8,10},{9,11},{10,... | collective-permute-start | bytes 638984 | tf_op jit(solution)/shard_map/ppermute | solution.py:38
  49.4 7.0 %collective-permute-done.12.refs_1_ = bf16[64,1664]{1,0:T(8,128)(2,1)S(1)} collective-permute-done((bf16[64,1664]{1,0:T(8,128)(2,1)S(1)}, bf16[64,1664]{1,0:T(8,128)(2,1)S(1)}, u32[]{:S(2)}, u32[]{:S(2)}) %collective-permute-start.12) | collective-permute-done | bytes 213024 | tf_op jit(solution)/shard_map/ppermute | solution.py:38
  56.4 0.4 merge.3
  56.8 1.9 %collective-permute-done.7.refs_1_ = bf16[64,1664]{1,0:T(8,128)(2,1)S(1)} collective-permute-done((bf16[64,1664]{1,0:T(8,128)(2,1)S(1)}, bf16[64,1664]{1,0:T(8,128)(2,1)S(1)}, u32[]{:S(2)}, u32[]{:S(2)}) %collective-permute-start.7) | collective-permute-done | bytes 213024 | tf_op jit(solution)/shard_map/ppermute | solution.py:38
  58.7 0.0 collective-permute-done.9.refs_2_
  58.7 0.0 slice-done
  58.7 0.0 slice-done.1
  58.7 0.0 slice-done.2
  58.7 0.0 slice-done.3
  58.7 0.0 slice-done.4
  58.7 3.7 %project.2 = (bf16[32,6144]{1,0:T(8,128)(2,1)S(1)}, bf16[32,6144]{1,0:T(8,128)(2,1)S(1)}) custom-call(bf16[64,1664]{1,0:T(8,128)(2,1)S(1)} %get-tuple-element.89.refs_0_, bf16[64,1664]{1,0:T(8,128)(2,1)S(1)} %collective-permute-done.7.refs_1_, bf16[64,1664]{1,0:T(8,128)(2,1)S(1)} %collective-permute-done.9.refs_2_, bf16[1536,6144]{1,0:T(8,128)(2,1)S(1)} %bitcast.1), custom_call_target="tpu_custom_call" | custom-call | flops 1 | bytes 1 | tf_op jit(solution)/shard_map/project/pallas_call | solution.py:195
  62.5 0.1 collective-permute-start.14
  62.6 0.5 collective-permute-start.15
  63.1 2.6 %collective-permute-start.6 = (bf16[64,1664]{1,0:T(8,128)(2,1)S(1)}, bf16[64,1664]{1,0:T(8,128)(2,1)S(1)}, u32[]{:S(2)}, u32[]{:S(2)}) collective-permute-start(bf16[64,1664]{1,0:T(8,128)(2,1)S(1)} %get-tuple-element.74), channel_id=1, source_target_pairs={{0,1},{1,0},{2,3},{3,2},{4,5},{5,4},{6,7},{7,6},{8,9},{9,8},{10,11... | collective-permute-start | bytes 638984 | tf_op jit(solution)/shard_map/ppermute | solution.py:38
  65.6 0.5 collective-permute-start.13
  66.1 0.0 collective-permute-done.14
  66.1 0.0 collective-permute-done.15
  66.1 0.1 add_convert_fusion.2
  66.2 0.6 collective-permute-start.18
  66.8 7.6 %collective-permute-done.6.refs_1_ = bf16[64,1664]{1,0:T(8,128)(2,1)S(1)} collective-permute-done((bf16[64,1664]{1,0:T(8,128)(2,1)S(1)}, bf16[64,1664]{1,0:T(8,128)(2,1)S(1)}, u32[]{:S(2)}, u32[]{:S(2)}) %collective-permute-start.6) | collective-permute-done | bytes 213024 | tf_op jit(solution)/shard_map/ppermute | solution.py:38
  74.4 3.7 %collective-permute-done.13.refs_2_ = bf16[64,1664]{1,0:T(8,128)(2,1)S(1)} collective-permute-done((bf16[64,1664]{1,0:T(8,128)(2,1)S(1)}, bf16[64,1664]{1,0:T(8,128)(2,1)S(1)}, u32[]{:S(2)}, u32[]{:S(2)}) %collective-permute-start.13) | collective-permute-done | bytes 213024 | tf_op jit(solution)/shard_map/ppermute | solution.py:38
  78.1 3.7 %project.3 = (bf16[32,6144]{1,0:T(8,128)(2,1)S(1)}, bf16[32,6144]{1,0:T(8,128)(2,1)S(1)}) custom-call(bf16[64,1664]{1,0:T(8,128)(2,1)S(1)} %get-tuple-element.94.refs_0_, bf16[64,1664]{1,0:T(8,128)(2,1)S(1)} %collective-permute-done.6.refs_1_, bf16[64,1664]{1,0:T(8,128)(2,1)S(1)} %collective-permute-done.13.refs_2_, bf16[1536,6144]{1,0:T(8,128)(2,1)S(1)} %bitcast.1), custom_call_target="tpu_custom_call" | custom-call | flops 1 | bytes 1 | tf_op jit(solution)/shard_map/project/pallas_call | solution.py:195
  81.9 0.1 collective-permute-start.16
  81.9 0.5 collective-permute-start.17
  82.4 0.9 %collective-permute-done.16 = bf16[32,3072]{1,0:T(8,128)(2,1)S(1)} collective-permute-done((bf16[32,3072]{1,0:T(8,128)(2,1)S(1)}, bf16[32,3072]{1,0:T(8,128)(2,1)S(1)}, u32[]{:S(2)}, u32[]{:S(2)}) %collective-permute-start.16) | collective-permute-done | bytes 196640 | tf_op jit(solution)/shard_map/ppermute | solution.py:38
  83.4 0.3 collective-permute-done.17
  83.6 0.0 collective-permute-done.18
  83.7 0.9 %add_convert_fusion = bf16[32,6144]{1,0:T(8,128)(2,1)} fusion(bf16[32,6144]{1,0:T(8,128)(2,1)S(1)} %collective-permute-done.18, bf16[32,6144]{1,0:T(8,128)(2,1)S(1)} %get-tuple-element.97, bf16[32,3072]{1,0:T(8,128)(2,1)S(1)} %collective-permute-done.17, bf16[32,3072]{1,0:T(8,128)(2,1)S(1)} %collective-permute-done.16), kind=kLoop, calls=%fused_computation | loop fusion | flops 2162688 | bytes 1572864 | tf_op jit(solution)/shard_map/convert_element_type | solution.py:320
  (7 shorter events, 0.1 us)
Async XLA Ops:
  1.1 1.6 %collective-permute-start = (bf16[64,1536]{1,0:T(8,128)(2,1)S(1)}, bf16[64,1536]{1,0:T(8,128)(2,1)S(1)}, u32[]{:S(2)}, u32[]{:S(2)}) collective-permute-start(bf16[64,1536]{1,0:T(8,128)(2,1)S(1)} %pad_maximum_fusion), channel_id=1, source_target_pairs={{0,4},{4,0},{8,12},{12,8},{1,5},{5,1},{9,13},{13,9},{2,6},{6,2},{1... | collective-permute-start | bytes 589832 | tf_op jit(solution)/shard_map/ppermute | solution.py:38
  2.7 10.6 %collective-permute-start.1 = (bf16[64,1536]{1,0:T(8,128)(2,1)S(1)}, bf16[64,1536]{1,0:T(8,128)(2,1)S(1)}, u32[]{:S(2)}, u32[]{:S(2)}) collective-permute-start(bf16[64,1536]{1,0:T(8,128)(2,1)S(1)} %pad_maximum_fusion.1.refs_0_), channel_id=1, source_target_pairs={{0,1},{1,0},{2,3},{3,2},{4,5},{5,4},{6,7},{7,6},{8,9},{9,8},{10,11... | collective-permute-start | bytes 589832 | tf_op jit(solution)/shard_map/ppermute | solution.py:38
  5.7 7.6 %collective-permute-start.2 = (bf16[64,1536]{1,0:T(8,128)(2,1)S(1)}, bf16[64,1536]{1,0:T(8,128)(2,1)S(1)}, u32[]{:S(2)}, u32[]{:S(2)}) collective-permute-start(bf16[64,1536]{1,0:T(8,128)(2,1)S(1)} %pad_maximum_fusion.2), channel_id=1, source_target_pairs={{0,8},{4,12},{8,0},{12,4},{1,9},{5,13},{9,1},{13,5},{2,10},{6,14},... | collective-permute-start | bytes 589832 | tf_op jit(solution)/shard_map/ppermute | solution.py:38
  7.3 24.7 %collective-permute-start.10 = (bf16[64,1536]{1,0:T(8,128)(2,1)S(1)}, bf16[64,1536]{1,0:T(8,128)(2,1)S(1)}, u32[]{:S(2)}, u32[]{:S(2)}) collective-permute-start(bf16[64,1536]{1,0:T(8,128)(2,1)S(1)} %pad_maximum_fusion.1.refs_0_), channel_id=1, source_target_pairs={{0,2},{1,3},{2,0},{3,1},{4,6},{5,7},{6,4},{7,5},{8,10},{9,11},{10,... | collective-permute-start | bytes 589832 | tf_op jit(solution)/shard_map/ppermute | solution.py:38
  13.4 12.7 %collective-permute-start.5 = (bf16[64,1536]{1,0:T(8,128)(2,1)S(1)}, bf16[64,1536]{1,0:T(8,128)(2,1)S(1)}, u32[]{:S(2)}, u32[]{:S(2)}) collective-permute-start(bf16[64,1536]{1,0:T(8,128)(2,1)S(1)} %collective-permute-done.2.refs_0_), channel_id=1, source_target_pairs={{0,1},{1,0},{2,3},{3,2},{4,5},{5,4},{6,7},{7,6},{8,9},{9,8},{10,11... | collective-permute-start | bytes 589832 | tf_op jit(solution)/shard_map/ppermute | solution.py:38
  13.4 14.0 %collective-permute-start.3 = (bf16[64,1536]{1,0:T(8,128)(2,1)S(1)}, bf16[64,1536]{1,0:T(8,128)(2,1)S(1)}, u32[]{:S(2)}, u32[]{:S(2)}) collective-permute-start(bf16[64,1536]{1,0:T(8,128)(2,1)S(1)} %collective-permute-done.2.refs_0_), channel_id=1, source_target_pairs={{0,2},{1,3},{2,0},{3,1},{4,6},{5,7},{6,4},{7,5},{8,10},{9,11},{10,... | collective-permute-start | bytes 589832 | tf_op jit(solution)/shard_map/ppermute | solution.py:38
  16.9 0.7 copy-start
  27.3 6.8 %collective-permute-start.4 = (bf16[64,1536]{1,0:T(8,128)(2,1)S(1)}, bf16[64,1536]{1,0:T(8,128)(2,1)S(1)}, u32[]{:S(2)}, u32[]{:S(2)}) collective-permute-start(bf16[64,1536]{1,0:T(8,128)(2,1)S(1)} %collective-permute-done.3.refs_0_), channel_id=1, source_target_pairs={{0,1},{1,0},{2,3},{3,2},{4,5},{5,4},{6,7},{7,6},{8,9},{9,8},{10,11... | collective-permute-start | bytes 589832 | tf_op jit(solution)/shard_map/ppermute | solution.py:38
  27.3 6.8 %copy-start.1 = (s32[16]{0:T(128)S(1)}, s32[16]{0:T(128)}, u32[]{:S(2)}) copy-start(s32[16]{0:T(128)} %kept_ref.3) | copy-start | bytes 196
  32.0 7.0 %collective-permute-start.11 = (bf16[64,1536]{1,0:T(8,128)(2,1)S(1)}, bf16[64,1536]{1,0:T(8,128)(2,1)S(1)}, u32[]{:S(2)}, u32[]{:S(2)}) collective-permute-start(bf16[64,1536]{1,0:T(8,128)(2,1)S(1)} %collective-permute-done.10.refs_0_), channel_id=1, source_target_pairs={{0,1},{1,0},{2,3},{3,2},{4,5},{5,4},{6,7},{7,6},{8,9},{9,8},{10,11... | collective-permute-start | bytes 589832 | tf_op jit(solution)/shard_map/ppermute | solution.py:38
  34.1 24.5 %slice-start = ((s8[18874368]{0:T(1024)(128)(4,1)}), s8[4194304]{0:T(1024)(128)(4,1)S(1)}, s32[]{:S(2)}) async-start(s8[18874368]{0:T(1024)(128)(4,1)} %bitcast), calls=%async_computation | async-start | bytes 8388608
  34.1 24.5 %slice-start.1 = ((s8[18874368]{0:T(1024)(128)(4,1)}), s8[4194304]{0:T(1024)(128)(4,1)S(1)}, s32[]{:S(2)}) async-start(s8[18874368]{0:T(1024)(128)(4,1)} %bitcast), calls=%async_computation.1 | async-start | bytes 8388608
  34.1 24.5 %slice-start.2 = ((s8[18874368]{0:T(1024)(128)(4,1)}), s8[4194304]{0:T(1024)(128)(4,1)S(1)}, s32[]{:S(2)}) async-start(s8[18874368]{0:T(1024)(128)(4,1)} %bitcast), calls=%async_computation.2 | async-start | bytes 8388608
  39.0 19.7 %slice-start.3 = ((s8[18874368]{0:T(1024)(128)(4,1)}), s8[4194304]{0:T(1024)(128)(4,1)S(1)}, s32[]{:S(2)}) async-start(s8[18874368]{0:T(1024)(128)(4,1)} %bitcast), calls=%async_computation.3 | async-start | bytes 8388608
  39.0 19.7 %slice-start.4 = ((s8[18874368]{0:T(1024)(128)(4,1)}), s8[2097152]{0:T(1024)(128)(4,1)S(1)}, s32[]{:S(2)}) async-start(s8[18874368]{0:T(1024)(128)(4,1)} %bitcast), calls=%async_computation.4 | async-start | bytes 4194304
  39.0 7.5 %collective-permute-start.8 = (bf16[64,1664]{1,0:T(8,128)(2,1)S(1)}, bf16[64,1664]{1,0:T(8,128)(2,1)S(1)}, u32[]{:S(2)}, u32[]{:S(2)}) collective-permute-start(bf16[64,1664]{1,0:T(8,128)(2,1)S(1)} %get-tuple-element.78), channel_id=1, source_target_pairs={{0,1},{1,0},{2,3},{3,2},{4,5},{5,4},{6,7},{7,6},{8,9},{9,8},{10,11... | collective-permute-start | bytes 638984 | tf_op jit(solution)/shard_map/ppermute | solution.py:38
  44.5 11.9 %collective-permute-start.12 = (bf16[64,1664]{1,0:T(8,128)(2,1)S(1)}, bf16[64,1664]{1,0:T(8,128)(2,1)S(1)}, u32[]{:S(2)}, u32[]{:S(2)}) collective-permute-start(bf16[64,1664]{1,0:T(8,128)(2,1)S(1)} %get-tuple-element.87), channel_id=1, source_target_pairs={{0,1},{1,0},{2,3},{3,2},{4,5},{5,4},{6,7},{7,6},{8,9},{9,8},{10,11... | collective-permute-start | bytes 638984 | tf_op jit(solution)/shard_map/ppermute | solution.py:38
  45.9 12.8 %collective-permute-start.7 = (bf16[64,1664]{1,0:T(8,128)(2,1)S(1)}, bf16[64,1664]{1,0:T(8,128)(2,1)S(1)}, u32[]{:S(2)}, u32[]{:S(2)}) collective-permute-start(bf16[64,1664]{1,0:T(8,128)(2,1)S(1)} %get-tuple-element.77), channel_id=1, source_target_pairs={{0,1},{1,0},{2,3},{3,2},{4,5},{5,4},{6,7},{7,6},{8,9},{9,8},{10,11... | collective-permute-start | bytes 638984 | tf_op jit(solution)/shard_map/ppermute | solution.py:38
  47.0 11.7 %collective-permute-start.9 = (bf16[64,1664]{1,0:T(8,128)(2,1)S(1)}, bf16[64,1664]{1,0:T(8,128)(2,1)S(1)}, u32[]{:S(2)}, u32[]{:S(2)}) collective-permute-start(bf16[64,1664]{1,0:T(8,128)(2,1)S(1)} %merge.2), channel_id=1, source_target_pairs={{0,2},{1,3},{2,0},{3,1},{4,6},{5,7},{6,4},{7,5},{8,10},{9,11},{10,... | collective-permute-start | bytes 638984 | tf_op jit(solution)/shard_map/ppermute | solution.py:38
  62.5 3.6 %collective-permute-start.14 = (bf16[32,3072]{1,0:T(8,128)(2,1)S(1)}, bf16[32,3072]{1,0:T(8,128)(2,1)S(1)}, u32[]{:S(2)}, u32[]{:S(2)}) collective-permute-start(bf16[32,3072]{1,0:T(8,128)(2,1)S(1)} %get-tuple-element.101), channel_id=1, source_target_pairs={{0,4},{4,0},{8,12},{12,8},{1,5},{5,1},{9,13},{13,9},{2,6},{6,2},{1... | collective-permute-start | bytes 589832 | tf_op jit(solution)/shard_map/ppermute | solution.py:38
  62.6 3.5 %collective-permute-start.15 = (bf16[32,3072]{1,0:T(8,128)(2,1)S(1)}, bf16[32,3072]{1,0:T(8,128)(2,1)S(1)}, u32[]{:S(2)}, u32[]{:S(2)}) collective-permute-start(bf16[32,3072]{1,0:T(8,128)(2,1)S(1)} %get-tuple-element.102), channel_id=1, source_target_pairs={{0,4},{4,0},{8,12},{12,8},{1,5},{5,1},{9,13},{13,9},{2,6},{6,2},{1... | collective-permute-start | bytes 589832 | tf_op jit(solution)/shard_map/ppermute | solution.py:38
  63.1 11.3 %collective-permute-start.6 = (bf16[64,1664]{1,0:T(8,128)(2,1)S(1)}, bf16[64,1664]{1,0:T(8,128)(2,1)S(1)}, u32[]{:S(2)}, u32[]{:S(2)}) collective-permute-start(bf16[64,1664]{1,0:T(8,128)(2,1)S(1)} %get-tuple-element.74), channel_id=1, source_target_pairs={{0,1},{1,0},{2,3},{3,2},{4,5},{5,4},{6,7},{7,6},{8,9},{9,8},{10,11... | collective-permute-start | bytes 638984 | tf_op jit(solution)/shard_map/ppermute | solution.py:38
  65.6 12.5 %collective-permute-start.13 = (bf16[64,1664]{1,0:T(8,128)(2,1)S(1)}, bf16[64,1664]{1,0:T(8,128)(2,1)S(1)}, u32[]{:S(2)}, u32[]{:S(2)}) collective-permute-start(bf16[64,1664]{1,0:T(8,128)(2,1)S(1)} %merge.3), channel_id=1, source_target_pairs={{0,2},{1,3},{2,0},{3,1},{4,6},{5,7},{6,4},{7,5},{8,10},{9,11},{10,... | collective-permute-start | bytes 638984 | tf_op jit(solution)/shard_map/ppermute | solution.py:38
  66.2 17.5 %collective-permute-start.18 = (bf16[32,6144]{1,0:T(8,128)(2,1)S(1)}, bf16[32,6144]{1,0:T(8,128)(2,1)S(1)}, u32[]{:S(2)}, u32[]{:S(2)}) collective-permute-start(bf16[32,6144]{1,0:T(8,128)(2,1)S(1)} %add_convert_fusion.2), channel_id=1, source_target_pairs={{0,8},{4,12},{8,0},{12,4},{1,9},{5,13},{9,1},{13,5},{2,10},{6,14},... | collective-permute-start | bytes 1179656 | tf_op jit(solution)/shard_map/ppermute | solution.py:38
  81.9 1.5 %collective-permute-start.16 = (bf16[32,3072]{1,0:T(8,128)(2,1)S(1)}, bf16[32,3072]{1,0:T(8,128)(2,1)S(1)}, u32[]{:S(2)}, u32[]{:S(2)}) collective-permute-start(bf16[32,3072]{1,0:T(8,128)(2,1)S(1)} %get-tuple-element.99), channel_id=1, source_target_pairs={{0,4},{4,0},{8,12},{12,8},{1,5},{5,1},{9,13},{13,9},{2,6},{6,2},{1... | collective-permute-start | bytes 589832 | tf_op jit(solution)/shard_map/ppermute | solution.py:38
  81.9 1.7 %collective-permute-start.17 = (bf16[32,3072]{1,0:T(8,128)(2,1)S(1)}, bf16[32,3072]{1,0:T(8,128)(2,1)S(1)}, u32[]{:S(2)}, u32[]{:S(2)}) collective-permute-start(bf16[32,3072]{1,0:T(8,128)(2,1)S(1)} %get-tuple-element.100), channel_id=1, source_target_pairs={{0,4},{4,0},{8,12},{12,8},{1,5},{5,1},{9,13},{13,9},{2,6},{6,2},{1... | collective-permute-start | bytes 589832 | tf_op jit(solution)/shard_map/ppermute | solution.py:38

commit v5 on v4

--- a/solution.py
+++ b/solution.py
@@ -301,9 +301,8 @@
     own[far_off] = after(own[far_off], parts[1][0])
     sides[0] = rest(own, n_ctx)
     run([(1, d) for d in [far_off] + others], [])
-    for side in (0, 1):
-        parts[side][1] = after(parts[side][1], parts[1][far_off])
-        send(side, 1)
+    parts[1][1] = after(parts[1][1], parts[1][far_off])
+    send(1, 1)
     relay = passed(1)
     run([(0, d) for d in [far_off] + others], [])
     theirs_through = merge(relay, local_heads)
@@ -314,6 +313,7 @@
     theirs, through = lax.optimization_barrier((theirs, through))
     mine.append(swap(through, "ctx", n_ctx, far_off))
     done = fold(*project(theirs, out_weight, group), n_head, top, group)
+    mine[1] = swap(after(mine[1], done), "ctx", n_ctx, 1)
     other = swap(done, "head", n_head, top)
     mine = after(mine, done)
     done = fold(*project(mine, out_weight, group), n_head, top, group)

time: 84.7 us -> 82.4 us (0.973)
  waiting for transfers between devices: 27.2 us -> 24.2 us
    ppermute x19, waiting for transfers between devices: 27.2 us -> 24.2 us  [swap(): return lax.ppermute(x, axis, [(i, i ^ bit) for i in range(size)])]
  transfers between devices with their start and end apart: 19 -> 19, of which waited for: 9 -> 8; matrix products, arithmetic and copies ran while one was open for 0% -> 0% of each run, Pallas kernels for 32% -> 33%
where the time goes in v5:
time: 82.4 us; the launch traced here: 82.2 us
  Pallas kernels  31 us (38%)
  waiting for transfers between devices  24.2 us (29%)
  starting transfers between devices  24 us (29%)
  local copies, waits for them, and re-layouts  1.82 us (2%)
  other arithmetic  1.03 us (1%)
    ppermute x19, waiting for transfers between devices, swap(): return lax.ppermute(x, axis, [(i, i ^ bit) for i in range(size)])  24.2 us
    ppermute x19, starting transfers between devices, swap(): return lax.ppermute(x, axis, [(i, i ^ bit) for i in range(size)])  24 us
    pallas_call x4, Pallas kernels, attend(): pl.pallas_call(functools.partial(attend_body, pieces=pieces, heads=heads,...  22.7 us
    pallas_call x2, Pallas kernels, project(): pl.pallas_call(functools.partial(project_body, count=len(parts), heads=we...  7.47 us
  transfers between devices with their start and end apart: 19, of which 8 were waited for; matrix products, arithmetic and copies ran while one was open for 0% of the time, Pallas kernels for 33%

profile of v5, /device:TPU:0, one launch (start us, length us, event | category | flops | bytes accessed | tf_op | source)
XLA Modules:
  0.0 82.2 jit_solution(6729362951914435924)
XLA Ops:
  0.0 1.1 %constant_dynamic-slice_fusion.3 = (bf16[32,1536]{1,0:T(8,128)(2,1)S(1)}, bf16[32,1536]{1,0:T(8,128)(2,1)S(1)}, bf16[32,1536]{1,0:T(8,128)(2,1)S(1)}, bf16[32,1536]{1,0:T(8,128)(2,1)S(1)}) fusion(bf16[32,6144]{1,0:T(8,128)(2,1)} %param.5, s32[]{:T(128)S(6)} %select_n.12, s32[]{:T(128)S(6)} %select_n.13, s32[]{:T(128)S(6)} %select_n.15, s32[]{:T(128)S(6)} %select_n.14), kind=kLoop, calls=%fused_computation.9 | loop fusion | bytes 786448 | tf_op jit(solution)/shard_map/dynamic_slice | solution.py:260
  1.1 0.5 collective-permute-start
  1.6 1.1 %collective-permute-done = bf16[64,1536]{1,0:T(8,128)(2,1)S(1)} collective-permute-done((bf16[64,1536]{1,0:T(8,128)(2,1)S(1)}, bf16[64,1536]{1,0:T(8,128)(2,1)S(1)}, u32[]{:S(2)}, u32[]{:S(2)}) %collective-permute-start) | collective-permute-done | bytes 196640 | tf_op jit(solution)/shard_map/ppermute | solution.py:38
  2.7 3.0 %collective-permute-start.1 = (bf16[64,1536]{1,0:T(8,128)(2,1)S(1)}, bf16[64,1536]{1,0:T(8,128)(2,1)S(1)}, u32[]{:S(2)}, u32[]{:S(2)}) collective-permute-start(bf16[64,1536]{1,0:T(8,128)(2,1)S(1)} %pad_maximum_fusion.1.refs_0_), channel_id=1, source_target_pairs={{0,1},{1,0},{2,3},{3,2},{4,5},{5,4},{6,7},{7,6},{8,9},{9,8},{10,11... | collective-permute-start | bytes 589832 | tf_op jit(solution)/shard_map/ppermute | solution.py:38
  5.7 1.6 %collective-permute-start.2 = (bf16[64,1536]{1,0:T(8,128)(2,1)S(1)}, bf16[64,1536]{1,0:T(8,128)(2,1)S(1)}, u32[]{:S(2)}, u32[]{:S(2)}) collective-permute-start(bf16[64,1536]{1,0:T(8,128)(2,1)S(1)} %pad_maximum_fusion.2), channel_id=1, source_target_pairs={{0,8},{4,12},{8,0},{12,4},{1,9},{5,13},{9,1},{13,5},{2,10},{6,14},... | collective-permute-start | bytes 589832 | tf_op jit(solution)/shard_map/ppermute | solution.py:38
  7.3 2.6 %collective-permute-start.9 = (bf16[64,1536]{1,0:T(8,128)(2,1)S(1)}, bf16[64,1536]{1,0:T(8,128)(2,1)S(1)}, u32[]{:S(2)}, u32[]{:S(2)}) collective-permute-start(bf16[64,1536]{1,0:T(8,128)(2,1)S(1)} %pad_maximum_fusion.1.refs_0_), channel_id=1, source_target_pairs={{0,2},{1,3},{2,0},{3,1},{4,6},{5,7},{6,4},{7,5},{8,10},{9,11},{10,... | collective-permute-start | bytes 589832 | tf_op jit(solution)/shard_map/ppermute | solution.py:38
  9.9 3.5 %collective-permute-done.1.refs_1_ = bf16[64,1536]{1,0:T(8,128)(2,1)S(1)} collective-permute-done((bf16[64,1536]{1,0:T(8,128)(2,1)S(1)}, bf16[64,1536]{1,0:T(8,128)(2,1)S(1)}, u32[]{:S(2)}, u32[]{:S(2)}) %collective-permute-start.1) | collective-permute-done | bytes 196640 | tf_op jit(solution)/shard_map/ppermute | solution.py:38
  13.4 0.0 collective-permute-done.2.refs_0_
  13.4 0.0 collective-permute-start.3
  13.4 3.6 %collective-permute-start.4 = (bf16[64,1536]{1,0:T(8,128)(2,1)S(1)}, bf16[64,1536]{1,0:T(8,128)(2,1)S(1)}, u32[]{:S(2)}, u32[]{:S(2)}) collective-permute-start(bf16[64,1536]{1,0:T(8,128)(2,1)S(1)} %collective-permute-done.2.refs_0_), channel_id=1, source_target_pairs={{0,2},{1,3},{2,0},{3,1},{4,6},{5,7},{6,4},{7,5},{8,10},{9,11},{10,... | collective-permute-start | bytes 589832 | tf_op jit(solution)/shard_map/ppermute | solution.py:38
  16.9 0.0 copy-start
  16.9 0.7 copy-done
  17.6 8.4 %attend.4 = (bf16[64,1664]{1,0:T(8,128)(2,1)S(1)}, bf16[64,1664]{1,0:T(8,128)(2,1)S(1)}, bf16[2048,1536]{1,0:T(8,128)(2,1)S(1)}, bf16[2048,1536]{1,0:T(8,128)(2,1)S(1)}) custom-call(s32[16]{0:T(128)S(1)} %copy-done, bf16[64,1536]{1,0:T(8,128)(2,1)S(1)} %pad_maximum_fusion.1.refs_0_, bf16[64,1536]{1,0:T(8,128)(2,1)S(1)} %collective-permute-done.1.refs_1_, ...), custom_call_target="tpu_custom_call" | custom-call | flops 6442450944 | bytes 12582912 | tf_op jit(solution)/shard_map/attend/pallas_call | solution.py:122
  26.0 0.0 collective-permute-done.3.refs_1_
  26.0 1.3 %collective-permute-done.4.refs_0_ = bf16[64,1536]{1,0:T(8,128)(2,1)S(1)} collective-permute-done((bf16[64,1536]{1,0:T(8,128)(2,1)S(1)}, bf16[64,1536]{1,0:T(8,128)(2,1)S(1)}, u32[]{:S(2)}, u32[]{:S(2)}) %collective-permute-start.4) | collective-permute-done | bytes 196640 | tf_op jit(solution)/shard_map/ppermute | solution.py:38
  27.3 0.0 collective-permute-start.5
  27.3 0.0 copy-start.1
  27.3 4.7 %attend.5 = (bf16[64,1664]{1,0:T(8,128)(2,1)S(1)}, bf16[64,1664]{1,0:T(8,128)(2,1)S(1)}) custom-call(s32[16]{0:T(128)S(1)} %copy-done, bf16[64,1536]{1,0:T(8,128)(2,1)S(1)} %collective-permute-done.2.refs_0_, bf16[64,1536]{1,0:T(8,128)(2,1)S(1)} %collective-permute-done.3.refs_1_, bf16[2048,1536]{1,0:T(8,128)(2,1)S(1)} %get-tuple-element.63.refs_2_, ...), custom_call_target="tpu_custom_call" | custom-call | flops 6442450944 | bytes 12582912 | tf_op jit(solution)/shard_map/attend/pallas_call | solution.py:122
  32.0 0.0 collective-permute-done.9.refs_0_
  32.0 2.1 %collective-permute-start.10 = (bf16[64,1536]{1,0:T(8,128)(2,1)S(1)}, bf16[64,1536]{1,0:T(8,128)(2,1)S(1)}, u32[]{:S(2)}, u32[]{:S(2)}) collective-permute-start(bf16[64,1536]{1,0:T(8,128)(2,1)S(1)} %collective-permute-done.9.refs_0_), channel_id=1, source_target_pairs={{0,1},{1,0},{2,3},{3,2},{4,5},{5,4},{6,7},{7,6},{8,9},{9,8},{10,11... | collective-permute-start | bytes 589832 | tf_op jit(solution)/shard_map/ppermute | solution.py:38
  34.1 0.0 collective-permute-done.5.refs_1_
  34.1 0.0 copy-done.1
  34.1 0.0 slice-start
  34.1 0.0 slice-start.1
  34.1 0.0 slice-start.2
  34.1 4.9 %attend.6 = (bf16[64,1664]{1,0:T(8,128)(2,1)S(1)}, bf16[64,1664]{1,0:T(8,128)(2,1)S(1)}) custom-call(s32[16]{0:T(128)S(1)} %copy-done.1, bf16[64,1536]{1,0:T(8,128)(2,1)S(1)} %collective-permute-done.4.refs_0_, bf16[64,1536]{1,0:T(8,128)(2,1)S(1)} %collective-permute-done.5.refs_1_, bf16[2048,1536]{1,0:T(8,128)(2,1)S(1)} %get-tuple-element.63.refs_2_, ...), custom_call_target="tpu_custom_call" | custom-call | flops 6442450944 | bytes 12582912 | tf_op jit(solution)/shard_map/attend/pallas_call | solution.py:122
  39.0 0.0 slice-start.3
  39.0 0.0 slice-start.4
  39.0 0.1 collective-permute-start.7
  39.1 0.0 collective-permute-done.10.refs_1_
  39.2 4.7 %attend.7 = (bf16[64,1664]{1,0:T(8,128)(2,1)S(1)}, bf16[64,1664]{1,0:T(8,128)(2,1)S(1)}) custom-call(s32[16]{0:T(128)S(1)} %copy-done.1, bf16[64,1536]{1,0:T(8,128)(2,1)S(1)} %collective-permute-done.9.refs_0_, bf16[64,1536]{1,0:T(8,128)(2,1)S(1)} %collective-permute-done.10.refs_1_, bf16[2048,1536]{1,0:T(8,128)(2,1)S(1)} %get-tuple-element.63.refs_2_, ...), custom_call_target="tpu_custom_call" | custom-call | flops 6442450944 | bytes 12582912 | tf_op jit(solution)/shard_map/attend/pallas_call | solution.py:122
  43.8 2.0 %collective-permute-start.11 = (bf16[64,1664]{1,0:T(8,128)(2,1)S(1)}, bf16[64,1664]{1,0:T(8,128)(2,1)S(1)}, u32[]{:S(2)}, u32[]{:S(2)}) collective-permute-start(bf16[64,1664]{1,0:T(8,128)(2,1)S(1)} %get-tuple-element.86), channel_id=1, source_target_pairs={{0,1},{1,0},{2,3},{3,2},{4,5},{5,4},{6,7},{7,6},{8,9},{9,8},{10,11... | collective-permute-start | bytes 638984 | tf_op jit(solution)/shard_map/ppermute | solution.py:38
  45.9 0.1 collective-permute-start.6
  46.0 0.0 collective-permute-done.7.refs_1_
  46.0 0.4 merge.2
  46.4 3.0 %collective-permute-start.8 = (bf16[64,1664]{1,0:T(8,128)(2,1)S(1)}, bf16[64,1664]{1,0:T(8,128)(2,1)S(1)}, u32[]{:S(2)}, u32[]{:S(2)}) collective-permute-start(bf16[64,1664]{1,0:T(8,128)(2,1)S(1)} %merge.2), channel_id=1, source_target_pairs={{0,2},{1,3},{2,0},{3,1},{4,6},{5,7},{6,4},{7,5},{8,10},{9,11},{10,... | collective-permute-start | bytes 638984 | tf_op jit(solution)/shard_map/ppermute | solution.py:38
  49.4 7.0 %collective-permute-done.11.refs_1_ = bf16[64,1664]{1,0:T(8,128)(2,1)S(1)} collective-permute-done((bf16[64,1664]{1,0:T(8,128)(2,1)S(1)}, bf16[64,1664]{1,0:T(8,128)(2,1)S(1)}, u32[]{:S(2)}, u32[]{:S(2)}) %collective-permute-start.11) | collective-permute-done | bytes 213024 | tf_op jit(solution)/shard_map/ppermute | solution.py:38
  56.4 0.4 merge.3
  56.8 1.9 %collective-permute-done.6.refs_1_ = bf16[64,1664]{1,0:T(8,128)(2,1)S(1)} collective-permute-done((bf16[64,1664]{1,0:T(8,128)(2,1)S(1)}, bf16[64,1664]{1,0:T(8,128)(2,1)S(1)}, u32[]{:S(2)}, u32[]{:S(2)}) %collective-permute-start.6) | collective-permute-done | bytes 213024 | tf_op jit(solution)/shard_map/ppermute | solution.py:38
  58.6 0.0 collective-permute-done.8.refs_2_
  58.6 0.0 slice-done
  58.6 0.0 slice-done.1
  58.7 0.0 slice-done.2
  58.7 0.0 slice-done.3
  58.7 0.0 slice-done.4
  58.7 3.7 %project.2 = (bf16[32,6144]{1,0:T(8,128)(2,1)S(1)}, bf16[32,6144]{1,0:T(8,128)(2,1)S(1)}) custom-call(bf16[64,1664]{1,0:T(8,128)(2,1)S(1)} %get-tuple-element.87.refs_0_, bf16[64,1664]{1,0:T(8,128)(2,1)S(1)} %collective-permute-done.6.refs_1_, bf16[64,1664]{1,0:T(8,128)(2,1)S(1)} %collective-permute-done.8.refs_2_, bf16[1536,6144]{1,0:T(8,128)(2,1)S(1)} %bitcast.1), custom_call_target="tpu_custom_call" | custom-call | flops 1 | bytes 1 | tf_op jit(solution)/shard_map/project/pallas_call | solution.py:195
  62.5 0.1 collective-permute-start.13
  62.6 0.5 collective-permute-start.12
  63.0 2.4 %collective-permute-start.15 = (bf16[64,1664]{1,0:T(8,128)(2,1)S(1)}, bf16[64,1664]{1,0:T(8,128)(2,1)S(1)}, u32[]{:S(2)}, u32[]{:S(2)}) collective-permute-start(bf16[64,1664]{1,0:T(8,128)(2,1)S(1)} %merge.3), channel_id=1, source_target_pairs={{0,2},{1,3},{2,0},{3,1},{4,6},{5,7},{6,4},{7,5},{8,10},{9,11},{10,... | collective-permute-start | bytes 638984 | tf_op jit(solution)/shard_map/ppermute | solution.py:38
  65.5 0.0 collective-permute-done.13
  65.5 0.0 collective-permute-done.12
  65.5 0.1 add_convert_fusion.2
  65.6 1.4 %collective-permute-start.14 = (bf16[64,1664]{1,0:T(8,128)(2,1)S(1)}, bf16[64,1664]{1,0:T(8,128)(2,1)S(1)}, u32[]{:S(2)}, u32[]{:S(2)}) collective-permute-start(bf16[64,1664]{1,0:T(8,128)(2,1)S(1)} %get-tuple-element.92), channel_id=1, source_target_pairs={{0,1},{1,0},{2,3},{3,2},{4,5},{5,4},{6,7},{7,6},{8,9},{9,8},{10,11... | collective-permute-start | bytes 638984 | tf_op jit(solution)/shard_map/ppermute | solution.py:38
  67.0 0.4 collective-permute-start.18
  67.4 8.4 %collective-permute-done.15.refs_2_ = bf16[64,1664]{1,0:T(8,128)(2,1)S(1)} collective-permute-done((bf16[64,1664]{1,0:T(8,128)(2,1)S(1)}, bf16[64,1664]{1,0:T(8,128)(2,1)S(1)}, u32[]{:S(2)}, u32[]{:S(2)}) %collective-permute-start.15) | collective-permute-done | bytes 213024 | tf_op jit(solution)/shard_map/ppermute | solution.py:38
  75.7 0.0 collective-permute-done.14.refs_1_
  75.8 3.7 %project.3 = (bf16[32,6144]{1,0:T(8,128)(2,1)S(1)}, bf16[32,6144]{1,0:T(8,128)(2,1)S(1)}) custom-call(bf16[64,1664]{1,0:T(8,128)(2,1)S(1)} %get-tuple-element.94.refs_0_, bf16[64,1664]{1,0:T(8,128)(2,1)S(1)} %collective-permute-done.14.refs_1_, bf16[64,1664]{1,0:T(8,128)(2,1)S(1)} %collective-permute-done.15.refs_2_, bf16[1536,6144]{1,0:T(8,128)(2,1)S(1)} %bitcast.1), custom_call_target="tpu_custom_call" | custom-call | flops 1 | bytes 1 | tf_op jit(solution)/shard_map/project/pallas_call | solution.py:195
  79.5 0.1 collective-permute-start.17
  79.6 0.5 collective-permute-start.16
  80.1 0.0 collective-permute-done.18
  80.1 0.9 %collective-permute-done.17 = bf16[32,3072]{1,0:T(8,128)(2,1)S(1)} collective-permute-done((bf16[32,3072]{1,0:T(8,128)(2,1)S(1)}, bf16[32,3072]{1,0:T(8,128)(2,1)S(1)}, u32[]{:S(2)}, u32[]{:S(2)}) %collective-permute-start.17) | collective-permute-done | bytes 196640 | tf_op jit(solution)/shard_map/ppermute | solution.py:38
  81.0 0.3 collective-permute-done.16
  81.3 0.9 %add_convert_fusion = bf16[32,6144]{1,0:T(8,128)(2,1)} fusion(bf16[32,6144]{1,0:T(8,128)(2,1)S(1)} %collective-permute-done.18, bf16[32,6144]{1,0:T(8,128)(2,1)S(1)} %get-tuple-element.97, bf16[32,3072]{1,0:T(8,128)(2,1)S(1)} %collective-permute-done.17, bf16[32,3072]{1,0:T(8,128)(2,1)S(1)} %collective-permute-done.16), kind=kLoop, calls=%fused_computation | loop fusion | flops 2162688 | bytes 1572864 | tf_op jit(solution)/shard_map/convert_element_type | solution.py:320
  (7 shorter events, 0.1 us)
Async XLA Ops:
  1.1 1.6 %collective-permute-start = (bf16[64,1536]{1,0:T(8,128)(2,1)S(1)}, bf16[64,1536]{1,0:T(8,128)(2,1)S(1)}, u32[]{:S(2)}, u32[]{:S(2)}) collective-permute-start(bf16[64,1536]{1,0:T(8,128)(2,1)S(1)} %pad_maximum_fusion), channel_id=1, source_target_pairs={{0,4},{4,0},{8,12},{12,8},{1,5},{5,1},{9,13},{13,9},{2,6},{6,2},{1... | collective-permute-start | bytes 589832 | tf_op jit(solution)/shard_map/ppermute | solution.py:38
  2.7 10.6 %collective-permute-start.1 = (bf16[64,1536]{1,0:T(8,128)(2,1)S(1)}, bf16[64,1536]{1,0:T(8,128)(2,1)S(1)}, u32[]{:S(2)}, u32[]{:S(2)}) collective-permute-start(bf16[64,1536]{1,0:T(8,128)(2,1)S(1)} %pad_maximum_fusion.1.refs_0_), channel_id=1, source_target_pairs={{0,1},{1,0},{2,3},{3,2},{4,5},{5,4},{6,7},{7,6},{8,9},{9,8},{10,11... | collective-permute-start | bytes 589832 | tf_op jit(solution)/shard_map/ppermute | solution.py:38
  5.7 7.6 %collective-permute-start.2 = (bf16[64,1536]{1,0:T(8,128)(2,1)S(1)}, bf16[64,1536]{1,0:T(8,128)(2,1)S(1)}, u32[]{:S(2)}, u32[]{:S(2)}) collective-permute-start(bf16[64,1536]{1,0:T(8,128)(2,1)S(1)} %pad_maximum_fusion.2), channel_id=1, source_target_pairs={{0,8},{4,12},{8,0},{12,4},{1,9},{5,13},{9,1},{13,5},{2,10},{6,14},... | collective-permute-start | bytes 589832 | tf_op jit(solution)/shard_map/ppermute | solution.py:38
  7.3 24.7 %collective-permute-start.9 = (bf16[64,1536]{1,0:T(8,128)(2,1)S(1)}, bf16[64,1536]{1,0:T(8,128)(2,1)S(1)}, u32[]{:S(2)}, u32[]{:S(2)}) collective-permute-start(bf16[64,1536]{1,0:T(8,128)(2,1)S(1)} %pad_maximum_fusion.1.refs_0_), channel_id=1, source_target_pairs={{0,2},{1,3},{2,0},{3,1},{4,6},{5,7},{6,4},{7,5},{8,10},{9,11},{10,... | collective-permute-start | bytes 589832 | tf_op jit(solution)/shard_map/ppermute | solution.py:38
  13.4 12.7 %collective-permute-start.3 = (bf16[64,1536]{1,0:T(8,128)(2,1)S(1)}, bf16[64,1536]{1,0:T(8,128)(2,1)S(1)}, u32[]{:S(2)}, u32[]{:S(2)}) collective-permute-start(bf16[64,1536]{1,0:T(8,128)(2,1)S(1)} %collective-permute-done.2.refs_0_), channel_id=1, source_target_pairs={{0,1},{1,0},{2,3},{3,2},{4,5},{5,4},{6,7},{7,6},{8,9},{9,8},{10,11... | collective-permute-start | bytes 589832 | tf_op jit(solution)/shard_map/ppermute | solution.py:38
  13.4 14.0 %collective-permute-start.4 = (bf16[64,1536]{1,0:T(8,128)(2,1)S(1)}, bf16[64,1536]{1,0:T(8,128)(2,1)S(1)}, u32[]{:S(2)}, u32[]{:S(2)}) collective-permute-start(bf16[64,1536]{1,0:T(8,128)(2,1)S(1)} %collective-permute-done.2.refs_0_), channel_id=1, source_target_pairs={{0,2},{1,3},{2,0},{3,1},{4,6},{5,7},{6,4},{7,5},{8,10},{9,11},{10,... | collective-permute-start | bytes 589832 | tf_op jit(solution)/shard_map/ppermute | solution.py:38
  16.9 0.7 copy-start
  27.3 6.8 %collective-permute-start.5 = (bf16[64,1536]{1,0:T(8,128)(2,1)S(1)}, bf16[64,1536]{1,0:T(8,128)(2,1)S(1)}, u32[]{:S(2)}, u32[]{:S(2)}) collective-permute-start(bf16[64,1536]{1,0:T(8,128)(2,1)S(1)} %collective-permute-done.4.refs_0_), channel_id=1, source_target_pairs={{0,1},{1,0},{2,3},{3,2},{4,5},{5,4},{6,7},{7,6},{8,9},{9,8},{10,11... | collective-permute-start | bytes 589832 | tf_op jit(solution)/shard_map/ppermute | solution.py:38
  27.3 6.8 %copy-start.1 = (s32[16]{0:T(128)S(1)}, s32[16]{0:T(128)}, u32[]{:S(2)}) copy-start(s32[16]{0:T(128)} %kept_ref.3) | copy-start | bytes 196
  32.0 7.1 %collective-permute-start.10 = (bf16[64,1536]{1,0:T(8,128)(2,1)S(1)}, bf16[64,1536]{1,0:T(8,128)(2,1)S(1)}, u32[]{:S(2)}, u32[]{:S(2)}) collective-permute-start(bf16[64,1536]{1,0:T(8,128)(2,1)S(1)} %collective-permute-done.9.refs_0_), channel_id=1, source_target_pairs={{0,1},{1,0},{2,3},{3,2},{4,5},{5,4},{6,7},{7,6},{8,9},{9,8},{10,11... | collective-permute-start | bytes 589832 | tf_op jit(solution)/shard_map/ppermute | solution.py:38
  34.1 24.5 %slice-start = ((s8[18874368]{0:T(1024)(128)(4,1)}), s8[4194304]{0:T(1024)(128)(4,1)S(1)}, s32[]{:S(2)}) async-start(s8[18874368]{0:T(1024)(128)(4,1)} %bitcast), calls=%async_computation | async-start | bytes 8388608
  34.1 24.5 %slice-start.1 = ((s8[18874368]{0:T(1024)(128)(4,1)}), s8[4194304]{0:T(1024)(128)(4,1)S(1)}, s32[]{:S(2)}) async-start(s8[18874368]{0:T(1024)(128)(4,1)} %bitcast), calls=%async_computation.1 | async-start | bytes 8388608
  34.1 24.5 %slice-start.2 = ((s8[18874368]{0:T(1024)(128)(4,1)}), s8[4194304]{0:T(1024)(128)(4,1)S(1)}, s32[]{:S(2)}) async-start(s8[18874368]{0:T(1024)(128)(4,1)} %bitcast), calls=%async_computation.2 | async-start | bytes 8388608
  39.0 19.7 %slice-start.3 = ((s8[18874368]{0:T(1024)(128)(4,1)}), s8[4194304]{0:T(1024)(128)(4,1)S(1)}, s32[]{:S(2)}) async-start(s8[18874368]{0:T(1024)(128)(4,1)} %bitcast), calls=%async_computation.3 | async-start | bytes 8388608
  39.0 19.6 %slice-start.4 = ((s8[18874368]{0:T(1024)(128)(4,1)}), s8[2097152]{0:T(1024)(128)(4,1)S(1)}, s32[]{:S(2)}) async-start(s8[18874368]{0:T(1024)(128)(4,1)} %bitcast), calls=%async_computation.4 | async-start | bytes 4194304
  39.0 6.9 %collective-permute-start.7 = (bf16[64,1664]{1,0:T(8,128)(2,1)S(1)}, bf16[64,1664]{1,0:T(8,128)(2,1)S(1)}, u32[]{:S(2)}, u32[]{:S(2)}) collective-permute-start(bf16[64,1664]{1,0:T(8,128)(2,1)S(1)} %get-tuple-element.77), channel_id=1, source_target_pairs={{0,1},{1,0},{2,3},{3,2},{4,5},{5,4},{6,7},{7,6},{8,9},{9,8},{10,11... | collective-permute-start | bytes 638984 | tf_op jit(solution)/shard_map/ppermute | solution.py:38
  43.8 12.5 %collective-permute-start.11 = (bf16[64,1664]{1,0:T(8,128)(2,1)S(1)}, bf16[64,1664]{1,0:T(8,128)(2,1)S(1)}, u32[]{:S(2)}, u32[]{:S(2)}) collective-permute-start(bf16[64,1664]{1,0:T(8,128)(2,1)S(1)} %get-tuple-element.86), channel_id=1, source_target_pairs={{0,1},{1,0},{2,3},{3,2},{4,5},{5,4},{6,7},{7,6},{8,9},{9,8},{10,11... | collective-permute-start | bytes 638984 | tf_op jit(solution)/shard_map/ppermute | solution.py:38
  45.9 12.8 %collective-permute-start.6 = (bf16[64,1664]{1,0:T(8,128)(2,1)S(1)}, bf16[64,1664]{1,0:T(8,128)(2,1)S(1)}, u32[]{:S(2)}, u32[]{:S(2)}) collective-permute-start(bf16[64,1664]{1,0:T(8,128)(2,1)S(1)} %get-tuple-element.76), channel_id=1, source_target_pairs={{0,1},{1,0},{2,3},{3,2},{4,5},{5,4},{6,7},{7,6},{8,9},{9,8},{10,11... | collective-permute-start | bytes 638984 | tf_op jit(solution)/shard_map/ppermute | solution.py:38
  46.4 12.3 %collective-permute-start.8 = (bf16[64,1664]{1,0:T(8,128)(2,1)S(1)}, bf16[64,1664]{1,0:T(8,128)(2,1)S(1)}, u32[]{:S(2)}, u32[]{:S(2)}) collective-permute-start(bf16[64,1664]{1,0:T(8,128)(2,1)S(1)} %merge.2), channel_id=1, source_target_pairs={{0,2},{1,3},{2,0},{3,1},{4,6},{5,7},{6,4},{7,5},{8,10},{9,11},{10,... | collective-permute-start | bytes 638984 | tf_op jit(solution)/shard_map/ppermute | solution.py:38
  62.5 3.0 %collective-permute-start.13 = (bf16[32,3072]{1,0:T(8,128)(2,1)S(1)}, bf16[32,3072]{1,0:T(8,128)(2,1)S(1)}, u32[]{:S(2)}, u32[]{:S(2)}) collective-permute-start(bf16[32,3072]{1,0:T(8,128)(2,1)S(1)} %get-tuple-element.102), channel_id=1, source_target_pairs={{0,4},{4,0},{8,12},{12,8},{1,5},{5,1},{9,13},{13,9},{2,6},{6,2},{1... | collective-permute-start | bytes 589832 | tf_op jit(solution)/shard_map/ppermute | solution.py:38
  62.6 2.9 %collective-permute-start.12 = (bf16[32,3072]{1,0:T(8,128)(2,1)S(1)}, bf16[32,3072]{1,0:T(8,128)(2,1)S(1)}, u32[]{:S(2)}, u32[]{:S(2)}) collective-permute-start(bf16[32,3072]{1,0:T(8,128)(2,1)S(1)} %get-tuple-element.101), channel_id=1, source_target_pairs={{0,4},{4,0},{8,12},{12,8},{1,5},{5,1},{9,13},{13,9},{2,6},{6,2},{1... | collective-permute-start | bytes 589832 | tf_op jit(solution)/shard_map/ppermute | solution.py:38
  63.0 12.7 %collective-permute-start.15 = (bf16[64,1664]{1,0:T(8,128)(2,1)S(1)}, bf16[64,1664]{1,0:T(8,128)(2,1)S(1)}, u32[]{:S(2)}, u32[]{:S(2)}) collective-permute-start(bf16[64,1664]{1,0:T(8,128)(2,1)S(1)} %merge.3), channel_id=1, source_target_pairs={{0,2},{1,3},{2,0},{3,1},{4,6},{5,7},{6,4},{7,5},{8,10},{9,11},{10,... | collective-permute-start | bytes 638984 | tf_op jit(solution)/shard_map/ppermute | solution.py:38
  65.6 10.2 %collective-permute-start.14 = (bf16[64,1664]{1,0:T(8,128)(2,1)S(1)}, bf16[64,1664]{1,0:T(8,128)(2,1)S(1)}, u32[]{:S(2)}, u32[]{:S(2)}) collective-permute-start(bf16[64,1664]{1,0:T(8,128)(2,1)S(1)} %get-tuple-element.92), channel_id=1, source_target_pairs={{0,1},{1,0},{2,3},{3,2},{4,5},{5,4},{6,7},{7,6},{8,9},{9,8},{10,11... | collective-permute-start | bytes 638984 | tf_op jit(solution)/shard_map/ppermute | solution.py:38
  67.0 13.1 %collective-permute-start.18 = (bf16[32,6144]{1,0:T(8,128)(2,1)S(1)}, bf16[32,6144]{1,0:T(8,128)(2,1)S(1)}, u32[]{:S(2)}, u32[]{:S(2)}) collective-permute-start(bf16[32,6144]{1,0:T(8,128)(2,1)S(1)} %add_convert_fusion.2), channel_id=1, source_target_pairs={{0,8},{4,12},{8,0},{12,4},{1,9},{5,13},{9,1},{13,5},{2,10},{6,14},... | collective-permute-start | bytes 1179656 | tf_op jit(solution)/shard_map/ppermute | solution.py:38
  79.5 1.5 %collective-permute-start.17 = (bf16[32,3072]{1,0:T(8,128)(2,1)S(1)}, bf16[32,3072]{1,0:T(8,128)(2,1)S(1)}, u32[]{:S(2)}, u32[]{:S(2)}) collective-permute-start(bf16[32,3072]{1,0:T(8,128)(2,1)S(1)} %get-tuple-element.100), channel_id=1, source_target_pairs={{0,4},{4,0},{8,12},{12,8},{1,5},{5,1},{9,13},{13,9},{2,6},{6,2},{1... | collective-permute-start | bytes 589832 | tf_op jit(solution)/shard_map/ppermute | solution.py:38
  79.6 1.7 %collective-permute-start.16 = (bf16[32,3072]{1,0:T(8,128)(2,1)S(1)}, bf16[32,3072]{1,0:T(8,128)(2,1)S(1)}, u32[]{:S(2)}, u32[]{:S(2)}) collective-permute-start(bf16[32,3072]{1,0:T(8,128)(2,1)S(1)} %get-tuple-element.99), channel_id=1, source_target_pairs={{0,4},{4,0},{8,12},{12,8},{1,5},{5,1},{9,13},{13,9},{2,6},{6,2},{1... | collective-permute-start | bytes 589832 | tf_op jit(solution)/shard_map/ppermute | solution.py:38
